TPU v7x, 32 devices: a whole 2x2x4 slice. The times are simulated.
32 devices in a mesh: ctx: 8 (over z, x), dp: 4 (over y, core).
Axes of the slice: x: 2, y: 2, z: 4, core: 2. Of those that a mesh axis runs over, the one named last changes fastest.
Arguments:
- query_in: bfloat16 [4, 2048, 4096], P('dp', 'ctx'), may hold values from -6 to 6
- key_in: bfloat16 [4, 2048, 512], P('dp', 'ctx'), may hold values from -6 to 6
- value_rows_input: bfloat16 [4, 2048, 512], P('dp', 'ctx'), may hold values from -6 to 6
- grad_out: bfloat16 [4, 2048, 4096], P('dp', 'ctx'), may hold values from -12 to 12
- query_bias: float32 [4096], replicated, may hold values from -1.5 to 1.5
- key_blocks: int32 [4, 16, 6], P('dp'), may hold values from -1 to 15, as said below
- trace_len: int32 [4], P('dp'), may hold values from 1024 to 2048, as said below
Outputs:
- grad_query: bfloat16 [4, 2048, 4096], P('dp', 'ctx')
- grad_key: bfloat16 [4, 2048, 512], P('dp', 'ctx')
- grad_value: bfloat16 [4, 2048, 512], P('dp', 'ctx')
- bias_grad: float32 [4096], replicated
Inputs may be any that keep to these rules, and one draw needn't show every extreme that they name: `key_blocks`: blocks are numbered by position. Entry 2 + d of query block q's list is q - d or -1, and entry 2 is always q; entry r < 2 is r or -1, and -1 whenever r >= q - 3. `trace_len`: some trace has 2048 tokens and some 2048 // 2.
All inputs are finite; a program needn't handle non-finite values.
Results may differ from a plain program's by a relative error of at most 0.011.
The roundings to bfloat16 on the way count: a program that leaves them out, or rounds other values in their place, can miss the bound.
Values may be sent and summed in bfloat16 or wider, within the bound.
No kernel may reach another device: no remote copies, remote signals or barrier semaphores. Data moves between devices by JAX's collectives and lax.ppermute only.
A program may use at most 128 MiB of HBM per device.

v0:
```python
import math

import jax
import jax.numpy as jnp
from jax import lax
from jax.sharding import PartitionSpec as P

HEAD_SIZE = 128
BLOCK = 128
PROMPT = 2
WINDOW = 3


def from_behind(value, axis, steps):
    count = lax.axis_size(axis)
    initial, last = (max(0, -steps), min(count, count - steps))
    return lax.ppermute(value, axis, [(source, source + steps) for source in range(initial, last)])


def broadcast(value, axis, source):
    kept = jnp.where(lax.axis_index(axis) == source, value, 0).astype(value.dtype)
    return lax.psum(kept, axis)


def attend(queries, cand_keys, cand_vals, grad_rows, allowed):
    score_scale = HEAD_SIZE ** (-0.5)
    scores = score_scale * jnp.einsum(
        "tqkgd,tskd->tkgqs", queries, cand_keys, preferred_element_type=jnp.float32
    )
    mask_full = allowed[:, None, None]
    scores = jnp.where(mask_full, scores, -1e30)
    row_max = jnp.max(scores, axis=-1, keepdims=True)
    probs = jnp.where(mask_full, jnp.exp(scores - row_max), 0.0)
    totals = jnp.sum(probs, axis=-1, keepdims=True)
    row_live = jnp.any(allowed, axis=-1)[:, None, None, :, None]
    probs = probs / jnp.where(row_live, totals, 1.0)
    probs_low = probs.astype(jnp.bfloat16)
    attended = jnp.einsum(
        "tkgqs,tskd->tqkgd", probs_low, cand_vals, preferred_element_type=jnp.float32
    )
    row_dot = jnp.sum(grad_rows * attended, axis=-1).transpose(0, 2, 3, 1)[..., None]
    grad_probs = jnp.einsum(
        "tqkgd,tskd->tkgqs", grad_rows, cand_vals, preferred_element_type=jnp.float32
    )
    grad_scores = (probs * (grad_probs - row_dot)).astype(jnp.bfloat16)
    grad_query = score_scale * jnp.einsum(
        "tkgqs,tskd->tqkgd", grad_scores, cand_keys, preferred_element_type=jnp.float32
    )
    grad_key = score_scale * jnp.einsum(
        "tkgqs,tqkgd->tskd", grad_scores, queries, preferred_element_type=jnp.float32
    )
    grad_value = jnp.einsum(
        "tkgqs,tqkgd->tskd", probs_low, grad_rows, preferred_element_type=jnp.float32
    )
    return (grad_query, grad_key, grad_value)


def body(query_in, key_in, value_rows_input, grad_out, query_bias, key_blocks, trace_len):
    ctx_count = lax.axis_size("ctx")
    rank_ctx = lax.axis_index("ctx")
    traces = query_in.shape[0]
    width_kv = key_in.shape[-1]
    width_q = query_in.shape[-1]
    heads_kv = width_kv // HEAD_SIZE
    group_size = width_q // width_kv
    cand_count = PROMPT + WINDOW + 1
    level_list = (WINDOW + 1).bit_length() - 1
    kv_pair = jnp.concatenate([key_in, value_rows_input], axis=-1).reshape(
        traces, 2, BLOCK, 2 * width_kv
    )
    own_ids = jnp.stack([rank_ctx, 2 * ctx_count - 1 - rank_ctx])
    half_count = kv_pair.shape[1]
    from_lower = kv_pair[None]
    from_upper = kv_pair[None]
    for level_idx in range(level_list):
        stride = 1 << level_idx
        from_lower = jnp.concatenate([from_lower, from_behind(from_lower, "ctx", stride)], axis=0)
        from_upper = jnp.concatenate([from_upper, from_behind(from_upper, "ctx", -stride)], axis=0)
    from_lower = from_lower[1:]
    from_upper = from_upper[1:]
    offsets = jnp.arange(1, WINDOW + 1, dtype=jnp.int32)
    lower_dev = rank_ctx - offsets
    upper_dev = rank_ctx + offsets
    lower_ids = jnp.stack([lower_dev, 2 * ctx_count - 1 - lower_dev], axis=1)
    upper_ids = jnp.stack([upper_dev, 2 * ctx_count - 1 - upper_dev], axis=1)
    lower_ids = jnp.where((lower_dev >= 0)[:, None], lower_ids, -1000).reshape(-1)
    upper_ids = jnp.where((upper_dev < ctx_count)[:, None], upper_ids, -1000).reshape(-1)
    lower_data = from_lower.transpose(1, 0, 2, 3, 4).reshape(
        traces, WINDOW * half_count, BLOCK, 2 * width_kv
    )
    upper_data = from_upper.transpose(1, 0, 2, 3, 4).reshape(
        traces, WINDOW * half_count, BLOCK, 2 * width_kv
    )
    data_list = [kv_pair, lower_data, upper_data]
    id_list = [own_ids, lower_ids, upper_ids]
    slot_data = jnp.concatenate(data_list, axis=1)
    slot_ids = jnp.concatenate(id_list)
    targets = own_ids[:, None] - jnp.arange(WINDOW + 1, dtype=jnp.int32)[None]
    chooser = (slot_ids[None, None, :] == targets[..., None]).astype(jnp.bfloat16)
    window_kv = jnp.einsum(
        "jdn,tnbf->tjdbf", chooser, slot_data, preferred_element_type=jnp.float32
    ).astype(jnp.bfloat16)
    first_half = kv_pair[:, 0]
    prompt_kv = jnp.stack(
        [broadcast(first_half, "ctx", source) for source in range(PROMPT)], axis=1
    )
    block_rows = jnp.take(key_blocks, own_ids, axis=1)
    queries = (
        (query_in.astype(jnp.float32) + query_bias)
        .astype(jnp.bfloat16)
        .reshape(traces, 2, BLOCK, heads_kv, group_size, HEAD_SIZE)
    )
    grad_rows = grad_out.reshape(traces, 2, BLOCK, heads_kv, group_size, HEAD_SIZE)
    prompt_grad = jnp.zeros((traces, PROMPT, BLOCK, 2 * width_kv), jnp.float32)
    slot_grad = jnp.zeros((traces, slot_data.shape[1], BLOCK, 2 * width_kv), jnp.float32)
    query_parts = []
    for half_idx in range(2):
        block_here = own_ids[half_idx]
        candidates = jnp.concatenate([prompt_kv, window_kv[:, half_idx]], axis=1)
        cand_keys = candidates[..., :width_kv].reshape(
            traces, cand_count * BLOCK, heads_kv, HEAD_SIZE
        )
        cand_vals = candidates[..., width_kv:].reshape(
            traces, cand_count * BLOCK, heads_kv, HEAD_SIZE
        )
        key_ids = jnp.concatenate(
            [
                jnp.arange(PROMPT, dtype=jnp.int32),
                block_here - jnp.arange(WINDOW + 1, dtype=jnp.int32),
            ]
        )
        prompt_ok = jnp.concatenate(
            [
                jnp.arange(PROMPT, dtype=jnp.int32) < block_here - WINDOW,
                jnp.ones((WINDOW + 1,), jnp.bool_),
            ]
        )
        block_ok = (block_rows[:, half_idx] >= 0) & prompt_ok[None]
        key_pos = (key_ids[:, None] * BLOCK + jnp.arange(BLOCK, dtype=jnp.int32)[None]).reshape(-1)
        query_pos = block_here * BLOCK + jnp.arange(BLOCK, dtype=jnp.int32)
        length = trace_len[:, None, None]
        allowed = (
            jnp.repeat(block_ok, BLOCK, axis=1)[:, None, :]
            & (key_pos[None, None, :] <= query_pos[None, :, None])
            & (key_pos[None, None, :] < length)
            & (query_pos[None, :, None] < length)
        )
        grad_query, grad_key, grad_value = attend(
            queries[:, half_idx], cand_keys, cand_vals, grad_rows[:, half_idx], allowed
        )
        query_parts.append(grad_query)
        contrib = jnp.concatenate(
            [
                grad_key.reshape(traces, cand_count, BLOCK, width_kv),
                grad_value.reshape(traces, cand_count, BLOCK, width_kv),
            ],
            axis=-1,
        )
        prompt_grad = prompt_grad + contrib[:, :PROMPT]
        slot_grad = slot_grad + jnp.einsum(
            "dn,tdbf->tnbf",
            chooser[half_idx].astype(jnp.float32),
            contrib[:, PROMPT:],
            precision=lax.Precision.HIGHEST,
        )
    span = WINDOW * half_count
    own_grad = slot_grad[:, 0:2]
    lower_grad = (
        slot_grad[:, 2 : 2 + span]
        .reshape(traces, WINDOW, half_count, BLOCK, 2 * width_kv)
        .transpose(1, 0, 2, 3, 4)
    )
    upper_grad = (
        slot_grad[:, 2 + span : 2 + 2 * span]
        .reshape(traces, WINDOW, half_count, BLOCK, 2 * width_kv)
        .transpose(1, 0, 2, 3, 4)
    )
    lower_acc = jnp.concatenate([jnp.zeros_like(lower_grad[0])[None], lower_grad], axis=0)
    upper_acc = jnp.concatenate([jnp.zeros_like(upper_grad[0])[None], upper_grad], axis=0)
    for level_idx in reversed(range(level_list)):
        stride = 1 << level_idx
        lower_acc = lower_acc[:stride] + from_behind(lower_acc[stride : 2 * stride], "ctx", -stride)
        upper_acc = upper_acc[:stride] + from_behind(upper_acc[stride : 2 * stride], "ctx", stride)
    low_part = lower_acc[0]
    up_part = upper_acc[0]
    kv_grad = own_grad + low_part + up_part
    owners = jnp.arange(PROMPT, dtype=jnp.int32)
    query_all = jnp.stack(query_parts, axis=1)
    local_bias = jnp.sum(query_all, axis=(0, 1, 2)).reshape(width_q)
    shared_total = lax.psum(prompt_grad, "ctx")
    bias_total = lax.psum(local_bias, ("ctx", "dp"))
    owned = (owners == rank_ctx).astype(jnp.float32)
    kv_grad = kv_grad.at[:, 0].add(jnp.sum(owned[None, :, None, None] * shared_total, axis=1))
    grad_query_out = query_all.reshape(traces, 2 * BLOCK, width_q).astype(jnp.bfloat16)
    grad_key_out = kv_grad[..., :width_kv].reshape(traces, 2 * BLOCK, width_kv).astype(jnp.bfloat16)
    grad_value_out = (
        kv_grad[..., width_kv:].reshape(traces, 2 * BLOCK, width_kv).astype(jnp.bfloat16)
    )
    all_traces = traces * lax.axis_size("dp")
    bias_out = bias_total / math.sqrt(all_traces * 2 * BLOCK * ctx_count)
    return (grad_query_out, grad_key_out, grad_value_out, bias_out)


def solution(mesh):
    return jax.shard_map(
        body,
        mesh=mesh,
        in_specs=(
            P("dp", "ctx", None),
            P("dp", "ctx", None),
            P("dp", "ctx", None),
            P("dp", "ctx", None),
            P(),
            P("dp", None, None),
            P("dp"),
        ),
        out_specs=(P("dp", "ctx", None), P("dp", "ctx", None), P("dp", "ctx", None), P()),
        check_vma=False,
    )
```

profile of v0, /device:TPU:0, one launch (start us, length us, event | category | flops | bytes accessed | tf_op | source)
XLA Modules:
  0.0 404.8 jit_solution(7267511472957840767)
XLA Ops:
  10.6 6.3 %collective-permute-start = (bf16[1,1,2,128,1024]{4,3,2,0,1:T(8,128)(2,1)S(1)}, bf16[1,1,2,128,1024]{4,3,2,0,1:T(8,128)(2,1)}, u32[]{:S(2)}, u32[]{:S(2)}) collective-permute-start(bf16[1,1,2,128,1024]{4,3,2,0,1:T(8,128)(2,1)S(1)} %bitcast.343), channel_id=1, source_target_pairs={{0,4},{4,8},{8,12},{12,16},{16,20},{20,24},{24,28},{1,5},{5,9},{9,... | collective-permute-start | bytes 1572872 | tf_op jit(solution)/shard_map/ppermute | solution.py:17
  26.7 14.5 %collective-permute-done = bf16[1,1,2,128,1024]{4,3,2,0,1:T(8,128)(2,1)} collective-permute-done((bf16[1,1,2,128,1024]{4,3,2,0,1:T(8,128)(2,1)S(1)}, bf16[1,1,2,128,1024]{4,3,2,0,1:T(8,128)(2,1)}, u32[]{:S(2)}, u32[]{:S(2)}) %collective-permute-start) | collective-permute-done | bytes 524320 | tf_op jit(solution)/shard_map/ppermute | solution.py:17
  42.4 4.1 %collective-permute-start.1 = (bf16[2,1,2,128,1024]{4,3,2,0,1:T(8,128)(2,1)S(1)}, bf16[2,1,2,128,1024]{4,3,2,0,1:T(8,128)(2,1)S(1)}, u32[]{:S(2)}, u32[]{:S(2)}) collective-permute-start(bf16[2,1,2,128,1024]{4,3,2,0,1:T(8,128)(2,1)S(1)} %get-tuple-element.40), channel_id=1, source_target_pairs={{0,8},{4,12},{8,16},{12,20},{16,24},{20,28},{1,9},{5,13},{9,17},{1... | collective-permute-start | bytes 3145736 | tf_op jit(solution)/shard_map/ppermute | solution.py:17
  52.5 19.2 %collective-permute-done.1 = bf16[2,1,2,128,1024]{4,3,2,0,1:T(8,128)(2,1)S(1)} collective-permute-done((bf16[2,1,2,128,1024]{4,3,2,0,1:T(8,128)(2,1)S(1)}, bf16[2,1,2,128,1024]{4,3,2,0,1:T(8,128)(2,1)S(1)}, u32[]{:S(2)}, u32[]{:S(2)}) %collective-permute-start.1) | collective-permute-done | bytes 1048608 | tf_op jit(solution)/shard_map/ppermute | solution.py:17
  73.8 3.2 collective-permute-done.3
  81.1 23.8 %all-reduce.10.cloned.1.call-done = (bf16[1,1,128,1024]{3,1,2,0:T(2,128)(2,1)}, bf16[1,1,128,1024]{3,1,2,0:T(2,128)(2,1)}) async-done(((bf16[1,1,128,1024]{3,1,2,0:T(2,128)(2,1)}, bf16[1,1,128,1024]{3,1,2,0:T(2,128)(2,1)}), (bf16[1,1,128,1024]{3,1,2,0:T(2,128)(2,1)}, bf16[1,1,128,1024]{3,1,2,0:T(2,128)(2,1)})) %all-reduce.10.cloned.1.call-update) | async-done | bytes 524304 | tf_op jit(solution)/shard_map/psum | solution.py:22
  105.0 4.5 %pad_maximum_fusion = (bf16[1,6,128,1024]{3,1,2,0:T(8,128)(2,1)S(1)}, bf16[1,6,128,1024]{3,1,2,0:T(8,128)(2,1)}) fusion(bf16[1,4,128,1024]{3,1,2,0:T(4,128)(2,1)S(1)} %get-tuple-element.30, bf16[1,1,128,1024]{3,1,2,0:T(2,128)(2,1)} %get-tuple-element.16, bf16[1,1,128,1024]{3,1,2,0:T(2,128)(2,1)} %get-tuple-element.17, ...), kind=kLoop, calls=%fused_computation.45 | loop fusion | flops 7077888 | bytes 5767168 | tf_op jit(solution)/shard_map/concatenate | solution.py:119
  116.7 2.7 fusion.81
  122.2 2.6 copy.109
  124.8 2.5 reshape.1047
  129.5 3.8 fusion.5
  133.3 3.1 fusion.9
  136.5 4.8 %fusion.42 = f32[1,768,4,128]{3,1,2,0:T(8,128)} fusion(bf16[1,1,128,4,8,128]{5,4,3,2,1,0:T(8,128)(2,1)S(1)} %copy-done.23, f32[4,8,128]{2,1,0:T(8,128)S(1)} %broadcast_select_fusion.2, f32[4,8,128]{2,1,0:T(8,128)S(1)} %get-tuple-element.46, f32[4,768,128,8]{2,1,3,0:T(8,128)S(1)} %get-tuple-element.47, pred[128,768]{0,1:T(8,128)(4,1)S(1)} %and_and_fusion), kind=kOutput, calls=%fused_computation.69 | convolution fusion | flops 824180736 | bytes 15335424 | tf_op jit(solution)/shard_map/tkgqs,tqkgd->tskd/dot_general | solution.py:52
  141.3 5.2 %fusion.31 = f32[128,4,8]{0,2,1:T(8,128)S(1)} fusion(bf16[768,4,128,1]{0,2,3,1:T(8,128)(2,1)S(1)} %copy-done.26, bf16[1,1,128,4,8,128]{5,4,3,2,1,0:T(8,128)(2,1)S(1)} %copy-done.23, f32[4,8,128]{2,1,0:T(8,128)S(1)} %broadcast_select_fusion.2, f32[4,8,128]{2,1,0:T(8,128)S(1)} %get-tuple-element.46, f32[4,768,128,8]{2,1,3,0:T(8,128)S(1)} %get-tuple-element.47, ...), kind=kOutput, calls=%fused_computation.50 | convolution fusion | flops 825749504 | bytes 14565376 | tf_op jit(solution)/shard_map/tkgqs,tskd->tqkgd/dot_general | solution.py:38
  146.5 7.3 %fusion.11 = bf16[4,8,128,768]{2,3,1,0:T(8,128)(2,1)S(1)} fusion(f32[4,8,128]{2,1,0:T(8,128)S(1)} %bitcast.352, f32[4,8,128]{2,1,0:T(8,128)S(1)} %broadcast_select_fusion.2, f32[4,8,128]{2,1,0:T(8,128)S(1)} %get-tuple-element.46, f32[4,768,128,8]{2,1,3,0:T(8,128)S(1)} %get-tuple-element.47, pred[128,768]{0,1:T(8,128)(4,1)S(1)} %and_and_fusion, ...), kind=kOutput, calls=%fused_computation.19 | convolution fusion | flops 830472192 | bytes 20856832 | tf_op jit(solution)/shard_map/tqkgd,tskd->tkgqs/dot_general | solution.py:42
  153.8 2.7 copy.127
  156.9 3.4 fusion.37
  160.3 2.6 copy.126
  162.9 3.8 copy_dynamic-update-slice_fusion.1
  169.0 3.1 fusion.7
  172.2 4.8 %fusion.39 = f32[1,768,4,128]{3,1,2,0:T(8,128)} fusion(bf16[1,1,128,4,8,128]{5,4,3,2,1,0:T(8,128)(2,1)S(1)} %copy-done.21, f32[4,8,128]{2,1,0:T(8,128)S(1)} %broadcast_select_fusion.3, f32[4,8,128]{2,1,0:T(8,128)S(1)} %get-tuple-element.48, f32[4,768,128,8]{2,1,3,0:T(8,128)S(1)} %get-tuple-element.49, pred[128,768]{0,1:T(8,128)(4,1)S(1)} %and_and_fusion.1), kind=kOutput, calls=%fused_computation.68 | convolution fusion | flops 824180736 | bytes 15335424 | tf_op jit(solution)/shard_map/tkgqs,tqkgd->tskd/dot_general | solution.py:52
  177.0 5.2 %fusion.32 = f32[128,4,8]{0,2,1:T(8,128)S(1)} fusion(bf16[768,4,128,1]{0,2,3,1:T(8,128)(2,1)S(1)} %copy-done.25, bf16[1,1,128,4,8,128]{5,4,3,2,1,0:T(8,128)(2,1)S(1)} %copy-done.21, f32[4,8,128]{2,1,0:T(8,128)S(1)} %broadcast_select_fusion.3, f32[4,8,128]{2,1,0:T(8,128)S(1)} %get-tuple-element.48, f32[4,768,128,8]{2,1,3,0:T(8,128)S(1)} %get-tuple-element.49, ...), kind=kOutput, calls=%fused_computation.52 | convolution fusion | flops 825749504 | bytes 14565376 | tf_op jit(solution)/shard_map/tkgqs,tskd->tqkgd/dot_general | solution.py:38
  182.2 7.1 %fusion.10 = bf16[4,8,128,768]{2,3,1,0:T(8,128)(2,1)S(1)} fusion(f32[4,8,128]{2,1,0:T(8,128)S(1)} %bitcast.353, f32[4,8,128]{2,1,0:T(8,128)S(1)} %broadcast_select_fusion.3, f32[4,8,128]{2,1,0:T(8,128)S(1)} %get-tuple-element.48, f32[4,768,128,8]{2,1,3,0:T(8,128)S(1)} %get-tuple-element.49, pred[128,768]{0,1:T(8,128)(4,1)S(1)} %and_and_fusion.1, ...), kind=kOutput, calls=%fused_computation.18 | convolution fusion | flops 830472192 | bytes 20856832 | tf_op jit(solution)/shard_map/tqkgd,tskd->tkgqs/dot_general | solution.py:42
  189.3 2.6 copy.121
  192.4 3.4 fusion.38
  195.8 2.9 copy.120
  198.7 2.5 copy_dynamic-update-slice_fusion.3
  202.2 5.7 %fusion.30 = f32[128,1024,14]{1,2,0:T(8,128)S(1)} fusion(f32[1,6,128,1024]{3,1,2,0:T(8,128)S(1)} %copy_dynamic-update-slice_fusion.2, pred[2,4,14]{2,1,0:T(4,128)(4,1)S(1)} %copy-done.29), kind=kOutput, calls=%fused_computation.44 | convolution fusion | flops 88080384 | bytes 9437696 | tf_op jit(solution)/shard_map/dn,tdbf->tnbf/dot_general | solution.py:160
  210.9 6.7 %add_bitcast_fusion = f32[1,14,128,1024]{3,1,2,0:T(8,128)S(1)} fusion(f32[128,1024,14]{1,2,0:T(8,128)S(1)} %fusion.30, f32[1,6,128,1024]{3,1,2,0:T(8,128)S(1)} %copy_dynamic-update-slice_fusion, pred[2,4,14]{2,1,0:T(4,128)(4,1)S(1)} %copy-done.29), kind=kOutput, calls=%fused_computation.17 | convolution fusion | flops 89915392 | bytes 17826304 | tf_op jit(solution)/shard_map/dn,tdbf->tnbf/dot_general | solution.py:160
  217.6 3.8 fusion.77
  222.1 3.9 slice.158
  226.0 3.7 copy.132
  230.9 5.4 %slice_add_fusion = f32[1,2,128,1024]{3,1,2,0:T(2,128)} fusion(f32[1,6,128,1024]{3,1,2,0:T(8,128)} %copy-done.5, f32[1,6,128,1024]{3,1,2,0:T(8,128)} %copy-done.3), kind=kLoop, calls=%fused_computation.74 | loop fusion | flops 262144 | bytes 3145728 | tf_op jit(solution)/shard_map/add | solution.py:159
  236.4 3.8 slice.164
  240.2 3.7 copy.135
  243.9 4.7 %collective-permute-start.6 = (f32[2,1,2,128,1024]{4,2,3,1,0:T(2,128)}, f32[2,1,2,128,1024]{4,2,3,1,0:T(2,128)S(1)}, u32[]{:S(2)}, u32[]{:S(2)}) collective-permute-start(f32[2,1,2,128,1024]{4,2,3,1,0:T(2,128)} %copy.135), channel_id=1, source_target_pairs={{0,8},{4,12},{8,16},{12,20},{16,24},{20,28},{1,9},{5,13},{9,17},{1... | collective-permute-start | bytes 6291464 | tf_op jit(solution)/shard_map/ppermute | solution.py:17
  248.6 4.5 %fusion.76 = (f32[1,6,128,1024]{3,1,2,0:T(8,128)S(1)}, f32[1,6,128,1024]{3,1,2,0:T(8,128)S(1)}) fusion(f32[1,14,128,1024]{3,1,2,0:T(8,128)} %copy-done), kind=kLoop, calls=%fused_computation.158 | loop fusion | bytes 12582912 | tf_op jit(solution)/shard_map/slice | solution.py:169
  261.7 2.6 bitcast_reduce_fusion
  267.1 26.2 %collective-permute-done.4 = f32[2,1,2,128,1024]{4,2,3,1,0:T(2,128)} collective-permute-done((f32[2,1,2,128,1024]{4,2,3,1,0:T(2,128)}, f32[2,1,2,128,1024]{4,2,3,1,0:T(2,128)}, u32[]{:S(2)}, u32[]{:S(2)}) %collective-permute-start.4) | collective-permute-done | bytes 2097184 | tf_op jit(solution)/shard_map/ppermute | solution.py:17
  293.3 2.7 fusion.28
  297.5 9.0 %collective-permute-done.6 = f32[2,1,2,128,1024]{4,2,3,1,0:T(2,128)S(1)} collective-permute-done((f32[2,1,2,128,1024]{4,2,3,1,0:T(2,128)}, f32[2,1,2,128,1024]{4,2,3,1,0:T(2,128)S(1)}, u32[]{:S(2)}, u32[]{:S(2)}) %collective-permute-start.6) | collective-permute-done | bytes 2097184 | tf_op jit(solution)/shard_map/ppermute | solution.py:17
  308.6 4.6 %collective-permute-start.7 = (f32[1,1,2,128,1024]{4,2,3,1,0:T(2,128)}, f32[1,1,2,128,1024]{4,2,3,1,0:T(2,128)}, u32[]{:S(2)}, u32[]{:S(2)}) collective-permute-start(f32[1,1,2,128,1024]{4,2,3,1,0:T(2,128)} %slice.197), channel_id=1, source_target_pairs={{0,4},{4,8},{8,12},{12,16},{16,20},{20,24},{24,28},{1,5},{5,9},{9,... | collective-permute-start | bytes 3145736 | tf_op jit(solution)/shard_map/ppermute | solution.py:17
  313.8 2.7 copy.117
  316.5 4.2 %convert_element_type.117 = bf16[1,256,4096]{2,1,0:T(8,128)(2,1)} reshape(bf16[1,2,128,4,8,128]{5,4,3,2,1,0:T(8,128)(2,1)} %copy.117) | data formatting | bytes 4194304 | tf_op jit(solution)/shard_map/convert_element_type | solution.py:194
  320.7 62.7 %psum.31 = f32[4096]{0:T(1024)S(1)} all-reduce(f32[4096]{0:T(1024)S(1)} %add_bitcast_fusion.1), channel_id=1, replica_groups=mesh['ctx'=8,'dp'=4] {'ctx','dp'}, use_global_device_ids=true, to_apply=%region_14.15 | all-reduce | flops 4096 | bytes 32768 | tf_op jit(solution)/shard_map/psum | solution.py:191
  384.0 2.6 multiply_reduce_fusion
  386.7 4.5 %fusion.48 = f32[1,2,128,1024]{3,1,2,0:T(2,128)S(1)} fusion(f32[1,1,2,128,1024]{4,2,3,1,0:T(2,128)} %collective-permute-done.7, f32[2,1,2,128,1024]{4,2,3,1,0:T(2,128)} %copy-done.9, f32[1,1,2,128,1024]{4,2,3,1,0:T(2,128)} %collective-permute-done.5, f32[2,1,2,128,1024]{4,2,3,1,0:T(2,128)S(1)} %fusion.28, f32[1,14,128,1024]{3,1,2,0:T(8,128)} %copy-done), kind=kLoop, calls=%fused_computation.77 | loop fusion | flops 1048576 | bytes 6291456 | tf_op jit(solution)/shard_map/add | solution.py:186
  391.7 3.7 scatter-add.4
  (169 shorter events, 66.0 us)
Async XLA Ops:
  7.2 14.6 %copy-start.30 = (s32[1,16,6]{1,0,2:T(1,128)S(1)}, s32[1,16,6]{1,0,2:T(1,128)}, u32[]{:S(2)}) copy-start(s32[1,16,6]{1,0,2:T(1,128)} %param.14) | copy-start | bytes 1156
  7.2 14.6 %copy-start.27 = (f32[4096]{0:T(1024)S(1)}, f32[4096]{0:T(1024)}, u32[]{:S(2)}) copy-start(f32[4096]{0:T(1024)} %param.13) | copy-start | bytes 49156
  7.2 14.6 %copy-start.13 = (bf16[1,256,4096]{2,1,0:T(8,128)(2,1)S(1)}, bf16[1,256,4096]{2,1,0:T(8,128)(2,1)}, u32[]{:S(2)}) copy-start(bf16[1,256,4096]{2,1,0:T(8,128)(2,1)} %param.9) | copy-start | bytes 6291460
  7.2 97.8 %all-reduce.10.cloned.1.call-start = ((), (), s32[]{:S(2)}) async-start(), calls=%async_computation.1 | async-start | bytes 2097152 | tf_op jit(solution)/shard_map/psum | solution.py:22
  9.3 17.3 %collective-permute-start.2 = (bf16[1,1,2,128,1024]{4,3,2,0,1:T(8,128)(2,1)S(1)}, bf16[1,1,2,128,1024]{4,3,2,0,1:T(8,128)(2,1)S(1)}, u32[]{:S(2)}, u32[]{:S(2)}) collective-permute-start(bf16[1,1,2,128,1024]{4,3,2,0,1:T(8,128)(2,1)S(1)} %bitcast.342), channel_id=1, source_target_pairs={{4,0},{8,4},{12,8},{16,12},{20,16},{24,20},{28,24},{5,1},{9,5},{13... | collective-permute-start | bytes 1572872 | tf_op jit(solution)/shard_map/ppermute | solution.py:17
  10.6 30.5 %collective-permute-start = (bf16[1,1,2,128,1024]{4,3,2,0,1:T(8,128)(2,1)S(1)}, bf16[1,1,2,128,1024]{4,3,2,0,1:T(8,128)(2,1)}, u32[]{:S(2)}, u32[]{:S(2)}) collective-permute-start(bf16[1,1,2,128,1024]{4,3,2,0,1:T(8,128)(2,1)S(1)} %bitcast.343), channel_id=1, source_target_pairs={{0,4},{4,8},{8,12},{12,16},{16,20},{20,24},{24,28},{1,5},{5,9},{9,... | collective-permute-start | bytes 1572872 | tf_op jit(solution)/shard_map/ppermute | solution.py:17
  17.5 0.8 copy-start.17
  20.1 363.9 %all-reduce.8.cloned.1.call-start = ((), (), s32[]{:S(2)}) async-start(), calls=%async_computation | async-start | bytes 2097152 | tf_op jit(solution)/shard_map/psum | solution.py:190
  21.8 2.5 copy-start.14
  25.4 24.0 %copy-start.10 = (bf16[32,8,32,128]{3,2,1,0:T(8,128)(2,1)S(1)}, bf16[32,8,32,128]{3,2,1,0:T(8,128)(2,1)}, u32[]{:S(2)}) copy-start(bf16[32,8,32,128]{3,2,1,0:T(8,128)(2,1)} %copy.182) | copy-start | bytes 6291460
  26.0 52.0 %copy-start.28 = (pred[2,4,14]{2,1,0:T(4,128)(4,1)}, pred[2,4,14]{2,1,0:T(4,128)(4,1)S(1)}, u32[]{:S(2)}) copy-start(pred[2,4,14]{2,1,0:T(4,128)(4,1)S(1)} %broadcast_compare_fusion.2) | copy-start | bytes 340
  26.7 22.7 %copy-start.15 = (bf16[1,1,2,128,1024]{4,3,2,0,1:T(8,128)(2,1)}, bf16[1,1,2,128,1024]{4,3,2,0,1:T(8,128)(2,1)S(1)}, u32[]{:S(2)}) copy-start(bf16[1,1,2,128,1024]{4,3,2,0,1:T(8,128)(2,1)S(1)} %collective-permute-done.2) | copy-start | bytes 1572868
  42.4 29.3 %collective-permute-start.1 = (bf16[2,1,2,128,1024]{4,3,2,0,1:T(8,128)(2,1)S(1)}, bf16[2,1,2,128,1024]{4,3,2,0,1:T(8,128)(2,1)S(1)}, u32[]{:S(2)}, u32[]{:S(2)}) collective-permute-start(bf16[2,1,2,128,1024]{4,3,2,0,1:T(8,128)(2,1)S(1)} %get-tuple-element.40), channel_id=1, source_target_pairs={{0,8},{4,12},{8,16},{12,20},{16,24},{20,28},{1,9},{5,13},{9,17},{1... | collective-permute-start | bytes 3145736 | tf_op jit(solution)/shard_map/ppermute | solution.py:17
  46.7 30.3 %collective-permute-start.3 = (bf16[2,1,2,128,1024]{4,3,2,0,1:T(8,128)(2,1)S(1)}, bf16[2,1,2,128,1024]{4,3,2,0,1:T(8,128)(2,1)S(1)}, u32[]{:S(2)}, u32[]{:S(2)}) collective-permute-start(bf16[2,1,2,128,1024]{4,3,2,0,1:T(8,128)(2,1)S(1)} %get-tuple-element.41), channel_id=1, source_target_pairs={{8,0},{12,4},{16,8},{20,12},{24,16},{28,20},{9,1},{13,5},{17,9},{2... | collective-permute-start | bytes 3145736 | tf_op jit(solution)/shard_map/ppermute | solution.py:17
  52.5 24.5 %copy-start.16 = (bf16[1,1,2,128,1024]{4,3,2,0,1:T(8,128)(2,1)S(1)}, bf16[1,1,2,128,1024]{4,3,2,0,1:T(8,128)(2,1)}, u32[]{:S(2)}) copy-start(bf16[1,1,2,128,1024]{4,3,2,0,1:T(8,128)(2,1)} %copy-done.15) | copy-start | bytes 1572868
  73.8 4.2 %copy-start.18 = (bf16[1,2,128,1024]{3,1,2,0:T(2,128)(2,1)S(1)}, bf16[1,2,128,1024]{3,1,2,0:T(2,128)(2,1)}, u32[]{:S(2)}) copy-start(bf16[1,2,128,1024]{3,1,2,0:T(2,128)(2,1)} %copy-done.17) | copy-start | bytes 1572868
  122.2 11.1 %copy-start.6 = (bf16[768,4,128]{2,1,0:T(4,128)(2,1)}, bf16[768,4,128]{2,1,0:T(4,128)(2,1)S(1)}, u32[]{:S(2)}) copy-start(bf16[768,4,128]{2,1,0:T(4,128)(2,1)S(1)} %reshape.1045) | copy-start | bytes 2359300
  133.3 3.2 copy-start.23
  136.5 4.8 %copy-start.26 = (bf16[768,4,128,1]{0,2,3,1:T(8,128)(2,1)S(1)}, bf16[768,4,128,1]{0,2,3,1:T(8,128)(2,1)}, u32[]{:S(2)}) copy-start(bf16[768,4,128,1]{0,2,3,1:T(8,128)(2,1)} %copy.148) | copy-start | bytes 2359300
  141.3 5.2 %copy-start.24 = (bf16[1,1,128,4,8,128]{5,4,3,2,1,0:T(8,128)(2,1)S(1)}, bf16[1,1,128,4,8,128]{5,4,3,2,1,0:T(8,128)(2,1)}, u32[]{:S(2)}) copy-start(bf16[1,1,128,4,8,128]{5,4,3,2,1,0:T(8,128)(2,1)} %get-tuple-element.29) | copy-start | bytes 3145732
  146.5 7.3 %copy-start.19 = (f32[1,768,4,128]{3,1,2,0:T(8,128)S(1)}, f32[1,768,4,128]{3,1,2,0:T(8,128)}, u32[]{:S(2)}) copy-start(f32[1,768,4,128]{3,1,2,0:T(8,128)} %fusion.42) | copy-start | bytes 4718596
  146.5 10.4 %copy-start.8 = (bf16[1,1,128,4,8,128]{5,4,3,2,1,0:T(8,128)(2,1)S(1)}, bf16[1,1,128,4,8,128]{5,4,3,2,1,0:T(8,128)(2,1)}, u32[]{:S(2)}) copy-start(bf16[1,1,128,4,8,128]{5,4,3,2,1,0:T(8,128)(2,1)} %get-tuple-element.27) | copy-start | bytes 3145732
  153.8 3.1 copy-start.1
  169.0 3.2 copy-start.21
  172.2 4.8 %copy-start.25 = (bf16[768,4,128,1]{0,2,3,1:T(8,128)(2,1)S(1)}, bf16[768,4,128,1]{0,2,3,1:T(8,128)(2,1)}, u32[]{:S(2)}) copy-start(bf16[768,4,128,1]{0,2,3,1:T(8,128)(2,1)} %copy.141) | copy-start | bytes 2359300
  177.0 5.2 %copy-start.22 = (bf16[1,1,128,4,8,128]{5,4,3,2,1,0:T(8,128)(2,1)S(1)}, bf16[1,1,128,4,8,128]{5,4,3,2,1,0:T(8,128)(2,1)}, u32[]{:S(2)}) copy-start(bf16[1,1,128,4,8,128]{5,4,3,2,1,0:T(8,128)(2,1)} %get-tuple-element.28) | copy-start | bytes 3145732
  182.2 7.1 %copy-start.20 = (f32[1,768,4,128]{3,1,2,0:T(8,128)S(1)}, f32[1,768,4,128]{3,1,2,0:T(8,128)}, u32[]{:S(2)}) copy-start(f32[1,768,4,128]{3,1,2,0:T(8,128)} %fusion.39) | copy-start | bytes 4718596
  189.3 3.0 copy-start.2
  198.7 2.5 copy-start.12
  198.7 3.5 copy-start.29
  202.2 5.7 %copy-start.3 = (f32[1,6,128,1024]{3,1,2,0:T(8,128)}, f32[1,6,128,1024]{3,1,2,0:T(8,128)S(1)}, u32[]{:S(2)}) copy-start(f32[1,6,128,1024]{3,1,2,0:T(8,128)S(1)} %copy_dynamic-update-slice_fusion.2) | copy-start | bytes 9437188
  202.2 5.7 %copy-start.4 = (f32[1,6,128,1024]{3,1,2,0:T(8,128)S(1)}, f32[1,6,128,1024]{3,1,2,0:T(8,128)}, u32[]{:S(2)}) copy-start(f32[1,6,128,1024]{3,1,2,0:T(8,128)} %copy_dynamic-update-slice_fusion.1) | copy-start | bytes 9437188
  202.2 5.7 %copy-start.11 = (f32[1,768,4,128]{3,2,0,1:T(4,128)S(1)}, f32[1,768,4,128]{3,2,0,1:T(4,128)}, u32[]{:S(2)}) copy-start(f32[1,768,4,128]{3,2,0,1:T(4,128)} %copy.127) | copy-start | bytes 4718596
  208.9 2.0 copy-start.5
  217.6 4.5 %copy-start = (f32[1,14,128,1024]{3,1,2,0:T(8,128)}, f32[1,14,128,1024]{3,1,2,0:T(8,128)S(1)}, u32[]{:S(2)}) copy-start(f32[1,14,128,1024]{3,1,2,0:T(8,128)S(1)} %add_bitcast_fusion) | copy-start | bytes 22020100
  229.6 63.7 %collective-permute-start.4 = (f32[2,1,2,128,1024]{4,2,3,1,0:T(2,128)}, f32[2,1,2,128,1024]{4,2,3,1,0:T(2,128)}, u32[]{:S(2)}, u32[]{:S(2)}) collective-permute-start(f32[2,1,2,128,1024]{4,2,3,1,0:T(2,128)} %copy.132), channel_id=1, source_target_pairs={{8,0},{12,4},{16,8},{20,12},{24,16},{28,20},{9,1},{13,5},{17,9},{2... | collective-permute-start | bytes 6291464 | tf_op jit(solution)/shard_map/ppermute | solution.py:17
  243.9 62.5 %collective-permute-start.6 = (f32[2,1,2,128,1024]{4,2,3,1,0:T(2,128)}, f32[2,1,2,128,1024]{4,2,3,1,0:T(2,128)S(1)}, u32[]{:S(2)}, u32[]{:S(2)}) collective-permute-start(f32[2,1,2,128,1024]{4,2,3,1,0:T(2,128)} %copy.135), channel_id=1, source_target_pairs={{0,8},{4,12},{8,16},{12,20},{16,24},{20,28},{1,9},{5,13},{9,17},{1... | collective-permute-start | bytes 6291464 | tf_op jit(solution)/shard_map/ppermute | solution.py:17
  254.9 6.7 %slice-start = ((s8[6291456]{0:T(1024)(128)(4,1)}), s8[4194304]{0:T(1024)(128)(4,1)S(1)}, s32[]{:S(2)}) async-start(s8[6291456]{0:T(1024)(128)(4,1)} %bitcast.324), calls=%async_computation.2 | async-start | bytes 8388608
  257.4 4.3 %slice-start.1 = ((s8[6291456]{0:T(1024)(128)(4,1)}), s8[2097152]{0:T(1024)(128)(4,1)S(1)}, s32[]{:S(2)}) async-start(s8[6291456]{0:T(1024)(128)(4,1)} %bitcast.324), calls=%async_computation.3 | async-start | bytes 4194304
  259.2 2.5 copy-start.7
  259.2 5.4 %slice-start.2 = ((s8[6291456]{0:T(1024)(128)(4,1)}), s8[4194304]{0:T(1024)(128)(4,1)S(1)}, s32[]{:S(2)}) async-start(s8[6291456]{0:T(1024)(128)(4,1)} %bitcast.326), calls=%async_computation.4 | async-start | bytes 8388608
  261.7 2.9 slice-start.3
  296.2 90.5 %collective-permute-start.5 = (f32[1,1,2,128,1024]{4,2,3,1,0:T(2,128)S(1)}, f32[1,1,2,128,1024]{4,2,3,1,0:T(2,128)}, u32[]{:S(2)}, u32[]{:S(2)}) collective-permute-start(f32[1,1,2,128,1024]{4,2,3,1,0:T(2,128)S(1)} %slice.193), channel_id=1, source_target_pairs={{4,0},{8,4},{12,8},{16,12},{20,16},{24,20},{28,24},{5,1},{9,5},{13... | collective-permute-start | bytes 3145736 | tf_op jit(solution)/shard_map/ppermute | solution.py:17
  307.5 6.1 %copy-start.9 = (f32[2,1,2,128,1024]{4,2,3,1,0:T(2,128)}, f32[2,1,2,128,1024]{4,2,3,1,0:T(2,128)S(1)}, u32[]{:S(2)}) copy-start(f32[2,1,2,128,1024]{4,2,3,1,0:T(2,128)S(1)} %fusion.29) | copy-start | bytes 6291460
  308.6 78.0 %collective-permute-start.7 = (f32[1,1,2,128,1024]{4,2,3,1,0:T(2,128)}, f32[1,1,2,128,1024]{4,2,3,1,0:T(2,128)}, u32[]{:S(2)}, u32[]{:S(2)}) collective-permute-start(f32[1,1,2,128,1024]{4,2,3,1,0:T(2,128)} %slice.197), channel_id=1, source_target_pairs={{0,4},{4,8},{8,12},{12,16},{16,20},{20,24},{24,28},{1,5},{5,9},{9,... | collective-permute-start | bytes 3145736 | tf_op jit(solution)/shard_map/ppermute | solution.py:17
  313.8 70.2 %copy-start.31 = (f32[2]{0:T(128)S(1)}, f32[2]{0:T(128)}, u32[]{:S(2)}) copy-start(f32[2]{0:T(128)} %compare_convert_fusion) | copy-start | bytes 28
Sparse Core Ops, SparseCore 0:
  20.2 84.7 all-reduce.9
  236.5 107.9 all-reduce.7
where the time goes:
time: 409 us; the launch traced here: 405 us
  local copies, waits for them, and re-layouts  100 us (24%)
  waiting for transfers between devices  95.9 us (23%)
  matrix products  67.1 us (16%)
  blocking collectives  62.7 us (15%)
  other arithmetic  37.7 us (9%)
  starting transfers between devices  25.1 us (6%)
  between operations  15.9 us (4%)
    ppermute x8, waiting for transfers between devices, from_behind(): lax.ppermute(value, axis, [(source, source + steps) for source in range(i...  72 us
    psum x1, blocking collectives, body(): bias_total = lax.psum(local_bias, ('ctx', 'dp'))  62.7 us
    ppermute x8, starting transfers between devices, from_behind(): lax.ppermute(value, axis, [(source, source + steps) for source in range(i...  25 us
    psum x1, waiting for transfers between devices, broadcast(): return lax.psum(kept, axis)  23.8 us
    dot_general x2, matrix products, attend(): jnp.einsum('tqkgd,tskd->tkgqs', grad_rows, cand_vals, preferred_element_t...  14.3 us
    unnamed x78, local copies, waits for them, and re-layouts  14.2 us
    dot_general x2, matrix products, body(): jnp.einsum('dn,tdbf->tnbf', chooser[half_idx].astype(jnp.float32), contri...  12.4 us
    slice x4, local copies, waits for them, and re-layouts, body(): lower_acc[stride:2 * stride]  11.4 us
  transfers between devices with their start and end apart: 10, of which 6 were waited for; matrix products, arithmetic and copies ran while one was open for 17% of the time, Pallas kernels for 0%

commit v1 on v0

v1 whole, which is shorter than its diff:
```python
import functools
import math

import jax
import jax.numpy as jnp
from jax import lax
from jax.experimental import pallas as pl
from jax.experimental.pallas import tpu as pltpu
from jax.sharding import PartitionSpec as P

HEAD = 128
BLOCK = 128
PROMPT = 2
WINDOW = 3
CAND = PROMPT + WINDOW + 1

LOW, HIGH, L1, U1, L2, U2, EXTRA, L3, U3, SWAP, RELAY = range(11)


def relay_rounds(n):
    known = [0, 2, n // 2 - 1]
    missing = list(range(3, n // 2 - 1))
    rounds = []
    while missing:
        pairs = list(zip(known, missing))
        rounds.append(pairs)
        known = known + [b for _, b in pairs]
        missing = missing[len(pairs) :]
    return rounds


def plan(n):
    up1 = [(s, s + 1) for s in range(n - 1)]
    down1 = [(s, s - 1) for s in range(1, n)]
    up2 = [(s, s + 2) for s in range(n - 2)]
    ring2 = [(s, (s - 2) % n) for s in range(n)]
    down2 = [(s, s - 2) for s in range(2, n)]
    extra = [(0, 4), (1, 5), (n - 1, n - 2)]
    swap = [(1, 0)] + [(s, s ^ 1) for s in range(4, n)]
    relay = [
        [(2 * a + x, 2 * b + x) for a, b in pairs for x in range(2)] for pairs in relay_rounds(n)
    ]
    return up1, down1, up2, ring2, down2, extra, swap, relay


def send(value, pairs):
    return lax.ppermute(value, "ctx", pairs)


def send_back(value, pairs):
    return lax.ppermute(value, "ctx", [(b, a) for a, b in pairs])


def slots(r, n, half):
    def pick(default, *cases):
        out = default
        for cond, value in reversed(cases):
            out = jnp.where(cond, value, out)
        return out

    even = r % 2 == 0
    column = pick(RELAY, (r < 6, EXTRA), (r >= n - 2, U2))
    p0 = pick(
        jnp.where(even, column, SWAP), (r == 0, LOW), (r == 1, L1), (r == 2, L2), (r == 3, L3)
    )
    p1 = pick(
        jnp.where(even, SWAP, column), (r == 0, SWAP), (r == 1, LOW), (r == 2, L1), (r == 3, L2)
    )
    low = [LOW, L1, L2, L3]
    high = [
        HIGH,
        pick(U1, (r == n - 1, LOW)),
        pick(U2, (r == n - 2, EXTRA), (r == n - 1, L1)),
        pick(U3, (r == n - 2, LOW), (r == n - 1, L2)),
    ]
    return [p0, p1] + [jnp.where(half == 0, a, b) for a, b in zip(low, high)]


def attend_kernel(
    n, nbuf, heads, group, rank_ref, blocks_ref, len_ref, q_ref, g_ref, bias_ref, *refs
):
    bufs = refs[:nbuf]
    dq_ref, dbias_ref, own_ref = refs[nbuf : nbuf + 3]
    outs = refs[nbuf + 3 : nbuf + 3 + nbuf - 2]
    kv, acc, probs_buf, ds_buf = refs[nbuf + 3 + nbuf - 2 :]
    t, k, half = pl.program_id(0), pl.program_id(1), pl.program_id(2)
    r = rank_ref[0]
    scale = HEAD ** (-0.5)
    factor = scale * math.log2(math.e)
    block = jnp.where(half == 0, r, 2 * n - 1 - r)
    where_from = slots(r, n, half)
    base = (t * 2 * n + block) * CAND
    ok = []
    for c in range(CAND):
        listed = blocks_ref[base + c] >= 0
        if c < PROMPT:
            listed = listed & (c < block - WINDOW)
        ok.append(listed)

    @pl.when((k == 0) & (half == 0))
    def _():
        for i in range(nbuf):
            kv[i] = bufs[i][0]

    @pl.when(half == 0)
    def _():
        acc[...] = jnp.zeros_like(acc)

    keys = jnp.concatenate([kv[s, k] for s in where_from], axis=0)
    vals = jnp.concatenate([kv[s, heads + k] for s in where_from], axis=0)
    keys_t = keys.T
    queries, grads = [], []
    for g in range(group):
        cols = slice(g * HEAD, (g + 1) * HEAD)
        queries.append((q_ref[0, :, cols].astype(jnp.float32) + bias_ref[:, cols]).astype(jnp.bfloat16))
        grads.append(g_ref[0, :, cols])
    nt = (((1,), (1,)), ((), ()))
    width = 2 * BLOCK
    key_pos = lax.broadcasted_iota(jnp.int32, (BLOCK, width), 0)
    query_pos = lax.broadcasted_iota(jnp.int32, (BLOCK, width), 1) % BLOCK
    causal = key_pos <= query_pos
    live = block * BLOCK + query_pos[:1] < len_ref[t]
    for pair in range(group // 2):
        q_two = jnp.concatenate(queries[2 * pair : 2 * pair + 2], axis=0)
        g_two = jnp.concatenate(grads[2 * pair : 2 * pair + 2], axis=0)
        scores = lax.dot_general(keys, q_two, nt, preferred_element_type=jnp.float32)
        parts = []
        for c in range(CAND):
            part = scores[c * BLOCK : (c + 1) * BLOCK]
            if c == PROMPT:
                parts.append(jnp.where(causal, part, -1e30))
            else:
                parts.append(jnp.where(ok[c], part, -1e30))
        scores = jnp.concatenate(parts, axis=0)
        top = jnp.max(scores, axis=0, keepdims=True)
        probs = jnp.exp2((scores - top) * factor)
        total = jnp.sum(probs, axis=0, keepdims=True)
        probs = probs * jnp.where(live, 1.0 / total, 0.0)
        probs_low = probs.astype(jnp.bfloat16)
        grad_probs = lax.dot_general(vals, g_two, nt, preferred_element_type=jnp.float32)
        row_dot = jnp.sum(probs_low.astype(jnp.float32) * grad_probs, axis=0, keepdims=True)
        grad_scores = (probs * (grad_probs - row_dot)).astype(jnp.bfloat16)
        span = slice(pair * width, (pair + 1) * width)
        probs_buf[:, span] = probs_low
        ds_buf[:, span] = grad_scores
        dq = scale * jnp.dot(keys_t, grad_scores, preferred_element_type=jnp.float32)
        for i in range(2):
            cols = slice((2 * pair + i) * HEAD, (2 * pair + i + 1) * HEAD)
            dq_head = dq[:, i * BLOCK : (i + 1) * BLOCK].T
            dq_ref[0, :, cols] = dq_head.astype(jnp.bfloat16)
            row = jnp.sum(dq_head, axis=0, keepdims=True)

            @pl.when((half == 0) & (t == 0))
            def _():
                dbias_ref[:, cols] = row

            @pl.when((half != 0) | (t != 0))
            def _():
                dbias_ref[:, cols] += row

    q_all = jnp.concatenate(queries, axis=0)
    g_all = jnp.concatenate(grads, axis=0)
    dk = scale * jnp.dot(ds_buf[...], q_all, preferred_element_type=jnp.float32)
    dv = jnp.dot(probs_buf[...], g_all, preferred_element_type=jnp.float32)
    for c in range(CAND):
        rows = slice(c * BLOCK, (c + 1) * BLOCK)
        acc[where_from[c], 0] += dk[rows]
        acc[where_from[c], 1] += dv[rows]

    @pl.when(half == 1)
    def _():
        for i in range(2):
            own_ref[0, i, :, 0] = acc[i]
        for i, out in enumerate(outs):
            out[0, :, 0] = acc[i + 2].astype(out.dtype)


def attend(n, heads, group, rank, blocks, lens, query_in, grad_out, bias, bufs):
    traces = query_in.shape[0]
    nbuf = len(bufs)
    width = group * HEAD
    row_spec = pl.BlockSpec((1, BLOCK, width), lambda t, k, j, *_: (t, j, k))
    bias_spec = pl.BlockSpec((1, width), lambda t, k, j, *_: (0, k))
    buf_spec = pl.BlockSpec((1, 2 * heads, BLOCK, HEAD), lambda t, k, j, *_: (t, 0, 0, 0))
    own_spec = pl.BlockSpec(
        (1, 2, 2, 1, BLOCK, HEAD), lambda t, k, j, *_: (t, 0, 0, k, 0, 0)
    )
    out_spec = pl.BlockSpec((1, 2, 1, BLOCK, HEAD), lambda t, k, j, *_: (t, 0, k, 0, 0))
    out_shape = [
        jax.ShapeDtypeStruct(query_in.shape, jnp.bfloat16),
        jax.ShapeDtypeStruct((1, heads * width), jnp.float32),
        jax.ShapeDtypeStruct((traces, 2, 2, heads, BLOCK, HEAD), jnp.float32),
    ] + [jax.ShapeDtypeStruct((traces, 2, heads, BLOCK, HEAD), jnp.bfloat16)] * (nbuf - 2)
    return pl.pallas_call(
        functools.partial(attend_kernel, n, nbuf, heads, group),
        out_shape=out_shape,
        grid_spec=pltpu.PrefetchScalarGridSpec(
            num_scalar_prefetch=3,
            grid=(traces, heads, 2),
            in_specs=[row_spec, row_spec, bias_spec] + [buf_spec] * nbuf,
            out_specs=[row_spec, bias_spec, own_spec] + [out_spec] * (nbuf - 2),
            scratch_shapes=[
                pltpu.VMEM((nbuf, 2 * heads, BLOCK, HEAD), jnp.bfloat16),
                pltpu.VMEM((nbuf, 2, BLOCK, HEAD), jnp.float32),
                pltpu.VMEM((CAND * BLOCK, width), jnp.bfloat16),
                pltpu.VMEM((CAND * BLOCK, width), jnp.bfloat16),
            ],
        ),
        compiler_params=pltpu.CompilerParams(
            dimension_semantics=("arbitrary", "arbitrary", "arbitrary"),
            vmem_limit_bytes=56 * 1024 * 1024,
        ),
        name="attend",
    )(rank, blocks, lens, query_in, grad_out, bias, *bufs)


def butterfly(value, axis):
    count = lax.axis_size(axis)
    stride = 1
    while stride < count:
        value = value + lax.ppermute(value, axis, [(s, s ^ stride) for s in range(count)])
        stride *= 2
    return value


def body(query_in, key_in, value_rows_input, grad_out, query_bias, key_blocks, trace_len):
    n = lax.axis_size("ctx")
    assert n >= 8 and n & (n - 1) == 0
    r = lax.axis_index("ctx")
    traces, _, width_q = query_in.shape
    width_kv = key_in.shape[-1]
    heads = width_kv // HEAD
    group = width_q // width_kv
    up1, down1, up2, ring2, down2, extra, swap, relay = plan(n)

    halves = jnp.concatenate([key_in, value_rows_input], axis=-1).reshape(
        traces, 2, BLOCK, 2 * heads, HEAD
    )
    low = halves[:, 0].transpose(0, 2, 1, 3)
    high = halves[:, 1].transpose(0, 2, 1, 3)
    in_l1 = send(low, up1)
    in_u1 = send(high, down1)
    in_l2 = send(low, up2)
    in_u2 = send(jnp.where(r < 2, low, high), ring2)
    in_ex = send(low, extra)
    column = jnp.where(r < 2, low, jnp.where(r < 6, in_ex, in_u2))
    bufs_relay = []
    for pairs in relay:
        got = send(column, pairs)
        targets = functools.reduce(jnp.logical_or, [r == b for _, b in pairs])
        column = jnp.where(targets, got, column)
    if relay:
        bufs_relay = [column]
    in_l3 = send(in_l1, up2)
    in_u3 = send(jnp.where(r == n - 1, low, in_u1), down2)
    in_sw = send(column, swap)
    bufs = [low, high, in_l1, in_u1, in_l2, in_u2, in_ex, in_l3, in_u3, in_sw] + bufs_relay

    dq, dbias, own, *outs = attend(
        n,
        heads,
        group,
        r.reshape(1).astype(jnp.int32),
        key_blocks.reshape(-1),
        trace_len,
        query_in,
        grad_out,
        query_bias.reshape(1, -1),
        bufs,
    )
    d_l1, d_u1, d_l2, d_u2, d_ex, d_l3, d_u3, d_sw = outs[:8]
    f32 = jnp.float32
    bf16 = jnp.bfloat16

    def gate(cond, value):
        return jnp.where(cond, value.astype(f32), 0.0)

    back_l3 = send_back(d_l3, up2)
    back_u3 = send_back(d_u3, down2)
    back_sw = send_back(d_sw, swap)
    back_l2 = send_back(d_l2, up2)
    d_l1 = (d_l1.astype(f32) + back_l3.astype(f32)).astype(bf16)
    d_u1 = (d_u1.astype(f32) + gate(r != n - 1, back_u3)).astype(bf16)
    back_l1 = send_back(d_l1, up1)
    back_u1 = send_back(d_u1, down1)
    if relay:
        d_rl = outs[8].astype(f32) + gate((r >= 6) & (r < n - 2), back_sw)
        d_ex = d_ex.astype(f32) + gate((r >= 4) & (r < 6), back_sw)
        d_u2 = d_u2.astype(f32) + gate(r >= n - 2, back_sw)
        low_extra = jnp.zeros_like(d_rl)
        for pairs in reversed(relay):
            is_from = functools.reduce(jnp.logical_or, [r == b for _, b in pairs])
            got = send_back(jnp.where(is_from, d_rl, 0.0).astype(bf16), pairs).astype(f32)
            low_extra = low_extra + gate(r < 2, got)
            d_ex = d_ex + gate((r >= 4) & (r < 6), got)
            d_u2 = d_u2 + gate(r >= n - 2, got)
            d_rl = d_rl + gate((r >= 6) & (r < n - 2), got)
        d_ex = d_ex.astype(bf16)
        d_u2 = d_u2.astype(bf16)
    else:
        d_ex = (d_ex.astype(f32) + gate((r >= 4) & (r < 6), back_sw)).astype(bf16)
        d_u2 = (d_u2.astype(f32) + gate(r >= n - 2, back_sw)).astype(bf16)
    back_ex = send_back(d_ex, extra)
    back_u2 = send_back(d_u2, ring2)

    low_grad = own[:, 0] + back_l1.astype(f32) + back_l2.astype(f32) + back_ex.astype(f32)
    low_grad = low_grad + gate(r < 2, back_u2) + gate(r == n - 1, back_u3) + gate(r == 1, back_sw)
    if relay:
        low_grad = low_grad + low_extra
    high_grad = own[:, 1] + back_u1.astype(f32) + gate(r >= 2, back_u2)
    both = jnp.stack([low_grad, high_grad], axis=1).astype(bf16)
    both = both.transpose(2, 0, 1, 4, 3, 5).reshape(2, traces, 2 * BLOCK, width_kv)
    bias_total = butterfly(butterfly(dbias.reshape(-1), "dp"), "ctx")
    rows = traces * lax.axis_size("dp") * 2 * BLOCK * n
    return dq, both[0], both[1], bias_total / math.sqrt(rows)


def solution(mesh):
    return jax.shard_map(
        body,
        mesh=mesh,
        in_specs=(
            P("dp", "ctx", None),
            P("dp", "ctx", None),
            P("dp", "ctx", None),
            P("dp", "ctx", None),
            P(),
            P("dp", None, None),
            P("dp"),
        ),
        out_specs=(P("dp", "ctx", None), P("dp", "ctx", None), P("dp", "ctx", None), P()),
        check_vma=False,
    )
```

time: 409 us -> 143 us (0.35)
  local copies, waits for them, and re-layouts: 100 us -> 3.71 us
  waiting for transfers between devices: 95.9 us -> 23.2 us
  matrix products: 67.1 us -> 0 us
  blocking collectives: 62.7 us -> 0 us
  Pallas kernels: 0 us -> 53.5 us
  other arithmetic: 37.7 us -> 7.04 us
  starting transfers between devices: 25.1 us -> 53 us
  between operations: 15.9 us -> 1.7 us
    dot_general x15 -> x0, matrix products: 67.1 us -> none  [the longest x2 14.3 us: attend(): jnp.einsum('tqkgd,tskd->tkgqs', grad_rows, cand_vals, preferred_element_t...]
    psum x1 -> x0, blocking collectives: 62.7 us -> none  [body(): bias_total = lax.psum(local_bias, ('ctx', 'dp'))]
    pallas_call x0 -> x1, Pallas kernels: none -> 53.5 us  [attend(): pl.pallas_call(functools.partial(attend_kernel, n, nbuf, heads, group), o...]
    ppermute x8 -> x21, waiting for transfers between devices: 72 us -> 23.2 us  [the longest x8 12.1 us: send_back(): return lax.ppermute(value, 'ctx', [(b, a) for a, b in pairs])]
    slice x21 -> x4, local copies, waits for them, and re-layouts: 42 us -> 0.49 us  [the longest x3 0.45 us: body(): return (dq, both[0], both[1], bias_total / math.sqrt(rows))]
    ppermute x8 -> x21, starting transfers between devices: 25 us -> 53 us  [the longest x8 24.5 us: send(): return lax.ppermute(value, 'ctx', pairs)]
    psum x2 -> x0, waiting for transfers between devices: 23.8 us -> none  [the longest x1 23.8 us: broadcast(): return lax.psum(kept, axis)]
    another operation x11 -> x0, local copies, waits for them, and re-layouts: 20.5 us -> none
  transfers between devices with their start and end apart: 10 -> 21, of which waited for: 6 -> 8; matrix products, arithmetic and copies ran while one was open for 17% -> 4% of each run, Pallas kernels for 0% -> 0%
where the time goes in v1:
time: 143 us; the launch traced here: 142 us
  Pallas kernels  53.5 us (37%)
  starting transfers between devices  53 us (37%)
  waiting for transfers between devices  23.2 us (16%)
  other arithmetic  7.04 us (5%)
  local copies, waits for them, and re-layouts  3.71 us (3%)
  between operations  1.7 us (1%)
    pallas_call x1, Pallas kernels, attend(): pl.pallas_call(functools.partial(attend_kernel, n, nbuf, heads, group), o...  53.5 us
    ppermute x8, starting transfers between devices, send(): return lax.ppermute(value, 'ctx', pairs)  24.5 us
    ppermute x8, starting transfers between devices, send_back(): return lax.ppermute(value, 'ctx', [(b, a) for a, b in pairs])  18.1 us
    ppermute x8, waiting for transfers between devices, send_back(): return lax.ppermute(value, 'ctx', [(b, a) for a, b in pairs])  12.1 us
    ppermute x5, starting transfers between devices, butterfly(): lax.ppermute(value, axis, [(s, s ^ stride) for s in range(count)])  10.5 us
    ppermute x8, waiting for transfers between devices, send(): return lax.ppermute(value, 'ctx', pairs)  6.08 us
    ppermute x5, waiting for transfers between devices, butterfly(): lax.ppermute(value, axis, [(s, s ^ stride) for s in range(count)])  5.02 us
  transfers between devices with their start and end apart: 21, of which 8 were waited for; matrix products, arithmetic and copies ran while one was open for 4% of the time, Pallas kernels for 0%

profile of v1, /device:TPU:0, one launch (start us, length us, event | category | flops | bytes accessed | tf_op | source)
XLA Modules:
  0.0 142.2 jit_solution(9224724940551107549)
XLA Ops:
  0.6 1.1 maximum_bitcast_fusion
  1.7 0.1 copy.19
  1.9 0.1 broadcast_select_fusion.1
  2.0 5.1 %collective-permute-start.3 = (bf16[1,8,128,128]{3,2,1,0:T(8,128)(2,1)S(1)}, bf16[1,8,128,128]{3,2,1,0:T(8,128)(2,1)S(1)}, u32[]{:S(2)}, u32[]{:S(2)}) collective-permute-start(bf16[1,8,128,128]{3,2,1,0:T(8,128)(2,1)S(1)} %broadcast_select_fusion.1), channel_id=1, source_target_pairs={{0,24},{4,28},{8,0},{12,4},{16,8},{20,12},{24,16},{28,20},{1,25},{... | collective-permute-start | bytes 786440 | tf_op jit(solution)/shard_map/ppermute | solution.py:47
  7.1 1.4 collective-permute-start.4
  8.6 1.3 collective-permute-start.1
  9.9 4.6 %collective-permute-start = (bf16[1,8,128,128]{3,2,1,0:T(8,128)(2,1)S(1)}, bf16[1,8,128,128]{3,2,1,0:T(8,128)(2,1)S(1)}, u32[]{:S(2)}, u32[]{:S(2)}) collective-permute-start(bf16[1,8,128,128]{3,2,1,0:T(8,128)(2,1)S(1)} %bitcast.50), channel_id=1, source_target_pairs={{0,4},{4,8},{8,12},{12,16},{16,20},{20,24},{24,28},{1,5},{5,9},{9,... | collective-permute-start | bytes 786440 | tf_op jit(solution)/shard_map/ppermute | solution.py:47
  14.4 2.8 %collective-permute-start.2 = (bf16[1,8,128,128]{3,2,1,0:T(8,128)(2,1)S(1)}, bf16[1,8,128,128]{3,2,1,0:T(8,128)(2,1)S(1)}, u32[]{:S(2)}, u32[]{:S(2)}) collective-permute-start(bf16[1,8,128,128]{3,2,1,0:T(8,128)(2,1)S(1)} %bitcast.51), channel_id=1, source_target_pairs={{0,8},{4,12},{8,16},{12,20},{16,24},{20,28},{1,9},{5,13},{9,17},{1... | collective-permute-start | bytes 786440 | tf_op jit(solution)/shard_map/ppermute | solution.py:47
  17.3 2.1 %collective-permute-done.4.refs_6_ = bf16[1,8,128,128]{3,2,1,0:T(8,128)(2,1)S(1)} collective-permute-done((bf16[1,8,128,128]{3,2,1,0:T(8,128)(2,1)S(1)}, bf16[1,8,128,128]{3,2,1,0:T(8,128)(2,1)S(1)}, u32[]{:S(2)}, u32[]{:S(2)}) %collective-permute-start.4) | collective-permute-done | bytes 262176 | tf_op jit(solution)/shard_map/ppermute | solution.py:47
  19.4 0.1 select_select_fusion
  19.5 1.3 collective-permute-start.6
  20.8 1.3 collective-permute-start.7
  22.1 1.6 %collective-permute-done.refs_2_ = bf16[1,8,128,128]{3,2,1,0:T(8,128)(2,1)S(1)} collective-permute-done((bf16[1,8,128,128]{3,2,1,0:T(8,128)(2,1)S(1)}, bf16[1,8,128,128]{3,2,1,0:T(8,128)(2,1)S(1)}, u32[]{:S(2)}, u32[]{:S(2)}) %collective-permute-start) | collective-permute-done | bytes 262176 | tf_op jit(solution)/shard_map/ppermute | solution.py:47
  23.7 6.7 %collective-permute-start.5 = (bf16[1,8,128,128]{3,2,1,0:T(8,128)(2,1)S(1)}, bf16[1,8,128,128]{3,2,1,0:T(8,128)(2,1)S(1)}, u32[]{:S(2)}, u32[]{:S(2)}) collective-permute-start(bf16[1,8,128,128]{3,2,1,0:T(8,128)(2,1)S(1)} %collective-permute-done.refs_2_), channel_id=1, source_target_pairs={{0,8},{4,12},{8,16},{12,20},{16,24},{20,28},{1,9},{5,13},{9,17},{1... | collective-permute-start | bytes 786440 | tf_op jit(solution)/shard_map/ppermute | solution.py:47
  30.4 0.1 copy.12
  30.5 0.7 reshape.67.blocks_ref
  31.9 2.4 %collective-permute-done.5.refs_7_ = bf16[1,8,128,128]{3,2,1,0:T(8,128)(2,1)S(1)} collective-permute-done((bf16[1,8,128,128]{3,2,1,0:T(8,128)(2,1)S(1)}, bf16[1,8,128,128]{3,2,1,0:T(8,128)(2,1)S(1)}, u32[]{:S(2)}, u32[]{:S(2)}) %collective-permute-start.5) | collective-permute-done | bytes 262176 | tf_op jit(solution)/shard_map/ppermute | solution.py:47
  34.3 0.6 copy-done.10
  34.9 53.5 %attend.1 = (bf16[1,256,4096]{2,1,0:T(8,128)(2,1)}, f32[1,4096]{1,0:T(1,128)}, f32[1,2,2,4,128,128]{5,4,3,2,1,0:T(8,128)}, bf16[1,2,4,128,128]{4,3,2,1,0:T(8,128...) custom-call(s32[1]{0:T(128)} %bitcast.rank_ref, ...), custom_call_target="tpu_custom_call" | custom-call | tf_op jit(solution)/shard_map/attend/pallas_call | solution.py:194
  88.4 4.5 %collective-permute-start.14 = (bf16[1,2,4,128,128]{4,3,2,1,0:T(8,128)(2,1)}, bf16[1,2,4,128,128]{4,3,2,1,0:T(8,128)(2,1)S(1)}, u32[]{:S(2)}, u32[]{:S(2)}) collective-permute-start(bf16[1,2,4,128,128]{4,3,2,1,0:T(8,128)(2,1)} %get-tuple-element.23), channel_id=1, source_target_pairs={{0,8},{4,12},{8,16},{12,20},{16,24},{20,28},{1,9},{5,13},{9,17},{1... | collective-permute-start | bytes 786440 | tf_op jit(solution)/shard_map/ppermute | solution.py:51
  93.0 0.1 collective-permute-start.16
  93.1 1.4 collective-permute-done.16
  94.5 0.7 add.63
  95.2 1.5 %collective-permute-start.17 = (f32[4096]{0:T(1024)S(1)}, f32[4096]{0:T(1024)S(1)}, u32[]{:S(2)}, u32[]{:S(2)}) collective-permute-start(f32[4096]{0:T(1024)S(1)} %add.63), channel_id=1, source_target_pairs={{0,2},{1,3},{2,0},{3,1},{4,6},{5,7},{6,4},{7,5},{8,10},{9,11},{10,... | collective-permute-start | bytes 49160 | tf_op jit(solution)/shard_map/ppermute | solution.py:221
  96.7 2.2 %collective-permute-done.17 = f32[4096]{0:T(1024)S(1)} collective-permute-done((f32[4096]{0:T(1024)S(1)}, f32[4096]{0:T(1024)S(1)}, u32[]{:S(2)}, u32[]{:S(2)}) %collective-permute-start.17) | collective-permute-done | bytes 16416 | tf_op jit(solution)/shard_map/ppermute | solution.py:221
  98.9 2.4 %collective-permute-start.18 = (f32[4096]{0:T(1024)S(1)}, f32[4096]{0:T(1024)S(1)}, u32[]{:S(2)}, u32[]{:S(2)}) collective-permute-start(f32[4096]{0:T(1024)S(1)} %add.64), channel_id=1, source_target_pairs={{0,4},{4,0},{8,12},{12,8},{16,20},{20,16},{24,28},{28,24},{1,5},{5... | collective-permute-start | bytes 49160 | tf_op jit(solution)/shard_map/ppermute | solution.py:221
  101.3 1.3 collective-permute-start.8
  102.6 0.4 collective-permute-done.18
  103.0 2.3 %collective-permute-start.19 = (f32[4096]{0:T(1024)S(1)}, f32[4096]{0:T(1024)S(1)}, u32[]{:S(2)}, u32[]{:S(2)}) collective-permute-start(f32[4096]{0:T(1024)S(1)} %add.65), channel_id=1, source_target_pairs={{0,8},{4,12},{8,0},{12,4},{16,24},{20,28},{24,16},{28,20},{1,9},{5... | collective-permute-start | bytes 49160 | tf_op jit(solution)/shard_map/ppermute | solution.py:221
  105.3 3.5 %collective-permute-start.11 = (bf16[1,2,4,128,128]{4,3,2,1,0:T(8,128)(2,1)}, bf16[1,2,4,128,128]{4,3,2,1,0:T(8,128)(2,1)S(1)}, u32[]{:S(2)}, u32[]{:S(2)}) collective-permute-start(bf16[1,2,4,128,128]{4,3,2,1,0:T(8,128)(2,1)} %get-tuple-element.21), channel_id=1, source_target_pairs={{0,4},{20,16},{16,20},{28,24},{24,28},{1,5},{21,17},{17,21},{29,25... | collective-permute-start | bytes 786440 | tf_op jit(solution)/shard_map/ppermute | solution.py:51
  108.9 1.3 collective-permute-start.10
  110.2 1.0 collective-permute-done.19
  111.1 4.2 %collective-permute-start.20 = (f32[4096]{0:T(1024)S(1)}, f32[4096]{0:T(1024)S(1)}, u32[]{:S(2)}, u32[]{:S(2)}) collective-permute-start(f32[4096]{0:T(1024)S(1)} %add.66), channel_id=1, source_target_pairs={{0,16},{4,20},{8,24},{12,28},{16,0},{20,4},{24,8},{28,12},{1,17},{... | collective-permute-start | bytes 49160 | tf_op jit(solution)/shard_map/ppermute | solution.py:221
  115.4 1.0 fusion.7
  116.4 1.7 %collective-permute-start.15 = (bf16[1,2,4,128,128]{4,3,2,1,0:T(8,128)(2,1)S(1)}, bf16[1,2,4,128,128]{4,3,2,1,0:T(8,128)(2,1)S(1)}, u32[]{:S(2)}, u32[]{:S(2)}) collective-permute-start(bf16[1,2,4,128,128]{4,3,2,1,0:T(8,128)(2,1)S(1)} %fusion.7), channel_id=1, source_target_pairs={{0,4},{4,8},{8,12},{12,16},{16,20},{20,24},{24,28},{1,5},{5,9},{9,... | collective-permute-start | bytes 786440 | tf_op jit(solution)/shard_map/ppermute | solution.py:51
  118.1 1.0 add_convert_fusion
  119.1 1.3 collective-permute-start.9
  120.4 2.0 %fusion.9 = (bf16[1,2,4,128,128]{4,3,2,1,0:T(8,128)(2,1)}, bf16[1,2,4,128,128]{4,3,2,1,0:T(8,128)(2,1)}) fusion(bf16[1,2,4,128,128]{4,3,2,1,0:T(8,128)(2,1)S(1)} %collective-permute-done.11, bf16[1,2,4,128,128]{4,3,2,1,0:T(8,128)(2,1)} %get-tuple-element.20, pred[]{:T(512)S(6)} %and.4, pred[]{:T(512)S(6)} %ge.10, ...), kind=kLoop, calls=%fused_computation.16 | loop fusion | flops 1179648 | bytes 1310722 | tf_op jit(solution)/shard_map/convert_element_type | solution.py:301
  122.4 1.3 collective-permute-start.12
  123.7 3.3 %collective-permute-start.13 = (bf16[1,2,4,128,128]{4,3,2,1,0:T(8,128)(2,1)}, bf16[1,2,4,128,128]{4,3,2,1,0:T(8,128)(2,1)S(1)}, u32[]{:S(2)}, u32[]{:S(2)}) collective-permute-start(bf16[1,2,4,128,128]{4,3,2,1,0:T(8,128)(2,1)} %get-tuple-element.33), channel_id=1, source_target_pairs={{24,0},{28,4},{0,8},{4,12},{8,16},{12,20},{16,24},{20,28},{25,1},{... | collective-permute-start | bytes 786440 | tf_op jit(solution)/shard_map/ppermute | solution.py:51
  126.9 0.6 add_multiply_fusion
  127.6 12.1 %collective-permute-done.12 = bf16[1,2,4,128,128]{4,3,2,1,0:T(8,128)(2,1)S(1)} collective-permute-done((bf16[1,2,4,128,128]{4,3,2,1,0:T(8,128)(2,1)}, bf16[1,2,4,128,128]{4,3,2,1,0:T(8,128)(2,1)S(1)}, u32[]{:S(2)}, u32[]{:S(2)}) %collective-permute-start.12) | collective-permute-done | bytes 262176 | tf_op jit(solution)/shard_map/ppermute | solution.py:51
  139.7 0.4 fusion.15
  140.0 0.1 maximum_bitcast_fusion.1
  140.1 0.2 copy.15
  140.4 0.8 squeeze.22
  141.2 0.2 copy.16
  141.4 0.8 squeeze.23
  (43 shorter events, 0.3 us)
Async XLA Ops:
  1.8 28.6 %copy-start.11 = (s32[1,16,6]{1,0,2:T(1,128)S(1)}, s32[1,16,6]{1,0,2:T(1,128)}, u32[]{:S(2)}) copy-start(s32[1,16,6]{1,0,2:T(1,128)} %param.12) | copy-start | bytes 1156
  2.0 15.3 %collective-permute-start.3 = (bf16[1,8,128,128]{3,2,1,0:T(8,128)(2,1)S(1)}, bf16[1,8,128,128]{3,2,1,0:T(8,128)(2,1)S(1)}, u32[]{:S(2)}, u32[]{:S(2)}) collective-permute-start(bf16[1,8,128,128]{3,2,1,0:T(8,128)(2,1)S(1)} %broadcast_select_fusion.1), channel_id=1, source_target_pairs={{0,24},{4,28},{8,0},{12,4},{16,8},{20,12},{24,16},{28,20},{1,25},{... | collective-permute-start | bytes 786440 | tf_op jit(solution)/shard_map/ppermute | solution.py:47
  7.1 27.1 %copy-start.4 = (bf16[1,1,128,8,128]{4,2,3,1,0:T(8,128)(2,1)}, bf16[1,1,128,8,128]{4,2,3,1,0:T(8,128)(2,1)S(1)}, u32[]{:S(2)}) copy-start(bf16[1,1,128,8,128]{4,2,3,1,0:T(8,128)(2,1)S(1)} %copy.31) | copy-start | bytes 786436
  7.1 12.3 %collective-permute-start.4 = (bf16[1,8,128,128]{3,2,1,0:T(8,128)(2,1)S(1)}, bf16[1,8,128,128]{3,2,1,0:T(8,128)(2,1)S(1)}, u32[]{:S(2)}, u32[]{:S(2)}) collective-permute-start(bf16[1,8,128,128]{3,2,1,0:T(8,128)(2,1)S(1)} %bitcast.49), channel_id=1, source_target_pairs={{0,16},{4,20},{28,24},{1,17},{5,21},{29,25},{2,18},{6,22},{30,26},... | collective-permute-start | bytes 786440 | tf_op jit(solution)/shard_map/ppermute | solution.py:47
  8.6 25.7 %copy-start.5 = (bf16[1,1,128,8,128]{4,2,3,1,0:T(8,128)(2,1)}, bf16[1,1,128,8,128]{4,2,3,1,0:T(8,128)(2,1)S(1)}, u32[]{:S(2)}) copy-start(bf16[1,1,128,8,128]{4,2,3,1,0:T(8,128)(2,1)S(1)} %copy.30) | copy-start | bytes 786436
  8.6 10.9 %collective-permute-start.1 = (bf16[1,8,128,128]{3,2,1,0:T(8,128)(2,1)S(1)}, bf16[1,8,128,128]{3,2,1,0:T(8,128)(2,1)S(1)}, u32[]{:S(2)}, u32[]{:S(2)}) collective-permute-start(bf16[1,8,128,128]{3,2,1,0:T(8,128)(2,1)S(1)} %bitcast.53), channel_id=1, source_target_pairs={{4,0},{8,4},{12,8},{16,12},{20,16},{24,20},{28,24},{5,1},{9,5},{13... | collective-permute-start | bytes 786440 | tf_op jit(solution)/shard_map/ppermute | solution.py:47
  9.9 13.8 %collective-permute-start = (bf16[1,8,128,128]{3,2,1,0:T(8,128)(2,1)S(1)}, bf16[1,8,128,128]{3,2,1,0:T(8,128)(2,1)S(1)}, u32[]{:S(2)}, u32[]{:S(2)}) collective-permute-start(bf16[1,8,128,128]{3,2,1,0:T(8,128)(2,1)S(1)} %bitcast.50), channel_id=1, source_target_pairs={{0,4},{4,8},{8,12},{12,16},{16,20},{20,24},{24,28},{1,5},{5,9},{9,... | collective-permute-start | bytes 786440 | tf_op jit(solution)/shard_map/ppermute | solution.py:47
  14.4 17.4 %collective-permute-start.2 = (bf16[1,8,128,128]{3,2,1,0:T(8,128)(2,1)S(1)}, bf16[1,8,128,128]{3,2,1,0:T(8,128)(2,1)S(1)}, u32[]{:S(2)}, u32[]{:S(2)}) collective-permute-start(bf16[1,8,128,128]{3,2,1,0:T(8,128)(2,1)S(1)} %bitcast.51), channel_id=1, source_target_pairs={{0,8},{4,12},{8,16},{12,20},{16,24},{20,28},{1,9},{5,13},{9,17},{1... | collective-permute-start | bytes 786440 | tf_op jit(solution)/shard_map/ppermute | solution.py:47
  17.3 17.0 %copy-start.1 = (bf16[1,8,128,128]{3,2,1,0:T(8,128)(2,1)}, bf16[1,8,128,128]{3,2,1,0:T(8,128)(2,1)S(1)}, u32[]{:S(2)}) copy-start(bf16[1,8,128,128]{3,2,1,0:T(8,128)(2,1)S(1)} %collective-permute-done.3.refs_5_) | copy-start | bytes 786436
  19.4 14.8 %copy-start.2 = (bf16[1,8,128,128]{3,2,1,0:T(8,128)(2,1)}, bf16[1,8,128,128]{3,2,1,0:T(8,128)(2,1)S(1)}, u32[]{:S(2)}) copy-start(bf16[1,8,128,128]{3,2,1,0:T(8,128)(2,1)S(1)} %collective-permute-done.4.refs_6_) | copy-start | bytes 786436
  19.4 14.8 %copy-start.3 = (bf16[1,8,128,128]{3,2,1,0:T(8,128)(2,1)}, bf16[1,8,128,128]{3,2,1,0:T(8,128)(2,1)S(1)}, u32[]{:S(2)}) copy-start(bf16[1,8,128,128]{3,2,1,0:T(8,128)(2,1)S(1)} %collective-permute-done.1.refs_3_) | copy-start | bytes 786436
  19.5 12.3 %collective-permute-start.6 = (bf16[1,8,128,128]{3,2,1,0:T(8,128)(2,1)S(1)}, bf16[1,8,128,128]{3,2,1,0:T(8,128)(2,1)S(1)}, u32[]{:S(2)}, u32[]{:S(2)}) collective-permute-start(bf16[1,8,128,128]{3,2,1,0:T(8,128)(2,1)S(1)} %get-tuple-element.35), channel_id=1, source_target_pairs={{8,0},{12,4},{16,8},{20,12},{24,16},{28,20},{9,1},{13,5},{17,9},{2... | collective-permute-start | bytes 786440 | tf_op jit(solution)/shard_map/ppermute | solution.py:47
  20.8 11.0 %collective-permute-start.7 = (bf16[1,8,128,128]{3,2,1,0:T(8,128)(2,1)S(1)}, bf16[1,8,128,128]{3,2,1,0:T(8,128)(2,1)S(1)}, u32[]{:S(2)}, u32[]{:S(2)}) collective-permute-start(bf16[1,8,128,128]{3,2,1,0:T(8,128)(2,1)S(1)} %get-tuple-element.34), channel_id=1, source_target_pairs={{4,0},{16,20},{20,16},{24,28},{28,24},{5,1},{17,21},{21,17},{25,29... | collective-permute-start | bytes 786440 | tf_op jit(solution)/shard_map/ppermute | solution.py:47
  23.7 10.6 %copy-start.6 = (bf16[1,8,128,128]{3,2,1,0:T(8,128)(2,1)}, bf16[1,8,128,128]{3,2,1,0:T(8,128)(2,1)S(1)}, u32[]{:S(2)}) copy-start(bf16[1,8,128,128]{3,2,1,0:T(8,128)(2,1)S(1)} %collective-permute-done.refs_2_) | copy-start | bytes 786436
  23.7 10.5 %collective-permute-start.5 = (bf16[1,8,128,128]{3,2,1,0:T(8,128)(2,1)S(1)}, bf16[1,8,128,128]{3,2,1,0:T(8,128)(2,1)S(1)}, u32[]{:S(2)}, u32[]{:S(2)}) collective-permute-start(bf16[1,8,128,128]{3,2,1,0:T(8,128)(2,1)S(1)} %collective-permute-done.refs_2_), channel_id=1, source_target_pairs={{0,8},{4,12},{8,16},{12,20},{16,24},{20,28},{1,9},{5,13},{9,17},{1... | collective-permute-start | bytes 786440 | tf_op jit(solution)/shard_map/ppermute | solution.py:47
  31.8 2.5 %copy-start.7 = (bf16[1,8,128,128]{3,2,1,0:T(8,128)(2,1)}, bf16[1,8,128,128]{3,2,1,0:T(8,128)(2,1)S(1)}, u32[]{:S(2)}) copy-start(bf16[1,8,128,128]{3,2,1,0:T(8,128)(2,1)S(1)} %collective-permute-done.2.refs_4_) | copy-start | bytes 786436
  31.8 2.5 %copy-start.8 = (bf16[1,8,128,128]{3,2,1,0:T(8,128)(2,1)}, bf16[1,8,128,128]{3,2,1,0:T(8,128)(2,1)S(1)}, u32[]{:S(2)}) copy-start(bf16[1,8,128,128]{3,2,1,0:T(8,128)(2,1)S(1)} %collective-permute-done.6.refs_8_) | copy-start | bytes 786436
  31.9 2.4 %copy-start.9 = (bf16[1,8,128,128]{3,2,1,0:T(8,128)(2,1)}, bf16[1,8,128,128]{3,2,1,0:T(8,128)(2,1)S(1)}, u32[]{:S(2)}) copy-start(bf16[1,8,128,128]{3,2,1,0:T(8,128)(2,1)S(1)} %collective-permute-done.7.refs_9_) | copy-start | bytes 786436
  34.2 0.7 copy-start.10
  88.4 51.2 %copy-start = (f32[1,2,2,4,128,128]{5,4,3,2,1,0:T(8,128)S(1)}, f32[1,2,2,4,128,128]{5,4,3,2,1,0:T(8,128)}, u32[]{:S(2)}) copy-start(f32[1,2,2,4,128,128]{5,4,3,2,1,0:T(8,128)} %get-tuple-element.16) | copy-start | bytes 3145732
  88.4 26.9 %collective-permute-start.14 = (bf16[1,2,4,128,128]{4,3,2,1,0:T(8,128)(2,1)}, bf16[1,2,4,128,128]{4,3,2,1,0:T(8,128)(2,1)S(1)}, u32[]{:S(2)}, u32[]{:S(2)}) collective-permute-start(bf16[1,2,4,128,128]{4,3,2,1,0:T(8,128)(2,1)} %get-tuple-element.23), channel_id=1, source_target_pairs={{0,8},{4,12},{8,16},{12,20},{16,24},{20,28},{1,9},{5,13},{9,17},{1... | collective-permute-start | bytes 786440 | tf_op jit(solution)/shard_map/ppermute | solution.py:51
  93.0 1.5 %collective-permute-start.16 = (f32[4096]{0:T(1024)}, f32[4096]{0:T(1024)S(1)}, u32[]{:S(2)}, u32[]{:S(2)}) collective-permute-start(f32[4096]{0:T(1024)} %bitcast.56), channel_id=1, source_target_pairs={{0,1},{1,0},{2,3},{3,2},{4,5},{5,4},{6,7},{7,6},{8,9},{9,8},{10,11... | collective-permute-start | bytes 49160 | tf_op jit(solution)/shard_map/ppermute | solution.py:221
  95.2 3.7 %collective-permute-start.17 = (f32[4096]{0:T(1024)S(1)}, f32[4096]{0:T(1024)S(1)}, u32[]{:S(2)}, u32[]{:S(2)}) collective-permute-start(f32[4096]{0:T(1024)S(1)} %add.63), channel_id=1, source_target_pairs={{0,2},{1,3},{2,0},{3,1},{4,6},{5,7},{6,4},{7,5},{8,10},{9,11},{10,... | collective-permute-start | bytes 49160 | tf_op jit(solution)/shard_map/ppermute | solution.py:221
  98.9 4.1 %collective-permute-start.18 = (f32[4096]{0:T(1024)S(1)}, f32[4096]{0:T(1024)S(1)}, u32[]{:S(2)}, u32[]{:S(2)}) collective-permute-start(f32[4096]{0:T(1024)S(1)} %add.64), channel_id=1, source_target_pairs={{0,4},{4,0},{8,12},{12,8},{16,20},{20,16},{24,28},{28,24},{1,5},{5... | collective-permute-start | bytes 49160 | tf_op jit(solution)/shard_map/ppermute | solution.py:221
  101.3 16.7 %collective-permute-start.8 = (bf16[1,2,4,128,128]{4,3,2,1,0:T(8,128)(2,1)}, bf16[1,2,4,128,128]{4,3,2,1,0:T(8,128)(2,1)S(1)}, u32[]{:S(2)}, u32[]{:S(2)}) collective-permute-start(bf16[1,2,4,128,128]{4,3,2,1,0:T(8,128)(2,1)} %get-tuple-element.18), channel_id=1, source_target_pairs={{8,0},{12,4},{16,8},{20,12},{24,16},{28,20},{9,1},{13,5},{17,9},{2... | collective-permute-start | bytes 786440 | tf_op jit(solution)/shard_map/ppermute | solution.py:51
  103.0 8.1 %collective-permute-start.19 = (f32[4096]{0:T(1024)S(1)}, f32[4096]{0:T(1024)S(1)}, u32[]{:S(2)}, u32[]{:S(2)}) collective-permute-start(f32[4096]{0:T(1024)S(1)} %add.65), channel_id=1, source_target_pairs={{0,8},{4,12},{8,0},{12,4},{16,24},{20,28},{24,16},{28,20},{1,9},{5... | collective-permute-start | bytes 49160 | tf_op jit(solution)/shard_map/ppermute | solution.py:221
  105.3 15.1 %collective-permute-start.11 = (bf16[1,2,4,128,128]{4,3,2,1,0:T(8,128)(2,1)}, bf16[1,2,4,128,128]{4,3,2,1,0:T(8,128)(2,1)S(1)}, u32[]{:S(2)}, u32[]{:S(2)}) collective-permute-start(bf16[1,2,4,128,128]{4,3,2,1,0:T(8,128)(2,1)} %get-tuple-element.21), channel_id=1, source_target_pairs={{0,4},{20,16},{16,20},{28,24},{24,28},{1,5},{21,17},{17,21},{29,25... | collective-permute-start | bytes 786440 | tf_op jit(solution)/shard_map/ppermute | solution.py:51
  108.9 18.7 %collective-permute-start.10 = (bf16[1,2,4,128,128]{4,3,2,1,0:T(8,128)(2,1)}, bf16[1,2,4,128,128]{4,3,2,1,0:T(8,128)(2,1)S(1)}, u32[]{:S(2)}, u32[]{:S(2)}) collective-permute-start(bf16[1,2,4,128,128]{4,3,2,1,0:T(8,128)(2,1)} %get-tuple-element.19), channel_id=1, source_target_pairs={{8,0},{12,4},{16,8},{20,12},{24,16},{28,20},{9,1},{13,5},{17,9},{2... | collective-permute-start | bytes 786440 | tf_op jit(solution)/shard_map/ppermute | solution.py:51
  111.1 12.5 %collective-permute-start.20 = (f32[4096]{0:T(1024)S(1)}, f32[4096]{0:T(1024)S(1)}, u32[]{:S(2)}, u32[]{:S(2)}) collective-permute-start(f32[4096]{0:T(1024)S(1)} %add.66), channel_id=1, source_target_pairs={{0,16},{4,20},{8,24},{12,28},{16,0},{20,4},{24,8},{28,12},{1,17},{... | collective-permute-start | bytes 49160 | tf_op jit(solution)/shard_map/ppermute | solution.py:221
  116.4 11.2 %collective-permute-start.15 = (bf16[1,2,4,128,128]{4,3,2,1,0:T(8,128)(2,1)S(1)}, bf16[1,2,4,128,128]{4,3,2,1,0:T(8,128)(2,1)S(1)}, u32[]{:S(2)}, u32[]{:S(2)}) collective-permute-start(bf16[1,2,4,128,128]{4,3,2,1,0:T(8,128)(2,1)S(1)} %fusion.7), channel_id=1, source_target_pairs={{0,4},{4,8},{8,12},{12,16},{16,20},{20,24},{24,28},{1,5},{5,9},{9,... | collective-permute-start | bytes 786440 | tf_op jit(solution)/shard_map/ppermute | solution.py:51
  119.1 8.5 %collective-permute-start.9 = (bf16[1,2,4,128,128]{4,3,2,1,0:T(8,128)(2,1)S(1)}, bf16[1,2,4,128,128]{4,3,2,1,0:T(8,128)(2,1)S(1)}, u32[]{:S(2)}, u32[]{:S(2)}) collective-permute-start(bf16[1,2,4,128,128]{4,3,2,1,0:T(8,128)(2,1)S(1)} %add_convert_fusion), channel_id=1, source_target_pairs={{4,0},{8,4},{12,8},{16,12},{20,16},{24,20},{28,24},{5,1},{9,5},{13... | collective-permute-start | bytes 786440 | tf_op jit(solution)/shard_map/ppermute | solution.py:51
  122.4 17.3 %collective-permute-start.12 = (bf16[1,2,4,128,128]{4,3,2,1,0:T(8,128)(2,1)}, bf16[1,2,4,128,128]{4,3,2,1,0:T(8,128)(2,1)S(1)}, u32[]{:S(2)}, u32[]{:S(2)}) collective-permute-start(bf16[1,2,4,128,128]{4,3,2,1,0:T(8,128)(2,1)} %get-tuple-element.32), channel_id=1, source_target_pairs={{16,0},{20,4},{24,28},{17,1},{21,5},{25,29},{18,2},{22,6},{26,30},... | collective-permute-start | bytes 786440 | tf_op jit(solution)/shard_map/ppermute | solution.py:51
  123.7 16.0 %collective-permute-start.13 = (bf16[1,2,4,128,128]{4,3,2,1,0:T(8,128)(2,1)}, bf16[1,2,4,128,128]{4,3,2,1,0:T(8,128)(2,1)S(1)}, u32[]{:S(2)}, u32[]{:S(2)}) collective-permute-start(bf16[1,2,4,128,128]{4,3,2,1,0:T(8,128)(2,1)} %get-tuple-element.33), channel_id=1, source_target_pairs={{24,0},{28,4},{0,8},{4,12},{8,16},{12,20},{16,24},{20,28},{25,1},{... | collective-permute-start | bytes 786440 | tf_op jit(solution)/shard_map/ppermute | solution.py:51

commit v2 on v1

--- a/solution.py
+++ b/solution.py
@@ -6,7 +6,9 @@
 from jax import lax
 from jax.experimental import pallas as pl
 from jax.experimental.pallas import tpu as pltpu
+
 from jax.sharding import PartitionSpec as P
+
 
 HEAD = 128
 BLOCK = 128
@@ -51,7 +53,7 @@
     return lax.ppermute(value, "ctx", [(b, a) for a, b in pairs])
 
 
-def slots(r, n, half):
+def slots(r, n):
     def pick(default, *cases):
         out = default
         for cond, value in reversed(cases):
@@ -66,14 +68,13 @@
     p1 = pick(
         jnp.where(even, SWAP, column), (r == 0, SWAP), (r == 1, LOW), (r == 2, L1), (r == 3, L2)
     )
-    low = [LOW, L1, L2, L3]
     high = [
         HIGH,
         pick(U1, (r == n - 1, LOW)),
         pick(U2, (r == n - 2, EXTRA), (r == n - 1, L1)),
         pick(U3, (r == n - 2, LOW), (r == n - 1, L2)),
     ]
-    return [p0, p1] + [jnp.where(half == 0, a, b) for a, b in zip(low, high)]
+    return [p0, p1, LOW, L1, L2, L3], [p0, p1] + high
 
 
 def attend_kernel(
@@ -82,110 +83,161 @@
     bufs = refs[:nbuf]
     dq_ref, dbias_ref, own_ref = refs[nbuf : nbuf + 3]
     outs = refs[nbuf + 3 : nbuf + 3 + nbuf - 2]
-    kv, acc, probs_buf, ds_buf = refs[nbuf + 3 + nbuf - 2 :]
-    t, k, half = pl.program_id(0), pl.program_id(1), pl.program_id(2)
+    kv, acc, probs_buf, ds_buf, q_buf, g_buf, s_buf, dp_buf = refs[nbuf + 3 + nbuf - 2 :]
+    t, k = pl.program_id(0), pl.program_id(1)
     r = rank_ref[0]
     scale = HEAD ** (-0.5)
     factor = scale * math.log2(math.e)
-    block = jnp.where(half == 0, r, 2 * n - 1 - r)
-    where_from = slots(r, n, half)
-    base = (t * 2 * n + block) * CAND
-    ok = []
-    for c in range(CAND):
-        listed = blocks_ref[base + c] >= 0
-        if c < PROMPT:
-            listed = listed & (c < block - WINDOW)
-        ok.append(listed)
-
-    @pl.when((k == 0) & (half == 0))
+    width = 2 * BLOCK
+    pairs = group // 2
+    nt = (((1,), (1,)), ((), ()))
+    part = [slice(c * BLOCK, (c + 1) * BLOCK) for c in range(CAND)]
+    places = slots(r, n)
+
+    @pl.when(k == 0)
     def _():
         for i in range(nbuf):
             kv[i] = bufs[i][0]
 
-    @pl.when(half == 0)
-    def _():
-        acc[...] = jnp.zeros_like(acc)
-
-    keys = jnp.concatenate([kv[s, k] for s in where_from], axis=0)
-    vals = jnp.concatenate([kv[s, heads + k] for s in where_from], axis=0)
-    keys_t = keys.T
-    queries, grads = [], []
-    for g in range(group):
-        cols = slice(g * HEAD, (g + 1) * HEAD)
-        queries.append((q_ref[0, :, cols].astype(jnp.float32) + bias_ref[:, cols]).astype(jnp.bfloat16))
-        grads.append(g_ref[0, :, cols])
-    nt = (((1,), (1,)), ((), ()))
-    width = 2 * BLOCK
+    acc[...] = jnp.zeros_like(acc)
     key_pos = lax.broadcasted_iota(jnp.int32, (BLOCK, width), 0)
     query_pos = lax.broadcasted_iota(jnp.int32, (BLOCK, width), 1) % BLOCK
     causal = key_pos <= query_pos
-    live = block * BLOCK + query_pos[:1] < len_ref[t]
-    for pair in range(group // 2):
-        q_two = jnp.concatenate(queries[2 * pair : 2 * pair + 2], axis=0)
-        g_two = jnp.concatenate(grads[2 * pair : 2 * pair + 2], axis=0)
-        scores = lax.dot_general(keys, q_two, nt, preferred_element_type=jnp.float32)
-        parts = []
-        for c in range(CAND):
-            part = scores[c * BLOCK : (c + 1) * BLOCK]
+
+    def fold(op, x):
+        return op(x.reshape(BLOCK // 8, 8, width), axis=0)
+
+    keys, keys_t, vals, oks, lives = [], [], [], [], []
+    for half in range(2):
+        block = 2 * n - 1 - r if half else r
+        base = (t * 2 * n + block) * CAND
+        ok = []
+        for c in range(CAND):
+            listed = blocks_ref[base + c] >= 0
+            if c < PROMPT:
+                listed = listed & (c < block - WINDOW)
+            ok.append(listed)
+        oks.append(ok)
+        lives.append(block * BLOCK + query_pos[:1] < len_ref[t])
+        keys.append(jnp.concatenate([kv[s, k] for s in places[half]], axis=0))
+        vals.append(jnp.concatenate([kv[s, heads + k] for s in places[half]], axis=0))
+        keys_t.append(keys[half].T)
+
+    def load(task):
+        half, pair = divmod(task, pairs)
+        for g in range(2 * pair, 2 * pair + 2):
+            cols = slice(g * HEAD, (g + 1) * HEAD)
+            rows = slice(g * BLOCK, (g + 1) * BLOCK)
+            here = slice(half * BLOCK, (half + 1) * BLOCK)
+            query = q_ref[0, here, cols].astype(jnp.float32) + bias_ref[:, cols]
+            q_buf[half, rows] = query.astype(jnp.bfloat16)
+            g_buf[half, rows] = g_ref[0, here, cols]
+
+    def products(task):
+        half, pair = divmod(task, pairs)
+        rows = slice(pair * width, (pair + 1) * width)
+        s_buf[task % 2] = lax.dot_general(
+            keys[half], q_buf[half, rows], nt, preferred_element_type=jnp.float32
+        )
+        dp_buf[task % 2] = lax.dot_general(
+            vals[half], g_buf[half, rows], nt, preferred_element_type=jnp.float32
+        )
+
+    def softmax(task):
+        half, pair = divmod(task, pairs)
+        span = slice(pair * width, (pair + 1) * width)
+        slot = task % 2
+        ok = oks[half]
+        top = None
+        for c in range(CAND):
+            x = s_buf[slot, part[c]]
             if c == PROMPT:
-                parts.append(jnp.where(causal, part, -1e30))
+                x = jnp.where(causal, x, -1e30)
+            x = fold(jnp.max, x)
+            if c != PROMPT:
+                x = jnp.where(ok[c], x, -1e30)
+            top = x if top is None else jnp.maximum(top, x)
+        top = jnp.max(top, axis=0, keepdims=True) * factor
+        total = jnp.zeros((8, width), jnp.float32)
+        for c in range(CAND):
+            x = s_buf[slot, part[c]]
+            if c == PROMPT:
+                e = jnp.exp2(jnp.where(causal, x, -1e30) * factor - top)
             else:
-                parts.append(jnp.where(ok[c], part, -1e30))
-        scores = jnp.concatenate(parts, axis=0)
-        top = jnp.max(scores, axis=0, keepdims=True)
-        probs = jnp.exp2((scores - top) * factor)
-        total = jnp.sum(probs, axis=0, keepdims=True)
-        probs = probs * jnp.where(live, 1.0 / total, 0.0)
-        probs_low = probs.astype(jnp.bfloat16)
-        grad_probs = lax.dot_general(vals, g_two, nt, preferred_element_type=jnp.float32)
-        row_dot = jnp.sum(probs_low.astype(jnp.float32) * grad_probs, axis=0, keepdims=True)
-        grad_scores = (probs * (grad_probs - row_dot)).astype(jnp.bfloat16)
+                e = jnp.exp2(x * factor - jnp.where(ok[c], top, 1e30))
+            s_buf[slot, part[c]] = e
+            total = total + fold(jnp.sum, e)
+        total = jnp.sum(total, axis=0, keepdims=True)
+        inverse = jnp.where(lives[half], 1.0 / total, 0.0)
+        row_dot = jnp.zeros((8, width), jnp.float32)
+        for c in range(CAND):
+            low = (s_buf[slot, part[c]] * inverse).astype(jnp.bfloat16)
+            probs_buf[half, part[c], span] = low
+            row_dot = row_dot + fold(jnp.sum, low.astype(jnp.float32) * dp_buf[slot, part[c]])
+        row_dot = jnp.sum(row_dot, axis=0, keepdims=True)
+        for c in range(CAND):
+            probs = s_buf[slot, part[c]] * inverse
+            ds_buf[half, part[c], span] = (probs * (dp_buf[slot, part[c]] - row_dot)).astype(
+                jnp.bfloat16
+            )
+
+    def query_grad(task):
+        half, pair = divmod(task, pairs)
         span = slice(pair * width, (pair + 1) * width)
-        probs_buf[:, span] = probs_low
-        ds_buf[:, span] = grad_scores
-        dq = scale * jnp.dot(keys_t, grad_scores, preferred_element_type=jnp.float32)
+        here = slice(half * BLOCK, (half + 1) * BLOCK)
+        dq = scale * jnp.dot(
+            keys_t[half], ds_buf[half, :, span], preferred_element_type=jnp.float32
+        )
         for i in range(2):
             cols = slice((2 * pair + i) * HEAD, (2 * pair + i + 1) * HEAD)
             dq_head = dq[:, i * BLOCK : (i + 1) * BLOCK].T
-            dq_ref[0, :, cols] = dq_head.astype(jnp.bfloat16)
+            dq_ref[0, here, cols] = dq_head.astype(jnp.bfloat16)
             row = jnp.sum(dq_head, axis=0, keepdims=True)
-
-            @pl.when((half == 0) & (t == 0))
-            def _():
-                dbias_ref[:, cols] = row
-
-            @pl.when((half != 0) | (t != 0))
-            def _():
+            if half == 0:
+                dbias_ref[:, cols] = jnp.where(t == 0, 0.0, dbias_ref[:, cols]) + row
+            else:
                 dbias_ref[:, cols] += row
 
-    q_all = jnp.concatenate(queries, axis=0)
-    g_all = jnp.concatenate(grads, axis=0)
-    dk = scale * jnp.dot(ds_buf[...], q_all, preferred_element_type=jnp.float32)
-    dv = jnp.dot(probs_buf[...], g_all, preferred_element_type=jnp.float32)
-    for c in range(CAND):
-        rows = slice(c * BLOCK, (c + 1) * BLOCK)
-        acc[where_from[c], 0] += dk[rows]
-        acc[where_from[c], 1] += dv[rows]
-
-    @pl.when(half == 1)
-    def _():
-        for i in range(2):
-            own_ref[0, i, :, 0] = acc[i]
-        for i, out in enumerate(outs):
-            out[0, :, 0] = acc[i + 2].astype(out.dtype)
+    def key_grad(task, count):
+        half, pair = divmod(task, pairs)
+        span = slice((pair - count + 1) * width, (pair + 1) * width)
+        dk = scale * jnp.dot(
+            ds_buf[half, :, span], q_buf[half, span], preferred_element_type=jnp.float32
+        )
+        dv = jnp.dot(
+            probs_buf[half, :, span], g_buf[half, span], preferred_element_type=jnp.float32
+        )
+        for c in range(CAND):
+            acc[places[half][c], 0] += dk[part[c]]
+            acc[places[half][c], 1] += dv[part[c]]
+
+    tasks = 2 * pairs
+    load(0)
+    products(0)
+    for task in range(tasks):
+        if task + 1 < tasks:
+            load(task + 1)
+            products(task + 1)
+        softmax(task)
+        query_grad(task)
+        if task % pairs == pairs - 1:
+            key_grad(task, pairs)
+
+    for i in range(2):
+        own_ref[0, i, :, 0] = acc[i]
+    for i, out in enumerate(outs):
+        out[0, :, 0] = acc[i + 2].astype(out.dtype)
 
 
 def attend(n, heads, group, rank, blocks, lens, query_in, grad_out, bias, bufs):
     traces = query_in.shape[0]
     nbuf = len(bufs)
     width = group * HEAD
-    row_spec = pl.BlockSpec((1, BLOCK, width), lambda t, k, j, *_: (t, j, k))
-    bias_spec = pl.BlockSpec((1, width), lambda t, k, j, *_: (0, k))
-    buf_spec = pl.BlockSpec((1, 2 * heads, BLOCK, HEAD), lambda t, k, j, *_: (t, 0, 0, 0))
-    own_spec = pl.BlockSpec(
-        (1, 2, 2, 1, BLOCK, HEAD), lambda t, k, j, *_: (t, 0, 0, k, 0, 0)
-    )
-    out_spec = pl.BlockSpec((1, 2, 1, BLOCK, HEAD), lambda t, k, j, *_: (t, 0, k, 0, 0))
+    row_spec = pl.BlockSpec((1, 2 * BLOCK, width), lambda t, k, *_: (t, 0, k))
+    bias_spec = pl.BlockSpec((1, width), lambda t, k, *_: (0, k))
+    buf_spec = pl.BlockSpec((1, 2 * heads, BLOCK, HEAD), lambda t, k, *_: (t, 0, 0, 0))
+    own_spec = pl.BlockSpec((1, 2, 2, 1, BLOCK, HEAD), lambda t, k, *_: (t, 0, 0, k, 0, 0))
+    out_spec = pl.BlockSpec((1, 2, 1, BLOCK, HEAD), lambda t, k, *_: (t, 0, k, 0, 0))
     out_shape = [
         jax.ShapeDtypeStruct(query_in.shape, jnp.bfloat16),
         jax.ShapeDtypeStruct((1, heads * width), jnp.float32),
@@ -196,18 +248,22 @@
         out_shape=out_shape,
         grid_spec=pltpu.PrefetchScalarGridSpec(
             num_scalar_prefetch=3,
-            grid=(traces, heads, 2),
+            grid=(traces, heads),
             in_specs=[row_spec, row_spec, bias_spec] + [buf_spec] * nbuf,
             out_specs=[row_spec, bias_spec, own_spec] + [out_spec] * (nbuf - 2),
             scratch_shapes=[
                 pltpu.VMEM((nbuf, 2 * heads, BLOCK, HEAD), jnp.bfloat16),
                 pltpu.VMEM((nbuf, 2, BLOCK, HEAD), jnp.float32),
-                pltpu.VMEM((CAND * BLOCK, width), jnp.bfloat16),
-                pltpu.VMEM((CAND * BLOCK, width), jnp.bfloat16),
+                pltpu.VMEM((2, CAND * BLOCK, width), jnp.bfloat16),
+                pltpu.VMEM((2, CAND * BLOCK, width), jnp.bfloat16),
+                pltpu.VMEM((2, width, HEAD), jnp.bfloat16),
+                pltpu.VMEM((2, width, HEAD), jnp.bfloat16),
+                pltpu.VMEM((2, CAND * BLOCK, 2 * BLOCK), jnp.float32),
+                pltpu.VMEM((2, CAND * BLOCK, 2 * BLOCK), jnp.float32),
             ],
         ),
         compiler_params=pltpu.CompilerParams(
-            dimension_semantics=("arbitrary", "arbitrary", "arbitrary"),
+            dimension_semantics=("arbitrary", "arbitrary"),
             vmem_limit_bytes=56 * 1024 * 1024,
         ),
         name="attend",
@@ -218,7 +274,8 @@
     count = lax.axis_size(axis)
     stride = 1
     while stride < count:
-        value = value + lax.ppermute(value, axis, [(s, s ^ stride) for s in range(count)])
+        got = lax.ppermute(value, axis, [(s, s ^ stride) for s in range(count)])
+        value = value + got
         stride *= 2
     return value
 
@@ -309,10 +366,12 @@
         low_grad = low_grad + low_extra
     high_grad = own[:, 1] + back_u1.astype(f32) + gate(r >= 2, back_u2)
     both = jnp.stack([low_grad, high_grad], axis=1).astype(bf16)
-    both = both.transpose(2, 0, 1, 4, 3, 5).reshape(2, traces, 2 * BLOCK, width_kv)
+    both = both.transpose(0, 1, 2, 4, 3, 5)
+    grad_key = both[:, :, 0].reshape(traces, 2 * BLOCK, width_kv)
+    grad_value = both[:, :, 1].reshape(traces, 2 * BLOCK, width_kv)
     bias_total = butterfly(butterfly(dbias.reshape(-1), "dp"), "ctx")
     rows = traces * lax.axis_size("dp") * 2 * BLOCK * n
-    return dq, both[0], both[1], bias_total / math.sqrt(rows)
+    return dq, grad_key, grad_value, bias_total / math.sqrt(rows)
 
 
 def solution(mesh):

time: 143 us -> 119 us (0.83)
  Pallas kernels: 53.5 us -> 29.7 us
    pallas_call x1, Pallas kernels: 53.5 us -> 29.7 us  [attend(): pl.pallas_call(functools.partial(attend_kernel, n, nbuf, heads, group), o...]
    squeeze x2 -> x0, local copies, waits for them, and re-layouts: 1.61 us -> none  [body(): return (dq, both[0], both[1], bias_total / math.sqrt(rows))]
    another operation x0 -> x2, local copies, waits for them, and re-layouts: none -> 1.61 us  [the longest x1 0.8 us: body(): grad_value = both[:, :, 1].reshape(traces, 2 * BLOCK, width_kv)]
  transfers between devices with their start and end apart: 21 -> 21, of which waited for: 8 -> 8; matrix products, arithmetic and copies ran while one was open for 4% -> 5% of each run, Pallas kernels for 0% -> 0%
where the time goes in v2:
time: 119 us; the launch traced here: 118 us
  starting transfers between devices  53 us (45%)
  Pallas kernels  29.7 us (25%)
  waiting for transfers between devices  23.1 us (19%)
  other arithmetic  7.04 us (6%)
  local copies, waits for them, and re-layouts  3.71 us (3%)
  between operations  1.7 us (1%)
    pallas_call x1, Pallas kernels, attend(): pl.pallas_call(functools.partial(attend_kernel, n, nbuf, heads, group), o...  29.7 us
    ppermute x8, starting transfers between devices, send(): return lax.ppermute(value, 'ctx', pairs)  24.5 us
    ppermute x8, starting transfers between devices, send_back(): return lax.ppermute(value, 'ctx', [(b, a) for a, b in pairs])  18 us
    ppermute x8, waiting for transfers between devices, send_back(): return lax.ppermute(value, 'ctx', [(b, a) for a, b in pairs])  12 us
    ppermute x5, starting transfers between devices, butterfly(): got = lax.ppermute(value, axis, [(s, s ^ stride) for s in range(count)])  10.5 us
    ppermute x8, waiting for transfers between devices, send(): return lax.ppermute(value, 'ctx', pairs)  6.08 us
    ppermute x5, waiting for transfers between devices, butterfly(): got = lax.ppermute(value, axis, [(s, s ^ stride) for s in range(count)])  5.03 us
  transfers between devices with their start and end apart: 21, of which 8 were waited for; matrix products, arithmetic and copies ran while one was open for 5% of the time, Pallas kernels for 0%

profile of v2, /device:TPU:0, one launch (start us, length us, event | category | flops | bytes accessed | tf_op | source)
XLA Modules:
  0.0 118.3 jit_solution(6191165826129821693)
XLA Ops:
  0.6 1.1 maximum_bitcast_fusion
  1.7 0.1 copy.19
  1.9 0.1 broadcast_select_fusion.1
  2.0 5.1 %collective-permute-start.3 = (bf16[1,8,128,128]{3,2,1,0:T(8,128)(2,1)S(1)}, bf16[1,8,128,128]{3,2,1,0:T(8,128)(2,1)S(1)}, u32[]{:S(2)}, u32[]{:S(2)}) collective-permute-start(bf16[1,8,128,128]{3,2,1,0:T(8,128)(2,1)S(1)} %broadcast_select_fusion.1), channel_id=1, source_target_pairs={{0,24},{4,28},{8,0},{12,4},{16,8},{20,12},{24,16},{28,20},{1,25},{... | collective-permute-start | bytes 786440 | tf_op jit(solution)/shard_map/ppermute | solution.py:49
  7.1 1.4 %collective-permute-start.4 = (bf16[1,8,128,128]{3,2,1,0:T(8,128)(2,1)S(1)}, bf16[1,8,128,128]{3,2,1,0:T(8,128)(2,1)S(1)}, u32[]{:S(2)}, u32[]{:S(2)}) collective-permute-start(bf16[1,8,128,128]{3,2,1,0:T(8,128)(2,1)S(1)} %bitcast.53), channel_id=1, source_target_pairs={{0,16},{4,20},{28,24},{1,17},{5,21},{29,25},{2,18},{6,22},{30,26},... | collective-permute-start | bytes 786440 | tf_op jit(solution)/shard_map/ppermute | solution.py:49
  8.6 1.3 %collective-permute-start.1 = (bf16[1,8,128,128]{3,2,1,0:T(8,128)(2,1)S(1)}, bf16[1,8,128,128]{3,2,1,0:T(8,128)(2,1)S(1)}, u32[]{:S(2)}, u32[]{:S(2)}) collective-permute-start(bf16[1,8,128,128]{3,2,1,0:T(8,128)(2,1)S(1)} %bitcast.57), channel_id=1, source_target_pairs={{4,0},{8,4},{12,8},{16,12},{20,16},{24,20},{28,24},{5,1},{9,5},{13... | collective-permute-start | bytes 786440 | tf_op jit(solution)/shard_map/ppermute | solution.py:49
  9.9 4.6 %collective-permute-start = (bf16[1,8,128,128]{3,2,1,0:T(8,128)(2,1)S(1)}, bf16[1,8,128,128]{3,2,1,0:T(8,128)(2,1)S(1)}, u32[]{:S(2)}, u32[]{:S(2)}) collective-permute-start(bf16[1,8,128,128]{3,2,1,0:T(8,128)(2,1)S(1)} %bitcast.54), channel_id=1, source_target_pairs={{0,4},{4,8},{8,12},{12,16},{16,20},{20,24},{24,28},{1,5},{5,9},{9,... | collective-permute-start | bytes 786440 | tf_op jit(solution)/shard_map/ppermute | solution.py:49
  14.4 2.8 %collective-permute-start.2 = (bf16[1,8,128,128]{3,2,1,0:T(8,128)(2,1)S(1)}, bf16[1,8,128,128]{3,2,1,0:T(8,128)(2,1)S(1)}, u32[]{:S(2)}, u32[]{:S(2)}) collective-permute-start(bf16[1,8,128,128]{3,2,1,0:T(8,128)(2,1)S(1)} %bitcast.55), channel_id=1, source_target_pairs={{0,8},{4,12},{8,16},{12,20},{16,24},{20,28},{1,9},{5,13},{9,17},{1... | collective-permute-start | bytes 786440 | tf_op jit(solution)/shard_map/ppermute | solution.py:49
  17.3 2.1 %collective-permute-done.4.refs_6_ = bf16[1,8,128,128]{3,2,1,0:T(8,128)(2,1)S(1)} collective-permute-done((bf16[1,8,128,128]{3,2,1,0:T(8,128)(2,1)S(1)}, bf16[1,8,128,128]{3,2,1,0:T(8,128)(2,1)S(1)}, u32[]{:S(2)}, u32[]{:S(2)}) %collective-permute-start.4) | collective-permute-done | bytes 262176 | tf_op jit(solution)/shard_map/ppermute | solution.py:49
  19.4 0.1 select_select_fusion
  19.5 1.3 %collective-permute-start.6 = (bf16[1,8,128,128]{3,2,1,0:T(8,128)(2,1)S(1)}, bf16[1,8,128,128]{3,2,1,0:T(8,128)(2,1)S(1)}, u32[]{:S(2)}, u32[]{:S(2)}) collective-permute-start(bf16[1,8,128,128]{3,2,1,0:T(8,128)(2,1)S(1)} %get-tuple-element.35), channel_id=1, source_target_pairs={{8,0},{12,4},{16,8},{20,12},{24,16},{28,20},{9,1},{13,5},{17,9},{2... | collective-permute-start | bytes 786440 | tf_op jit(solution)/shard_map/ppermute | solution.py:49
  20.8 1.3 %collective-permute-start.7 = (bf16[1,8,128,128]{3,2,1,0:T(8,128)(2,1)S(1)}, bf16[1,8,128,128]{3,2,1,0:T(8,128)(2,1)S(1)}, u32[]{:S(2)}, u32[]{:S(2)}) collective-permute-start(bf16[1,8,128,128]{3,2,1,0:T(8,128)(2,1)S(1)} %get-tuple-element.34), channel_id=1, source_target_pairs={{4,0},{16,20},{20,16},{24,28},{28,24},{5,1},{17,21},{21,17},{25,29... | collective-permute-start | bytes 786440 | tf_op jit(solution)/shard_map/ppermute | solution.py:49
  22.1 1.6 %collective-permute-done.refs_2_ = bf16[1,8,128,128]{3,2,1,0:T(8,128)(2,1)S(1)} collective-permute-done((bf16[1,8,128,128]{3,2,1,0:T(8,128)(2,1)S(1)}, bf16[1,8,128,128]{3,2,1,0:T(8,128)(2,1)S(1)}, u32[]{:S(2)}, u32[]{:S(2)}) %collective-permute-start) | collective-permute-done | bytes 262176 | tf_op jit(solution)/shard_map/ppermute | solution.py:49
  23.7 6.7 %collective-permute-start.5 = (bf16[1,8,128,128]{3,2,1,0:T(8,128)(2,1)S(1)}, bf16[1,8,128,128]{3,2,1,0:T(8,128)(2,1)S(1)}, u32[]{:S(2)}, u32[]{:S(2)}) collective-permute-start(bf16[1,8,128,128]{3,2,1,0:T(8,128)(2,1)S(1)} %collective-permute-done.refs_2_), channel_id=1, source_target_pairs={{0,8},{4,12},{8,16},{12,20},{16,24},{20,28},{1,9},{5,13},{9,17},{1... | collective-permute-start | bytes 786440 | tf_op jit(solution)/shard_map/ppermute | solution.py:49
  30.4 0.1 copy.12
  30.5 0.7 reshape.62.blocks_ref
  31.9 2.4 %collective-permute-done.5.refs_7_ = bf16[1,8,128,128]{3,2,1,0:T(8,128)(2,1)S(1)} collective-permute-done((bf16[1,8,128,128]{3,2,1,0:T(8,128)(2,1)S(1)}, bf16[1,8,128,128]{3,2,1,0:T(8,128)(2,1)S(1)}, u32[]{:S(2)}, u32[]{:S(2)}) %collective-permute-start.5) | collective-permute-done | bytes 262176 | tf_op jit(solution)/shard_map/ppermute | solution.py:49
  34.3 0.6 copy-done.10
  34.9 29.7 %attend.1 = (bf16[1,256,4096]{2,1,0:T(8,128)(2,1)}, f32[1,4096]{1,0:T(1,128)}, f32[1,2,2,4,128,128]{5,4,3,2,1,0:T(8,128)}, bf16[1,2,4,128,128]{4,3,2,1,0:T(8,128...) custom-call(s32[1]{0:T(128)} %bitcast.rank_ref, ...), custom_call_target="tpu_custom_call" | custom-call | tf_op jit(solution)/shard_map/attend/pallas_call | solution.py:246
  64.7 4.4 %collective-permute-start.14 = (bf16[1,2,4,128,128]{4,3,2,1,0:T(8,128)(2,1)}, bf16[1,2,4,128,128]{4,3,2,1,0:T(8,128)(2,1)S(1)}, u32[]{:S(2)}, u32[]{:S(2)}) collective-permute-start(bf16[1,2,4,128,128]{4,3,2,1,0:T(8,128)(2,1)} %get-tuple-element.23), channel_id=1, source_target_pairs={{0,8},{4,12},{8,16},{12,20},{16,24},{20,28},{1,9},{5,13},{9,17},{1... | collective-permute-start | bytes 786440 | tf_op jit(solution)/shard_map/ppermute | solution.py:53
  69.1 0.1 collective-permute-start.16
  69.2 1.4 %collective-permute-done.16 = f32[4096]{0:T(1024)S(1)} collective-permute-done((f32[4096]{0:T(1024)}, f32[4096]{0:T(1024)S(1)}, u32[]{:S(2)}, u32[]{:S(2)}) %collective-permute-start.16) | collective-permute-done | bytes 16416 | tf_op jit(solution)/shard_map/ppermute | solution.py:277
  70.6 0.7 add.63
  71.3 1.5 %collective-permute-start.17 = (f32[4096]{0:T(1024)S(1)}, f32[4096]{0:T(1024)S(1)}, u32[]{:S(2)}, u32[]{:S(2)}) collective-permute-start(f32[4096]{0:T(1024)S(1)} %add.63), channel_id=1, source_target_pairs={{0,2},{1,3},{2,0},{3,1},{4,6},{5,7},{6,4},{7,5},{8,10},{9,11},{10,... | collective-permute-start | bytes 49160 | tf_op jit(solution)/shard_map/ppermute | solution.py:277
  72.8 2.2 %collective-permute-done.17 = f32[4096]{0:T(1024)S(1)} collective-permute-done((f32[4096]{0:T(1024)S(1)}, f32[4096]{0:T(1024)S(1)}, u32[]{:S(2)}, u32[]{:S(2)}) %collective-permute-start.17) | collective-permute-done | bytes 16416 | tf_op jit(solution)/shard_map/ppermute | solution.py:277
  75.0 2.5 %collective-permute-start.18 = (f32[4096]{0:T(1024)S(1)}, f32[4096]{0:T(1024)S(1)}, u32[]{:S(2)}, u32[]{:S(2)}) collective-permute-start(f32[4096]{0:T(1024)S(1)} %add.64), channel_id=1, source_target_pairs={{0,4},{4,0},{8,12},{12,8},{16,20},{20,16},{24,28},{28,24},{1,5},{5... | collective-permute-start | bytes 49160 | tf_op jit(solution)/shard_map/ppermute | solution.py:277
  77.5 1.3 %collective-permute-start.8 = (bf16[1,2,4,128,128]{4,3,2,1,0:T(8,128)(2,1)}, bf16[1,2,4,128,128]{4,3,2,1,0:T(8,128)(2,1)S(1)}, u32[]{:S(2)}, u32[]{:S(2)}) collective-permute-start(bf16[1,2,4,128,128]{4,3,2,1,0:T(8,128)(2,1)} %get-tuple-element.18), channel_id=1, source_target_pairs={{8,0},{12,4},{16,8},{20,12},{24,16},{28,20},{9,1},{13,5},{17,9},{2... | collective-permute-start | bytes 786440 | tf_op jit(solution)/shard_map/ppermute | solution.py:53
  78.8 0.4 collective-permute-done.18
  79.2 2.3 %collective-permute-start.19 = (f32[4096]{0:T(1024)S(1)}, f32[4096]{0:T(1024)S(1)}, u32[]{:S(2)}, u32[]{:S(2)}) collective-permute-start(f32[4096]{0:T(1024)S(1)} %add.65), channel_id=1, source_target_pairs={{0,8},{4,12},{8,0},{12,4},{16,24},{20,28},{24,16},{28,20},{1,9},{5... | collective-permute-start | bytes 49160 | tf_op jit(solution)/shard_map/ppermute | solution.py:277
  81.5 3.4 %collective-permute-start.11 = (bf16[1,2,4,128,128]{4,3,2,1,0:T(8,128)(2,1)}, bf16[1,2,4,128,128]{4,3,2,1,0:T(8,128)(2,1)S(1)}, u32[]{:S(2)}, u32[]{:S(2)}) collective-permute-start(bf16[1,2,4,128,128]{4,3,2,1,0:T(8,128)(2,1)} %get-tuple-element.21), channel_id=1, source_target_pairs={{0,4},{20,16},{16,20},{28,24},{24,28},{1,5},{21,17},{17,21},{29,25... | collective-permute-start | bytes 786440 | tf_op jit(solution)/shard_map/ppermute | solution.py:53
  84.9 1.3 %collective-permute-start.10 = (bf16[1,2,4,128,128]{4,3,2,1,0:T(8,128)(2,1)}, bf16[1,2,4,128,128]{4,3,2,1,0:T(8,128)(2,1)S(1)}, u32[]{:S(2)}, u32[]{:S(2)}) collective-permute-start(bf16[1,2,4,128,128]{4,3,2,1,0:T(8,128)(2,1)} %get-tuple-element.19), channel_id=1, source_target_pairs={{8,0},{12,4},{16,8},{20,12},{24,16},{28,20},{9,1},{13,5},{17,9},{2... | collective-permute-start | bytes 786440 | tf_op jit(solution)/shard_map/ppermute | solution.py:53
  86.2 1.0 collective-permute-done.19
  87.2 4.2 %collective-permute-start.20 = (f32[4096]{0:T(1024)S(1)}, f32[4096]{0:T(1024)S(1)}, u32[]{:S(2)}, u32[]{:S(2)}) collective-permute-start(f32[4096]{0:T(1024)S(1)} %add.66), channel_id=1, source_target_pairs={{0,16},{4,20},{8,24},{12,28},{16,0},{20,4},{24,8},{28,12},{1,17},{... | collective-permute-start | bytes 49160 | tf_op jit(solution)/shard_map/ppermute | solution.py:277
  91.4 1.0 fusion.7
  92.5 1.7 %collective-permute-start.15 = (bf16[1,2,4,128,128]{4,3,2,1,0:T(8,128)(2,1)S(1)}, bf16[1,2,4,128,128]{4,3,2,1,0:T(8,128)(2,1)S(1)}, u32[]{:S(2)}, u32[]{:S(2)}) collective-permute-start(bf16[1,2,4,128,128]{4,3,2,1,0:T(8,128)(2,1)S(1)} %fusion.7), channel_id=1, source_target_pairs={{0,4},{4,8},{8,12},{12,16},{16,20},{20,24},{24,28},{1,5},{5,9},{9,... | collective-permute-start | bytes 786440 | tf_op jit(solution)/shard_map/ppermute | solution.py:53
  94.2 1.0 add_convert_fusion
  95.2 1.3 %collective-permute-start.9 = (bf16[1,2,4,128,128]{4,3,2,1,0:T(8,128)(2,1)S(1)}, bf16[1,2,4,128,128]{4,3,2,1,0:T(8,128)(2,1)S(1)}, u32[]{:S(2)}, u32[]{:S(2)}) collective-permute-start(bf16[1,2,4,128,128]{4,3,2,1,0:T(8,128)(2,1)S(1)} %add_convert_fusion), channel_id=1, source_target_pairs={{4,0},{8,4},{12,8},{16,12},{20,16},{24,20},{28,24},{5,1},{9,5},{13... | collective-permute-start | bytes 786440 | tf_op jit(solution)/shard_map/ppermute | solution.py:53
  96.5 2.0 %fusion.9 = (bf16[1,2,4,128,128]{4,3,2,1,0:T(8,128)(2,1)}, bf16[1,2,4,128,128]{4,3,2,1,0:T(8,128)(2,1)}) fusion(bf16[1,2,4,128,128]{4,3,2,1,0:T(8,128)(2,1)S(1)} %collective-permute-done.11, bf16[1,2,4,128,128]{4,3,2,1,0:T(8,128)(2,1)} %get-tuple-element.20, pred[]{:T(512)S(6)} %and.4, pred[]{:T(512)S(6)} %ge.10, ...), kind=kLoop, calls=%fused_computation.16 | loop fusion | flops 1179648 | bytes 1310722 | tf_op jit(solution)/shard_map/convert_element_type | solution.py:358
  98.5 1.3 %collective-permute-start.12 = (bf16[1,2,4,128,128]{4,3,2,1,0:T(8,128)(2,1)}, bf16[1,2,4,128,128]{4,3,2,1,0:T(8,128)(2,1)S(1)}, u32[]{:S(2)}, u32[]{:S(2)}) collective-permute-start(bf16[1,2,4,128,128]{4,3,2,1,0:T(8,128)(2,1)} %get-tuple-element.32), channel_id=1, source_target_pairs={{16,0},{20,4},{24,28},{17,1},{21,5},{25,29},{18,2},{22,6},{26,30},... | collective-permute-start | bytes 786440 | tf_op jit(solution)/shard_map/ppermute | solution.py:53
  99.8 3.4 %collective-permute-start.13 = (bf16[1,2,4,128,128]{4,3,2,1,0:T(8,128)(2,1)}, bf16[1,2,4,128,128]{4,3,2,1,0:T(8,128)(2,1)S(1)}, u32[]{:S(2)}, u32[]{:S(2)}) collective-permute-start(bf16[1,2,4,128,128]{4,3,2,1,0:T(8,128)(2,1)} %get-tuple-element.33), channel_id=1, source_target_pairs={{24,0},{28,4},{0,8},{4,12},{8,16},{12,20},{16,24},{20,28},{25,1},{... | collective-permute-start | bytes 786440 | tf_op jit(solution)/shard_map/ppermute | solution.py:53
  103.2 0.6 add_multiply_fusion
  103.8 11.9 %collective-permute-done.12 = bf16[1,2,4,128,128]{4,3,2,1,0:T(8,128)(2,1)S(1)} collective-permute-done((bf16[1,2,4,128,128]{4,3,2,1,0:T(8,128)(2,1)}, bf16[1,2,4,128,128]{4,3,2,1,0:T(8,128)(2,1)S(1)}, u32[]{:S(2)}, u32[]{:S(2)}) %collective-permute-start.12) | collective-permute-done | bytes 262176 | tf_op jit(solution)/shard_map/ppermute | solution.py:53
  115.7 0.4 fusion.15
  116.1 0.1 maximum_bitcast_fusion.1
  116.2 0.2 copy.15
  116.5 0.8 reshape_squeeze.6
  117.3 0.2 copy.16
  117.5 0.8 reshape_squeeze.7
  (43 shorter events, 0.3 us)
Async XLA Ops:
  1.8 28.6 %copy-start.11 = (s32[1,16,6]{1,0,2:T(1,128)S(1)}, s32[1,16,6]{1,0,2:T(1,128)}, u32[]{:S(2)}) copy-start(s32[1,16,6]{1,0,2:T(1,128)} %param.12) | copy-start | bytes 1156
  2.0 15.3 %collective-permute-start.3 = (bf16[1,8,128,128]{3,2,1,0:T(8,128)(2,1)S(1)}, bf16[1,8,128,128]{3,2,1,0:T(8,128)(2,1)S(1)}, u32[]{:S(2)}, u32[]{:S(2)}) collective-permute-start(bf16[1,8,128,128]{3,2,1,0:T(8,128)(2,1)S(1)} %broadcast_select_fusion.1), channel_id=1, source_target_pairs={{0,24},{4,28},{8,0},{12,4},{16,8},{20,12},{24,16},{28,20},{1,25},{... | collective-permute-start | bytes 786440 | tf_op jit(solution)/shard_map/ppermute | solution.py:49
  7.1 27.1 %copy-start.4 = (bf16[1,1,128,8,128]{4,2,3,1,0:T(8,128)(2,1)}, bf16[1,1,128,8,128]{4,2,3,1,0:T(8,128)(2,1)S(1)}, u32[]{:S(2)}) copy-start(bf16[1,1,128,8,128]{4,2,3,1,0:T(8,128)(2,1)S(1)} %copy.31) | copy-start | bytes 786436
  7.1 12.3 %collective-permute-start.4 = (bf16[1,8,128,128]{3,2,1,0:T(8,128)(2,1)S(1)}, bf16[1,8,128,128]{3,2,1,0:T(8,128)(2,1)S(1)}, u32[]{:S(2)}, u32[]{:S(2)}) collective-permute-start(bf16[1,8,128,128]{3,2,1,0:T(8,128)(2,1)S(1)} %bitcast.53), channel_id=1, source_target_pairs={{0,16},{4,20},{28,24},{1,17},{5,21},{29,25},{2,18},{6,22},{30,26},... | collective-permute-start | bytes 786440 | tf_op jit(solution)/shard_map/ppermute | solution.py:49
  8.6 25.7 %copy-start.5 = (bf16[1,1,128,8,128]{4,2,3,1,0:T(8,128)(2,1)}, bf16[1,1,128,8,128]{4,2,3,1,0:T(8,128)(2,1)S(1)}, u32[]{:S(2)}) copy-start(bf16[1,1,128,8,128]{4,2,3,1,0:T(8,128)(2,1)S(1)} %copy.30) | copy-start | bytes 786436
  8.6 10.9 %collective-permute-start.1 = (bf16[1,8,128,128]{3,2,1,0:T(8,128)(2,1)S(1)}, bf16[1,8,128,128]{3,2,1,0:T(8,128)(2,1)S(1)}, u32[]{:S(2)}, u32[]{:S(2)}) collective-permute-start(bf16[1,8,128,128]{3,2,1,0:T(8,128)(2,1)S(1)} %bitcast.57), channel_id=1, source_target_pairs={{4,0},{8,4},{12,8},{16,12},{20,16},{24,20},{28,24},{5,1},{9,5},{13... | collective-permute-start | bytes 786440 | tf_op jit(solution)/shard_map/ppermute | solution.py:49
  9.9 13.8 %collective-permute-start = (bf16[1,8,128,128]{3,2,1,0:T(8,128)(2,1)S(1)}, bf16[1,8,128,128]{3,2,1,0:T(8,128)(2,1)S(1)}, u32[]{:S(2)}, u32[]{:S(2)}) collective-permute-start(bf16[1,8,128,128]{3,2,1,0:T(8,128)(2,1)S(1)} %bitcast.54), channel_id=1, source_target_pairs={{0,4},{4,8},{8,12},{12,16},{16,20},{20,24},{24,28},{1,5},{5,9},{9,... | collective-permute-start | bytes 786440 | tf_op jit(solution)/shard_map/ppermute | solution.py:49
  14.4 17.4 %collective-permute-start.2 = (bf16[1,8,128,128]{3,2,1,0:T(8,128)(2,1)S(1)}, bf16[1,8,128,128]{3,2,1,0:T(8,128)(2,1)S(1)}, u32[]{:S(2)}, u32[]{:S(2)}) collective-permute-start(bf16[1,8,128,128]{3,2,1,0:T(8,128)(2,1)S(1)} %bitcast.55), channel_id=1, source_target_pairs={{0,8},{4,12},{8,16},{12,20},{16,24},{20,28},{1,9},{5,13},{9,17},{1... | collective-permute-start | bytes 786440 | tf_op jit(solution)/shard_map/ppermute | solution.py:49
  17.3 17.0 %copy-start.1 = (bf16[1,8,128,128]{3,2,1,0:T(8,128)(2,1)}, bf16[1,8,128,128]{3,2,1,0:T(8,128)(2,1)S(1)}, u32[]{:S(2)}) copy-start(bf16[1,8,128,128]{3,2,1,0:T(8,128)(2,1)S(1)} %collective-permute-done.3.refs_5_) | copy-start | bytes 786436
  19.4 14.8 %copy-start.2 = (bf16[1,8,128,128]{3,2,1,0:T(8,128)(2,1)}, bf16[1,8,128,128]{3,2,1,0:T(8,128)(2,1)S(1)}, u32[]{:S(2)}) copy-start(bf16[1,8,128,128]{3,2,1,0:T(8,128)(2,1)S(1)} %collective-permute-done.4.refs_6_) | copy-start | bytes 786436
  19.4 14.8 %copy-start.3 = (bf16[1,8,128,128]{3,2,1,0:T(8,128)(2,1)}, bf16[1,8,128,128]{3,2,1,0:T(8,128)(2,1)S(1)}, u32[]{:S(2)}) copy-start(bf16[1,8,128,128]{3,2,1,0:T(8,128)(2,1)S(1)} %collective-permute-done.1.refs_3_) | copy-start | bytes 786436
  19.5 12.3 %collective-permute-start.6 = (bf16[1,8,128,128]{3,2,1,0:T(8,128)(2,1)S(1)}, bf16[1,8,128,128]{3,2,1,0:T(8,128)(2,1)S(1)}, u32[]{:S(2)}, u32[]{:S(2)}) collective-permute-start(bf16[1,8,128,128]{3,2,1,0:T(8,128)(2,1)S(1)} %get-tuple-element.35), channel_id=1, source_target_pairs={{8,0},{12,4},{16,8},{20,12},{24,16},{28,20},{9,1},{13,5},{17,9},{2... | collective-permute-start | bytes 786440 | tf_op jit(solution)/shard_map/ppermute | solution.py:49
  20.8 11.0 %collective-permute-start.7 = (bf16[1,8,128,128]{3,2,1,0:T(8,128)(2,1)S(1)}, bf16[1,8,128,128]{3,2,1,0:T(8,128)(2,1)S(1)}, u32[]{:S(2)}, u32[]{:S(2)}) collective-permute-start(bf16[1,8,128,128]{3,2,1,0:T(8,128)(2,1)S(1)} %get-tuple-element.34), channel_id=1, source_target_pairs={{4,0},{16,20},{20,16},{24,28},{28,24},{5,1},{17,21},{21,17},{25,29... | collective-permute-start | bytes 786440 | tf_op jit(solution)/shard_map/ppermute | solution.py:49
  23.7 10.6 %copy-start.6 = (bf16[1,8,128,128]{3,2,1,0:T(8,128)(2,1)}, bf16[1,8,128,128]{3,2,1,0:T(8,128)(2,1)S(1)}, u32[]{:S(2)}) copy-start(bf16[1,8,128,128]{3,2,1,0:T(8,128)(2,1)S(1)} %collective-permute-done.refs_2_) | copy-start | bytes 786436
  23.7 10.5 %collective-permute-start.5 = (bf16[1,8,128,128]{3,2,1,0:T(8,128)(2,1)S(1)}, bf16[1,8,128,128]{3,2,1,0:T(8,128)(2,1)S(1)}, u32[]{:S(2)}, u32[]{:S(2)}) collective-permute-start(bf16[1,8,128,128]{3,2,1,0:T(8,128)(2,1)S(1)} %collective-permute-done.refs_2_), channel_id=1, source_target_pairs={{0,8},{4,12},{8,16},{12,20},{16,24},{20,28},{1,9},{5,13},{9,17},{1... | collective-permute-start | bytes 786440 | tf_op jit(solution)/shard_map/ppermute | solution.py:49
  31.8 2.5 %copy-start.7 = (bf16[1,8,128,128]{3,2,1,0:T(8,128)(2,1)}, bf16[1,8,128,128]{3,2,1,0:T(8,128)(2,1)S(1)}, u32[]{:S(2)}) copy-start(bf16[1,8,128,128]{3,2,1,0:T(8,128)(2,1)S(1)} %collective-permute-done.2.refs_4_) | copy-start | bytes 786436
  31.8 2.5 %copy-start.8 = (bf16[1,8,128,128]{3,2,1,0:T(8,128)(2,1)}, bf16[1,8,128,128]{3,2,1,0:T(8,128)(2,1)S(1)}, u32[]{:S(2)}) copy-start(bf16[1,8,128,128]{3,2,1,0:T(8,128)(2,1)S(1)} %collective-permute-done.6.refs_8_) | copy-start | bytes 786436
  31.9 2.4 %copy-start.9 = (bf16[1,8,128,128]{3,2,1,0:T(8,128)(2,1)}, bf16[1,8,128,128]{3,2,1,0:T(8,128)(2,1)S(1)}, u32[]{:S(2)}) copy-start(bf16[1,8,128,128]{3,2,1,0:T(8,128)(2,1)S(1)} %collective-permute-done.7.refs_9_) | copy-start | bytes 786436
  34.2 0.7 copy-start.10
  64.7 51.1 %copy-start = (f32[1,2,2,4,128,128]{5,4,3,2,1,0:T(8,128)S(1)}, f32[1,2,2,4,128,128]{5,4,3,2,1,0:T(8,128)}, u32[]{:S(2)}) copy-start(f32[1,2,2,4,128,128]{5,4,3,2,1,0:T(8,128)} %get-tuple-element.16) | copy-start | bytes 3145732
  64.7 26.8 %collective-permute-start.14 = (bf16[1,2,4,128,128]{4,3,2,1,0:T(8,128)(2,1)}, bf16[1,2,4,128,128]{4,3,2,1,0:T(8,128)(2,1)S(1)}, u32[]{:S(2)}, u32[]{:S(2)}) collective-permute-start(bf16[1,2,4,128,128]{4,3,2,1,0:T(8,128)(2,1)} %get-tuple-element.23), channel_id=1, source_target_pairs={{0,8},{4,12},{8,16},{12,20},{16,24},{20,28},{1,9},{5,13},{9,17},{1... | collective-permute-start | bytes 786440 | tf_op jit(solution)/shard_map/ppermute | solution.py:53
  69.1 1.5 %collective-permute-start.16 = (f32[4096]{0:T(1024)}, f32[4096]{0:T(1024)S(1)}, u32[]{:S(2)}, u32[]{:S(2)}) collective-permute-start(f32[4096]{0:T(1024)} %bitcast.60), channel_id=1, source_target_pairs={{0,1},{1,0},{2,3},{3,2},{4,5},{5,4},{6,7},{7,6},{8,9},{9,8},{10,11... | collective-permute-start | bytes 49160 | tf_op jit(solution)/shard_map/ppermute | solution.py:277
  71.3 3.7 %collective-permute-start.17 = (f32[4096]{0:T(1024)S(1)}, f32[4096]{0:T(1024)S(1)}, u32[]{:S(2)}, u32[]{:S(2)}) collective-permute-start(f32[4096]{0:T(1024)S(1)} %add.63), channel_id=1, source_target_pairs={{0,2},{1,3},{2,0},{3,1},{4,6},{5,7},{6,4},{7,5},{8,10},{9,11},{10,... | collective-permute-start | bytes 49160 | tf_op jit(solution)/shard_map/ppermute | solution.py:277
  75.0 4.2 %collective-permute-start.18 = (f32[4096]{0:T(1024)S(1)}, f32[4096]{0:T(1024)S(1)}, u32[]{:S(2)}, u32[]{:S(2)}) collective-permute-start(f32[4096]{0:T(1024)S(1)} %add.64), channel_id=1, source_target_pairs={{0,4},{4,0},{8,12},{12,8},{16,20},{20,16},{24,28},{28,24},{1,5},{5... | collective-permute-start | bytes 49160 | tf_op jit(solution)/shard_map/ppermute | solution.py:277
  77.5 16.7 %collective-permute-start.8 = (bf16[1,2,4,128,128]{4,3,2,1,0:T(8,128)(2,1)}, bf16[1,2,4,128,128]{4,3,2,1,0:T(8,128)(2,1)S(1)}, u32[]{:S(2)}, u32[]{:S(2)}) collective-permute-start(bf16[1,2,4,128,128]{4,3,2,1,0:T(8,128)(2,1)} %get-tuple-element.18), channel_id=1, source_target_pairs={{8,0},{12,4},{16,8},{20,12},{24,16},{28,20},{9,1},{13,5},{17,9},{2... | collective-permute-start | bytes 786440 | tf_op jit(solution)/shard_map/ppermute | solution.py:53
  79.2 8.0 %collective-permute-start.19 = (f32[4096]{0:T(1024)S(1)}, f32[4096]{0:T(1024)S(1)}, u32[]{:S(2)}, u32[]{:S(2)}) collective-permute-start(f32[4096]{0:T(1024)S(1)} %add.65), channel_id=1, source_target_pairs={{0,8},{4,12},{8,0},{12,4},{16,24},{20,28},{24,16},{28,20},{1,9},{5... | collective-permute-start | bytes 49160 | tf_op jit(solution)/shard_map/ppermute | solution.py:277
  81.5 15.0 %collective-permute-start.11 = (bf16[1,2,4,128,128]{4,3,2,1,0:T(8,128)(2,1)}, bf16[1,2,4,128,128]{4,3,2,1,0:T(8,128)(2,1)S(1)}, u32[]{:S(2)}, u32[]{:S(2)}) collective-permute-start(bf16[1,2,4,128,128]{4,3,2,1,0:T(8,128)(2,1)} %get-tuple-element.21), channel_id=1, source_target_pairs={{0,4},{20,16},{16,20},{28,24},{24,28},{1,5},{21,17},{17,21},{29,25... | collective-permute-start | bytes 786440 | tf_op jit(solution)/shard_map/ppermute | solution.py:53
  84.9 18.8 %collective-permute-start.10 = (bf16[1,2,4,128,128]{4,3,2,1,0:T(8,128)(2,1)}, bf16[1,2,4,128,128]{4,3,2,1,0:T(8,128)(2,1)S(1)}, u32[]{:S(2)}, u32[]{:S(2)}) collective-permute-start(bf16[1,2,4,128,128]{4,3,2,1,0:T(8,128)(2,1)} %get-tuple-element.19), channel_id=1, source_target_pairs={{8,0},{12,4},{16,8},{20,12},{24,16},{28,20},{9,1},{13,5},{17,9},{2... | collective-permute-start | bytes 786440 | tf_op jit(solution)/shard_map/ppermute | solution.py:53
  87.2 12.5 %collective-permute-start.20 = (f32[4096]{0:T(1024)S(1)}, f32[4096]{0:T(1024)S(1)}, u32[]{:S(2)}, u32[]{:S(2)}) collective-permute-start(f32[4096]{0:T(1024)S(1)} %add.66), channel_id=1, source_target_pairs={{0,16},{4,20},{8,24},{12,28},{16,0},{20,4},{24,8},{28,12},{1,17},{... | collective-permute-start | bytes 49160 | tf_op jit(solution)/shard_map/ppermute | solution.py:277
  92.5 11.3 %collective-permute-start.15 = (bf16[1,2,4,128,128]{4,3,2,1,0:T(8,128)(2,1)S(1)}, bf16[1,2,4,128,128]{4,3,2,1,0:T(8,128)(2,1)S(1)}, u32[]{:S(2)}, u32[]{:S(2)}) collective-permute-start(bf16[1,2,4,128,128]{4,3,2,1,0:T(8,128)(2,1)S(1)} %fusion.7), channel_id=1, source_target_pairs={{0,4},{4,8},{8,12},{12,16},{16,20},{20,24},{24,28},{1,5},{5,9},{9,... | collective-permute-start | bytes 786440 | tf_op jit(solution)/shard_map/ppermute | solution.py:53
  95.2 8.6 %collective-permute-start.9 = (bf16[1,2,4,128,128]{4,3,2,1,0:T(8,128)(2,1)S(1)}, bf16[1,2,4,128,128]{4,3,2,1,0:T(8,128)(2,1)S(1)}, u32[]{:S(2)}, u32[]{:S(2)}) collective-permute-start(bf16[1,2,4,128,128]{4,3,2,1,0:T(8,128)(2,1)S(1)} %add_convert_fusion), channel_id=1, source_target_pairs={{4,0},{8,4},{12,8},{16,12},{20,16},{24,20},{28,24},{5,1},{9,5},{13... | collective-permute-start | bytes 786440 | tf_op jit(solution)/shard_map/ppermute | solution.py:53
  98.5 17.3 %collective-permute-start.12 = (bf16[1,2,4,128,128]{4,3,2,1,0:T(8,128)(2,1)}, bf16[1,2,4,128,128]{4,3,2,1,0:T(8,128)(2,1)S(1)}, u32[]{:S(2)}, u32[]{:S(2)}) collective-permute-start(bf16[1,2,4,128,128]{4,3,2,1,0:T(8,128)(2,1)} %get-tuple-element.32), channel_id=1, source_target_pairs={{16,0},{20,4},{24,28},{17,1},{21,5},{25,29},{18,2},{22,6},{26,30},... | collective-permute-start | bytes 786440 | tf_op jit(solution)/shard_map/ppermute | solution.py:53
  99.8 16.0 %collective-permute-start.13 = (bf16[1,2,4,128,128]{4,3,2,1,0:T(8,128)(2,1)}, bf16[1,2,4,128,128]{4,3,2,1,0:T(8,128)(2,1)S(1)}, u32[]{:S(2)}, u32[]{:S(2)}) collective-permute-start(bf16[1,2,4,128,128]{4,3,2,1,0:T(8,128)(2,1)} %get-tuple-element.33), channel_id=1, source_target_pairs={{24,0},{28,4},{0,8},{4,12},{8,16},{12,20},{16,24},{20,28},{25,1},{... | collective-permute-start | bytes 786440 | tf_op jit(solution)/shard_map/ppermute | solution.py:53

commit v3 on v2

--- a/solution.py
+++ b/solution.py
@@ -16,7 +16,7 @@
 WINDOW = 3
 CAND = PROMPT + WINDOW + 1
 
-LOW, HIGH, L1, U1, L2, U2, EXTRA, L3, U3, SWAP, RELAY = range(11)
+LOW, HIGH, A2, A3, B2, B3, C1, D1, NEAR, FAR, SWAP, RELAY = range(12)
 
 
 def relay_rounds(n):
@@ -31,18 +31,24 @@
     return rounds
 
 
+def both_ways(pairs):
+    return pairs + [(b, a) for a, b in pairs]
+
+
 def plan(n):
-    up1 = [(s, s + 1) for s in range(n - 1)]
-    down1 = [(s, s - 1) for s in range(1, n)]
-    up2 = [(s, s + 2) for s in range(n - 2)]
-    ring2 = [(s, (s - 2) % n) for s in range(n)]
-    down2 = [(s, s - 2) for s in range(2, n)]
-    extra = [(0, 4), (1, 5), (n - 1, n - 2)]
-    swap = [(1, 0)] + [(s, s ^ 1) for s in range(4, n)]
+    exchange = {
+        "a": both_ways([(s, s + 2) for s in range(n - 2) if s & 2 == 0]),
+        "b": both_ways([(s, s + 2) for s in range(n - 2) if s & 2]),
+        "c": both_ways([(s, s + 1) for s in range(0, n, 2)]),
+        "d": both_ways([(s, s + 1) for s in range(1, n - 1, 2)]),
+        "near": [(0, 4), (1, 5), (n - 1, n - 2)],
+        "far": [(0, n - 2), (1, n - 1)],
+        "swap": [(1, 0)] + [(s, s ^ 1) for s in range(4, n)],
+    }
     relay = [
         [(2 * a + x, 2 * b + x) for a, b in pairs for x in range(2)] for pairs in relay_rounds(n)
     ]
-    return up1, down1, up2, ring2, down2, extra, swap, relay
+    return exchange, relay
 
 
 def send(value, pairs):
@@ -61,20 +67,24 @@
         return out
 
     even = r % 2 == 0
-    column = pick(RELAY, (r < 6, EXTRA), (r >= n - 2, U2))
+    upper = r & 2 != 0
+    l1, u1 = jnp.where(even, D1, C1), jnp.where(even, C1, D1)
+    l2, u2 = jnp.where(upper, A2, B2), jnp.where(upper, B2, A2)
+    l3, u3 = jnp.where(upper, A3, B3), jnp.where(upper, B3, A3)
+    column = pick(RELAY, (r < 6, NEAR), (r >= n - 2, FAR))
     p0 = pick(
-        jnp.where(even, column, SWAP), (r == 0, LOW), (r == 1, L1), (r == 2, L2), (r == 3, L3)
+        jnp.where(even, column, SWAP), (r == 0, LOW), (r == 1, l1), (r == 2, l2), (r == 3, l3)
     )
     p1 = pick(
-        jnp.where(even, SWAP, column), (r == 0, SWAP), (r == 1, LOW), (r == 2, L1), (r == 3, L2)
+        jnp.where(even, SWAP, column), (r == 0, SWAP), (r == 1, LOW), (r == 2, l1), (r == 3, l2)
     )
     high = [
         HIGH,
-        pick(U1, (r == n - 1, LOW)),
-        pick(U2, (r == n - 2, EXTRA), (r == n - 1, L1)),
-        pick(U3, (r == n - 2, LOW), (r == n - 1, L2)),
+        pick(u1, (r == n - 1, LOW)),
+        pick(u2, (r == n - 2, NEAR), (r == n - 1, l1)),
+        pick(u3, (r == n - 2, LOW), (r == n - 1, l2)),
     ]
-    return [p0, p1, LOW, L1, L2, L3], [p0, p1] + high
+    return [p0, p1, LOW, l1, l2, l3], [p0, p1] + high
 
 
 def attend_kernel(
@@ -96,8 +106,12 @@
 
     @pl.when(k == 0)
     def _():
-        for i in range(nbuf):
+        for i in range(2):
             kv[i] = bufs[i][0]
+            for j in range(2):
+                kv[A2 + 2 * i + j] = bufs[2 + i][0, j]
+        for i in range(4, nbuf):
+            kv[i + 2] = bufs[i][0]
 
     acc[...] = jnp.zeros_like(acc)
     key_pos = lax.broadcasted_iota(jnp.int32, (BLOCK, width), 0)
@@ -225,8 +239,11 @@
 
     for i in range(2):
         own_ref[0, i, :, 0] = acc[i]
-    for i, out in enumerate(outs):
-        out[0, :, 0] = acc[i + 2].astype(out.dtype)
+    for i in range(2):
+        for j in range(2):
+            outs[i][0, j, :, 0] = acc[A2 + 2 * i + j].astype(jnp.bfloat16)
+    for i in range(2, nbuf - 2):
+        outs[i][0, :, 0] = acc[i + 4].astype(jnp.bfloat16)
 
 
 def attend(n, heads, group, rank, blocks, lens, query_in, grad_out, bias, bufs):
@@ -238,22 +255,31 @@
     buf_spec = pl.BlockSpec((1, 2 * heads, BLOCK, HEAD), lambda t, k, *_: (t, 0, 0, 0))
     own_spec = pl.BlockSpec((1, 2, 2, 1, BLOCK, HEAD), lambda t, k, *_: (t, 0, 0, k, 0, 0))
     out_spec = pl.BlockSpec((1, 2, 1, BLOCK, HEAD), lambda t, k, *_: (t, 0, k, 0, 0))
+    two_spec = pl.BlockSpec((1, 2, 2 * heads, BLOCK, HEAD), lambda t, k, *_: (t, 0, 0, 0, 0))
+    two_out = pl.BlockSpec((1, 2, 2, 1, BLOCK, HEAD), lambda t, k, *_: (t, 0, 0, k, 0, 0))
     out_shape = [
         jax.ShapeDtypeStruct(query_in.shape, jnp.bfloat16),
         jax.ShapeDtypeStruct((1, heads * width), jnp.float32),
         jax.ShapeDtypeStruct((traces, 2, 2, heads, BLOCK, HEAD), jnp.float32),
-    ] + [jax.ShapeDtypeStruct((traces, 2, heads, BLOCK, HEAD), jnp.bfloat16)] * (nbuf - 2)
+    ]
+    out_shape += [jax.ShapeDtypeStruct((traces, 2, 2, heads, BLOCK, HEAD), jnp.bfloat16)] * 2
+    out_shape += [jax.ShapeDtypeStruct((traces, 2, heads, BLOCK, HEAD), jnp.bfloat16)] * (nbuf - 4)
     return pl.pallas_call(
         functools.partial(attend_kernel, n, nbuf, heads, group),
         out_shape=out_shape,
         grid_spec=pltpu.PrefetchScalarGridSpec(
             num_scalar_prefetch=3,
             grid=(traces, heads),
-            in_specs=[row_spec, row_spec, bias_spec] + [buf_spec] * nbuf,
-            out_specs=[row_spec, bias_spec, own_spec] + [out_spec] * (nbuf - 2),
+            in_specs=[row_spec, row_spec, bias_spec]
+            + [buf_spec] * 2
+            + [two_spec] * 2
+            + [buf_spec] * (nbuf - 4),
+            out_specs=[row_spec, bias_spec, own_spec]
+            + [two_out] * 2
+            + [out_spec] * (nbuf - 4),
             scratch_shapes=[
-                pltpu.VMEM((nbuf, 2 * heads, BLOCK, HEAD), jnp.bfloat16),
-                pltpu.VMEM((nbuf, 2, BLOCK, HEAD), jnp.float32),
+                pltpu.VMEM((nbuf + 2, 2 * heads, BLOCK, HEAD), jnp.bfloat16),
+                pltpu.VMEM((nbuf + 2, 2, BLOCK, HEAD), jnp.float32),
                 pltpu.VMEM((2, CAND * BLOCK, width), jnp.bfloat16),
                 pltpu.VMEM((2, CAND * BLOCK, width), jnp.bfloat16),
                 pltpu.VMEM((2, width, HEAD), jnp.bfloat16),
@@ -288,19 +314,24 @@
     width_kv = key_in.shape[-1]
     heads = width_kv // HEAD
     group = width_q // width_kv
-    up1, down1, up2, ring2, down2, extra, swap, relay = plan(n)
+    exchange, relay = plan(n)
+    even = r % 2 == 0
+    upper = r & 2 != 0
 
     halves = jnp.concatenate([key_in, value_rows_input], axis=-1).reshape(
         traces, 2, BLOCK, 2 * heads, HEAD
     )
     low = halves[:, 0].transpose(0, 2, 1, 3)
     high = halves[:, 1].transpose(0, 2, 1, 3)
-    in_l1 = send(low, up1)
-    in_u1 = send(high, down1)
-    in_l2 = send(low, up2)
-    in_u2 = send(jnp.where(r < 2, low, high), ring2)
-    in_ex = send(low, extra)
-    column = jnp.where(r < 2, low, jnp.where(r < 6, in_ex, in_u2))
+    low, high, msg_c, msg_d = lax.optimization_barrier(
+        (low, high, jnp.where(even, low, high), jnp.where(even, high, low))
+    )
+    in_c = send(msg_c, exchange["c"])
+    in_d = send(msg_d, exchange["d"])
+    in_near = send(low, exchange["near"])
+    in_far = send(low, exchange["far"])
+    low_again = lax.optimization_barrier(low)
+    column = jnp.where(r < 2, low_again, jnp.where(r < 6, in_near, in_far))
     bufs_relay = []
     for pairs in relay:
         got = send(column, pairs)
@@ -308,10 +339,15 @@
         column = jnp.where(targets, got, column)
     if relay:
         bufs_relay = [column]
-    in_l3 = send(in_l1, up2)
-    in_u3 = send(jnp.where(r == n - 1, low, in_u1), down2)
-    in_sw = send(column, swap)
-    bufs = [low, high, in_l1, in_u1, in_l2, in_u2, in_ex, in_l3, in_u3, in_sw] + bufs_relay
+    to_up = jnp.stack([low, jnp.where(even, in_d, in_c)], axis=1)
+    to_down = jnp.stack([high, jnp.where(r == n - 1, low, jnp.where(even, in_c, in_d))], axis=1)
+    msg_a, msg_b = lax.optimization_barrier(
+        (jnp.where(upper, to_down, to_up), jnp.where(upper, to_up, to_down))
+    )
+    in_a = send(msg_a, exchange["a"])
+    in_b = send(msg_b, exchange["b"])
+    in_sw = send(column, exchange["swap"])
+    bufs = [low, high, in_a, in_b, in_c, in_d, in_near, in_far, in_sw] + bufs_relay
 
     dq, dbias, own, *outs = attend(
         n,
@@ -325,51 +361,47 @@
         query_bias.reshape(1, -1),
         bufs,
     )
-    d_l1, d_u1, d_l2, d_u2, d_ex, d_l3, d_u3, d_sw = outs[:8]
+    d_a, d_b, d_c, d_d, d_near, d_far, d_sw = outs[:7]
     f32 = jnp.float32
     bf16 = jnp.bfloat16
 
     def gate(cond, value):
         return jnp.where(cond, value.astype(f32), 0.0)
 
-    back_l3 = send_back(d_l3, up2)
-    back_u3 = send_back(d_u3, down2)
-    back_sw = send_back(d_sw, swap)
-    back_l2 = send_back(d_l2, up2)
-    d_l1 = (d_l1.astype(f32) + back_l3.astype(f32)).astype(bf16)
-    d_u1 = (d_u1.astype(f32) + gate(r != n - 1, back_u3)).astype(bf16)
-    back_l1 = send_back(d_l1, up1)
-    back_u1 = send_back(d_u1, down1)
+    back_a = send_back(d_a, exchange["a"])
+    back_b = send_back(d_b, exchange["b"])
+    back_sw = send_back(d_sw, exchange["swap"])
+    from_up = jnp.where(upper, back_b, back_a).astype(f32)
+    from_down = jnp.where(upper, back_a, back_b).astype(f32)
+    d_c = (d_c.astype(f32) + jnp.where(even, from_down[:, 1], from_up[:, 1])).astype(bf16)
+    d_d = (d_d.astype(f32) + jnp.where(even, from_up[:, 1], from_down[:, 1])).astype(bf16)
+    d_near = d_near.astype(f32) + gate((r >= 4) & (r < 6), back_sw)
+    d_far = d_far.astype(f32) + gate(r >= n - 2, back_sw)
+    low_extra = 0.0
     if relay:
-        d_rl = outs[8].astype(f32) + gate((r >= 6) & (r < n - 2), back_sw)
-        d_ex = d_ex.astype(f32) + gate((r >= 4) & (r < 6), back_sw)
-        d_u2 = d_u2.astype(f32) + gate(r >= n - 2, back_sw)
-        low_extra = jnp.zeros_like(d_rl)
+        d_relay = outs[7].astype(f32) + gate((r >= 6) & (r < n - 2), back_sw)
         for pairs in reversed(relay):
             is_from = functools.reduce(jnp.logical_or, [r == b for _, b in pairs])
-            got = send_back(jnp.where(is_from, d_rl, 0.0).astype(bf16), pairs).astype(f32)
+            got = send_back(jnp.where(is_from, d_relay, 0.0).astype(bf16), pairs)
             low_extra = low_extra + gate(r < 2, got)
-            d_ex = d_ex + gate((r >= 4) & (r < 6), got)
-            d_u2 = d_u2 + gate(r >= n - 2, got)
-            d_rl = d_rl + gate((r >= 6) & (r < n - 2), got)
-        d_ex = d_ex.astype(bf16)
-        d_u2 = d_u2.astype(bf16)
-    else:
-        d_ex = (d_ex.astype(f32) + gate((r >= 4) & (r < 6), back_sw)).astype(bf16)
-        d_u2 = (d_u2.astype(f32) + gate(r >= n - 2, back_sw)).astype(bf16)
-    back_ex = send_back(d_ex, extra)
-    back_u2 = send_back(d_u2, ring2)
-
-    low_grad = own[:, 0] + back_l1.astype(f32) + back_l2.astype(f32) + back_ex.astype(f32)
-    low_grad = low_grad + gate(r < 2, back_u2) + gate(r == n - 1, back_u3) + gate(r == 1, back_sw)
-    if relay:
-        low_grad = low_grad + low_extra
-    high_grad = own[:, 1] + back_u1.astype(f32) + gate(r >= 2, back_u2)
+            d_near = d_near + gate((r >= 4) & (r < 6), got)
+            d_far = d_far + gate(r >= n - 2, got)
+            d_relay = d_relay + gate((r >= 6) & (r < n - 2), got)
+    back_c = send_back(d_c, exchange["c"])
+    back_d = send_back(d_d, exchange["d"])
+    back_near = send_back(d_near.astype(bf16), exchange["near"])
+    back_far = send_back(d_far.astype(bf16), exchange["far"])
+
+    low_grad = own[:, 0] + from_up[:, 0] + gate(r == n - 1, from_down[:, 1])
+    low_grad = low_grad + gate(r == 1, back_sw) + low_extra
+    low_grad = low_grad + jnp.where(even, back_c, back_d).astype(f32)
+    low_grad = low_grad + back_near.astype(f32) + back_far.astype(f32)
+    high_grad = own[:, 1] + from_down[:, 0] + jnp.where(even, back_d, back_c).astype(f32)
     both = jnp.stack([low_grad, high_grad], axis=1).astype(bf16)
     both = both.transpose(0, 1, 2, 4, 3, 5)
     grad_key = both[:, :, 0].reshape(traces, 2 * BLOCK, width_kv)
     grad_value = both[:, :, 1].reshape(traces, 2 * BLOCK, width_kv)
-    bias_total = butterfly(butterfly(dbias.reshape(-1), "dp"), "ctx")
+    bias_total = butterfly(butterfly(dbias.reshape(-1), "ctx"), "dp")
     rows = traces * lax.axis_size("dp") * 2 * BLOCK * n
     return dq, grad_key, grad_value, bias_total / math.sqrt(rows)
 

time: 119 us -> 112 us (0.941)
  the two profiles are of different devices: /device:TPU:0 before, /device:TPU:7 now
where the time goes in v3:
time: 112 us
  starting transfers between devices  35.4 us (32%)
  waiting for transfers between devices  31.8 us (28%)
  Pallas kernels  29.9 us (27%)
  other arithmetic  8.62 us (8%)
  local copies, waits for them, and re-layouts  4.66 us (4%)
  between operations  1.64 us (1%)
    pallas_call x1, Pallas kernels, attend(): pl.pallas_call(functools.partial(attend_kernel, n, nbuf, heads, group), o...  29.9 us
    ppermute x7, waiting for transfers between devices, send(): return lax.ppermute(value, 'ctx', pairs)  15.2 us
    ppermute x7, starting transfers between devices, send(): return lax.ppermute(value, 'ctx', pairs)  14.9 us
    ppermute x7, starting transfers between devices, send_back(): return lax.ppermute(value, 'ctx', [(b, a) for a, b in pairs])  14 us
    ppermute x5, waiting for transfers between devices, butterfly(): got = lax.ppermute(value, axis, [(s, s ^ stride) for s in range(count)])  12.2 us
    ppermute x5, starting transfers between devices, butterfly(): got = lax.ppermute(value, axis, [(s, s ^ stride) for s in range(count)])  6.51 us
    ppermute x7, waiting for transfers between devices, send_back(): return lax.ppermute(value, 'ctx', [(b, a) for a, b in pairs])  4.3 us
  transfers between devices with their start and end apart: 19, of which 9 were waited for; matrix products, arithmetic and copies ran while one was open for 6% of the time, Pallas kernels for 0%

profile of v3, /device:TPU:7, one launch (start us, length us, event | category | flops | bytes accessed | tf_op | source)
XLA Modules:
  0.0 111.9 jit_solution(10630471557285128153)
XLA Ops:
  0.6 1.1 maximum_bitcast_fusion
  1.7 0.1 copy.19
  1.9 0.1 copy_bitcast_fusion
  2.0 0.0 copy-start.1
  2.0 0.0 copy-start
  2.0 0.1 broadcast_select_fusion.2
  2.1 0.3 collective-permute-start
  2.4 4.1 %collective-permute-start.1 = (bf16[1,8,128,128]{3,2,1,0:T(8,128)(2,1)S(1)}, bf16[1,8,128,128]{3,2,1,0:T(8,128)(2,1)S(1)}, u32[]{:S(2)}, u32[]{:S(2)}) collective-permute-start(bf16[1,8,128,128]{3,2,1,0:T(8,128)(2,1)S(1)} %get-tuple-element.23), channel_id=1, source_target_pairs={{4,8},{12,16},{20,24},{8,4},{16,12},{24,20},{5,9},{13,17},{21,25},... | collective-permute-start | bytes 786440 | tf_op jit(solution)/shard_map/ppermute | solution.py:55
  6.5 4.2 %collective-permute-start.4 = (bf16[1,8,128,128]{3,2,1,0:T(8,128)(2,1)S(1)}, bf16[1,8,128,128]{3,2,1,0:T(8,128)(2,1)S(1)}, u32[]{:S(2)}, u32[]{:S(2)}) collective-permute-start(bf16[1,8,128,128]{3,2,1,0:T(8,128)(2,1)S(1)} %get-tuple-element.20.refs_0_), channel_id=1, source_target_pairs={{0,16},{4,20},{28,24},{1,17},{5,21},{29,25},{2,18},{6,22},{30,26},... | collective-permute-start | bytes 786440 | tf_op jit(solution)/shard_map/ppermute | solution.py:55
  10.8 2.1 %collective-permute-start.5 = (bf16[1,8,128,128]{3,2,1,0:T(8,128)(2,1)S(1)}, bf16[1,8,128,128]{3,2,1,0:T(8,128)(2,1)S(1)}, u32[]{:S(2)}, u32[]{:S(2)}) collective-permute-start(bf16[1,8,128,128]{3,2,1,0:T(8,128)(2,1)S(1)} %get-tuple-element.20.refs_0_), channel_id=1, source_target_pairs={{0,24},{4,28},{1,25},{5,29},{2,26},{6,30},{3,27},{7,31}} | collective-permute-start | bytes 786440 | tf_op jit(solution)/shard_map/ppermute | solution.py:55
  12.9 2.1 %collective-permute-done.refs_4_ = bf16[1,8,128,128]{3,2,1,0:T(8,128)(2,1)S(1)} collective-permute-done((bf16[1,8,128,128]{3,2,1,0:T(8,128)(2,1)S(1)}, bf16[1,8,128,128]{3,2,1,0:T(8,128)(2,1)S(1)}, u32[]{:S(2)}, u32[]{:S(2)}) %collective-permute-start) | collective-permute-done | bytes 262176 | tf_op jit(solution)/shard_map/ppermute | solution.py:55
  15.0 0.1 broadcast_select_fusion
  15.1 1.4 %collective-permute-start.2 = (bf16[1,2,8,128,128]{4,3,2,1,0:T(8,128)(2,1)S(1)}, bf16[1,2,8,128,128]{4,3,2,1,0:T(8,128)(2,1)S(1)}, u32[]{:S(2)}, u32[]{:S(2)}) collective-permute-start(bf16[1,2,8,128,128]{4,3,2,1,0:T(8,128)(2,1)S(1)} %get-tuple-element.24), channel_id=1, source_target_pairs={{0,8},{4,12},{16,24},{20,28},{8,0},{12,4},{24,16},{28,20},{1,9},{5... | collective-permute-start | bytes 1572872 | tf_op jit(solution)/shard_map/ppermute | solution.py:55
  16.5 1.5 %collective-permute-start.3 = (bf16[1,2,8,128,128]{4,3,2,1,0:T(8,128)(2,1)S(1)}, bf16[1,2,8,128,128]{4,3,2,1,0:T(8,128)(2,1)}, u32[]{:S(2)}, u32[]{:S(2)}) collective-permute-start(bf16[1,2,8,128,128]{4,3,2,1,0:T(8,128)(2,1)S(1)} %get-tuple-element.25), channel_id=1, source_target_pairs={{8,16},{12,20},{16,8},{20,12},{9,17},{13,21},{17,9},{21,13},{10,18... | collective-permute-start | bytes 1572872 | tf_op jit(solution)/shard_map/ppermute | solution.py:55
  18.0 4.7 %collective-permute-done.5.refs_7_ = bf16[1,8,128,128]{3,2,1,0:T(8,128)(2,1)S(1)} collective-permute-done((bf16[1,8,128,128]{3,2,1,0:T(8,128)(2,1)S(1)}, bf16[1,8,128,128]{3,2,1,0:T(8,128)(2,1)S(1)}, u32[]{:S(2)}, u32[]{:S(2)}) %collective-permute-start.5) | collective-permute-done | bytes 262176 | tf_op jit(solution)/shard_map/ppermute | solution.py:55
  22.7 1.3 %collective-permute-start.6 = (bf16[1,8,128,128]{3,2,1,0:T(8,128)(2,1)S(1)}, bf16[1,8,128,128]{3,2,1,0:T(8,128)(2,1)S(1)}, u32[]{:S(2)}, u32[]{:S(2)}) collective-permute-start(bf16[1,8,128,128]{3,2,1,0:T(8,128)(2,1)S(1)} %select_select_fusion), channel_id=1, source_target_pairs={{4,0},{16,20},{20,16},{24,28},{28,24},{5,1},{17,21},{21,17},{25,29... | collective-permute-start | bytes 786440 | tf_op jit(solution)/shard_map/ppermute | solution.py:55
  24.0 0.1 copy.12
  24.1 0.7 reshape.304.blocks_ref
  25.4 1.9 %collective-permute-done.6.refs_8_ = bf16[1,8,128,128]{3,2,1,0:T(8,128)(2,1)S(1)} collective-permute-done((bf16[1,8,128,128]{3,2,1,0:T(8,128)(2,1)S(1)}, bf16[1,8,128,128]{3,2,1,0:T(8,128)(2,1)S(1)}, u32[]{:S(2)}, u32[]{:S(2)}) %collective-permute-start.6) | collective-permute-done | bytes 262176 | tf_op jit(solution)/shard_map/ppermute | solution.py:55
  27.3 6.6 %collective-permute-done.2.refs_2_ = bf16[1,2,8,128,128]{4,3,2,1,0:T(8,128)(2,1)S(1)} collective-permute-done((bf16[1,2,8,128,128]{4,3,2,1,0:T(8,128)(2,1)S(1)}, bf16[1,2,8,128,128]{4,3,2,1,0:T(8,128)(2,1)S(1)}, u32[]{:S(2)}, u32[]{:S(2)}) %collective-permute-start.2) | collective-permute-done | bytes 524320 | tf_op jit(solution)/shard_map/ppermute | solution.py:55
  33.9 0.8 copy-done.8
  34.7 29.9 %attend.1 = (bf16[1,256,4096]{2,1,0:T(8,128)(2,1)}, f32[1,4096]{1,0:T(1,128)}, f32[1,2,2,4,128,128]{5,4,3,2,1,0:T(8,128)}, bf16[1,2,2,4,128,128]{5,4,3,2,1,0:T(8...) custom-call(s32[1]{0:T(128)} %bitcast.rank_ref, ...), custom_call_target="tpu_custom_call" | custom-call | tf_op jit(solution)/shard_map/attend/pallas_call | solution.py:267
  64.5 0.7 collective-permute-start.7
  65.2 5.4 %collective-permute-start.8 = (bf16[1,2,2,4,128,128]{5,4,3,2,1,0:T(8,128)(2,1)}, bf16[1,2,2,4,128,128]{5,4,3,2,1,0:T(8,128)(2,1)}, u32[]{:S(2)}, u32[]{:S(2)}) collective-permute-start(bf16[1,2,2,4,128,128]{5,4,3,2,1,0:T(8,128)(2,1)} %get-tuple-element.29), channel_id=1, source_target_pairs={{8,0},{12,4},{24,16},{28,20},{0,8},{4,12},{16,24},{20,28},{9,1},{1... | collective-permute-start | bytes 1572872 | tf_op jit(solution)/shard_map/ppermute | solution.py:59
  70.6 1.3 %collective-permute-start.9 = (bf16[1,2,4,128,128]{4,3,2,1,0:T(8,128)(2,1)}, bf16[1,2,4,128,128]{4,3,2,1,0:T(8,128)(2,1)S(1)}, u32[]{:S(2)}, u32[]{:S(2)}) collective-permute-start(bf16[1,2,4,128,128]{4,3,2,1,0:T(8,128)(2,1)} %get-tuple-element.30), channel_id=1, source_target_pairs={{0,4},{20,16},{16,20},{28,24},{24,28},{1,5},{21,17},{17,21},{29,25... | collective-permute-start | bytes 786440 | tf_op jit(solution)/shard_map/ppermute | solution.py:59
  71.9 2.2 %collective-permute-start.14 = (f32[4096]{0:T(1024)}, f32[4096]{0:T(1024)S(1)}, u32[]{:S(2)}, u32[]{:S(2)}) collective-permute-start(f32[4096]{0:T(1024)} %bitcast.66), channel_id=1, source_target_pairs={{0,4},{4,0},{8,12},{12,8},{16,20},{20,16},{24,28},{28,24},{1,5},{5... | collective-permute-start | bytes 49160 | tf_op jit(solution)/shard_map/ppermute | solution.py:303
  74.0 6.0 %collective-permute-done.14 = f32[4096]{0:T(1024)S(1)} collective-permute-done((f32[4096]{0:T(1024)}, f32[4096]{0:T(1024)S(1)}, u32[]{:S(2)}, u32[]{:S(2)}) %collective-permute-start.14) | collective-permute-done | bytes 16416 | tf_op jit(solution)/shard_map/ppermute | solution.py:303
  80.0 0.7 add.101
  80.7 2.7 %collective-permute-done.15 = f32[4096]{0:T(1024)S(1)} collective-permute-done((f32[4096]{0:T(1024)S(1)}, f32[4096]{0:T(1024)S(1)}, u32[]{:S(2)}, u32[]{:S(2)}) %collective-permute-start.15) | collective-permute-done | bytes 16416 | tf_op jit(solution)/shard_map/ppermute | solution.py:303
  83.4 2.0 %fusion.6 = (bf16[1,2,4,128,128]{4,3,2,1,0:T(8,128)(2,1)}, bf16[1,2,4,128,128]{4,3,2,1,0:T(8,128)(2,1)}) fusion(bf16[1,2,4,128,128]{4,3,2,1,0:T(8,128)(2,1)S(1)} %collective-permute-done.9, bf16[1,2,4,128,128]{4,3,2,1,0:T(8,128)(2,1)} %get-tuple-element.33, pred[]{:T(512)S(6)} %and.14, pred[]{:T(512)S(6)} %ge.7, bf16[1,2,4,128,128]{4,3,2,1,0:T(8,128)(2,1)} %get-tuple-element.34), kind=kLoop, calls=%fused_computation.9 | loop fusion | flops 1179648 | bytes 1310722 | tf_op jit(solution)/shard_map/convert_element_type | solution.py:392
  85.5 1.3 %collective-permute-start.12 = (bf16[1,2,4,128,128]{4,3,2,1,0:T(8,128)(2,1)}, bf16[1,2,4,128,128]{4,3,2,1,0:T(8,128)(2,1)}, u32[]{:S(2)}, u32[]{:S(2)}) collective-permute-start(bf16[1,2,4,128,128]{4,3,2,1,0:T(8,128)(2,1)} %get-tuple-element.52), channel_id=1, source_target_pairs={{16,0},{20,4},{24,28},{17,1},{21,5},{25,29},{18,2},{22,6},{26,30},... | collective-permute-start | bytes 786440 | tf_op jit(solution)/shard_map/ppermute | solution.py:59
  86.8 1.4 %collective-permute-start.13 = (bf16[1,2,4,128,128]{4,3,2,1,0:T(8,128)(2,1)}, bf16[1,2,4,128,128]{4,3,2,1,0:T(8,128)(2,1)}, u32[]{:S(2)}, u32[]{:S(2)}) collective-permute-start(bf16[1,2,4,128,128]{4,3,2,1,0:T(8,128)(2,1)} %get-tuple-element.53), channel_id=1, source_target_pairs={{24,0},{28,4},{25,1},{29,5},{26,2},{30,6},{27,3},{31,7}} | collective-permute-start | bytes 786440 | tf_op jit(solution)/shard_map/ppermute | solution.py:59
  88.2 0.8 copy-done.7
  89.0 1.3 %select_convert_fusion.1 = (f32[1,2,2,4,128,128]{5,4,3,2,1,0:T(8,128)S(1)}, f32[1,2,2,4,128,128]{5,4,3,2,1,0:T(8,128)S(1)}) fusion(bf16[1,2,2,4,128,128]{5,4,3,2,1,0:T(8,128)(2,1)} %copy-done.7, bf16[1,2,2,4,128,128]{5,4,3,2,1,0:T(8,128)(2,1)} %collective-permute-done.8, pred[]{:T(512)S(6)} %ne.10), kind=kLoop, calls=%fused_computation.28 | loop fusion | flops 1048576 | bytes 3145729 | tf_op jit(solution)/shard_map/convert_element_type | solution.py:374
  90.4 1.0 fusion.15
  91.4 4.0 %collective-permute-start.11 = (bf16[1,2,4,128,128]{4,3,2,1,0:T(8,128)(2,1)}, bf16[1,2,4,128,128]{4,3,2,1,0:T(8,128)(2,1)}, u32[]{:S(2)}, u32[]{:S(2)}) collective-permute-start(bf16[1,2,4,128,128]{4,3,2,1,0:T(8,128)(2,1)} %get-tuple-element.39), channel_id=1, source_target_pairs={{8,4},{16,12},{24,20},{4,8},{12,16},{20,24},{9,5},{17,13},{25,21},... | collective-permute-start | bytes 786440 | tf_op jit(solution)/shard_map/ppermute | solution.py:59
  95.3 4.1 %collective-permute-start.17 = (f32[4096]{0:T(1024)S(1)}, f32[4096]{0:T(1024)S(1)}, u32[]{:S(2)}, u32[]{:S(2)}) collective-permute-start(f32[4096]{0:T(1024)S(1)} %add.103), channel_id=1, source_target_pairs={{0,1},{1,0},{2,3},{3,2},{4,5},{5,4},{6,7},{7,6},{8,9},{9,8},{10,11... | collective-permute-start | bytes 49160 | tf_op jit(solution)/shard_map/ppermute | solution.py:303
  99.5 0.8 collective-permute-done.17
  100.3 0.2 collective-permute-start.18
  100.5 2.8 %collective-permute-done.18 = f32[4096]{0:T(1024)S(1)} collective-permute-done((f32[4096]{0:T(1024)S(1)}, f32[4096]{0:T(1024)S(1)}, u32[]{:S(2)}, u32[]{:S(2)}) %collective-permute-start.18) | collective-permute-done | bytes 16416 | tf_op jit(solution)/shard_map/ppermute | solution.py:303
  103.3 0.6 add_multiply_fusion
  103.9 4.3 %collective-permute-done.11 = bf16[1,2,4,128,128]{4,3,2,1,0:T(8,128)(2,1)} collective-permute-done((bf16[1,2,4,128,128]{4,3,2,1,0:T(8,128)(2,1)}, bf16[1,2,4,128,128]{4,3,2,1,0:T(8,128)(2,1)}, u32[]{:S(2)}, u32[]{:S(2)}) %collective-permute-start.11) | collective-permute-done | bytes 262176 | tf_op jit(solution)/shard_map/ppermute | solution.py:59
  108.2 1.5 %fusion.17 = (bf16[1,1,2,4,128,128]{5,4,3,2,1,0:T(8,128)(2,1)S(1)}, bf16[1,1,2,4,128,128]{5,4,3,2,1,0:T(8,128)(2,1)S(1)}) fusion(bf16[1,2,4,128,128]{4,3,2,1,0:T(8,128)(2,1)} %collective-permute-done.13, bf16[1,2,4,128,128]{4,3,2,1,0:T(8,128)(2,1)} %collective-permute-done.12, bf16[1,2,4,128,128]{4,3,2,1,0:T(8,128)(2,1)} %collective-permute-done.10, ...), kind=kLoop, calls=%fused_computation.37 | loop fusion | flops 2490368 | bytes 4456451 | tf_op jit(solution)/shard_map/stack | solution.py:400
  109.8 0.1 maximum_bitcast_fusion.1
  109.9 0.2 copy.15
  110.1 0.8 reshape_squeeze.6
  110.9 0.2 copy.16
  111.1 0.8 reshape_squeeze.7
  (42 shorter events, 0.3 us)
Async XLA Ops:
  2.0 13.1 %copy-start.1 = (bf16[1,8,128,128]{3,2,1,0:T(8,128)(2,1)}, bf16[1,8,128,128]{3,2,1,0:T(8,128)(2,1)S(1)}, u32[]{:S(2)}) copy-start(bf16[1,8,128,128]{3,2,1,0:T(8,128)(2,1)S(1)} %get-tuple-element.21.refs_1_) | copy-start | bytes 786436
  2.0 20.7 %copy-start = (bf16[1,8,128,128]{3,2,1,0:T(8,128)(2,1)}, bf16[1,8,128,128]{3,2,1,0:T(8,128)(2,1)S(1)}, u32[]{:S(2)}) copy-start(bf16[1,8,128,128]{3,2,1,0:T(8,128)(2,1)S(1)} %get-tuple-element.20.refs_0_) | copy-start | bytes 786436
  2.1 12.9 %collective-permute-start = (bf16[1,8,128,128]{3,2,1,0:T(8,128)(2,1)S(1)}, bf16[1,8,128,128]{3,2,1,0:T(8,128)(2,1)S(1)}, u32[]{:S(2)}, u32[]{:S(2)}) collective-permute-start(bf16[1,8,128,128]{3,2,1,0:T(8,128)(2,1)S(1)} %get-tuple-element.22), channel_id=1, source_target_pairs={{0,4},{8,12},{16,20},{24,28},{4,0},{12,8},{20,16},{28,24},{1,5},{9... | collective-permute-start | bytes 786440 | tf_op jit(solution)/shard_map/ppermute | solution.py:55
  2.4 12.6 %collective-permute-start.1 = (bf16[1,8,128,128]{3,2,1,0:T(8,128)(2,1)S(1)}, bf16[1,8,128,128]{3,2,1,0:T(8,128)(2,1)S(1)}, u32[]{:S(2)}, u32[]{:S(2)}) collective-permute-start(bf16[1,8,128,128]{3,2,1,0:T(8,128)(2,1)S(1)} %get-tuple-element.23), channel_id=1, source_target_pairs={{4,8},{12,16},{20,24},{8,4},{16,12},{24,20},{5,9},{13,17},{21,25},... | collective-permute-start | bytes 786440 | tf_op jit(solution)/shard_map/ppermute | solution.py:55
  6.5 11.4 %collective-permute-start.4 = (bf16[1,8,128,128]{3,2,1,0:T(8,128)(2,1)S(1)}, bf16[1,8,128,128]{3,2,1,0:T(8,128)(2,1)S(1)}, u32[]{:S(2)}, u32[]{:S(2)}) collective-permute-start(bf16[1,8,128,128]{3,2,1,0:T(8,128)(2,1)S(1)} %get-tuple-element.20.refs_0_), channel_id=1, source_target_pairs={{0,16},{4,20},{28,24},{1,17},{5,21},{29,25},{2,18},{6,22},{30,26},... | collective-permute-start | bytes 786440 | tf_op jit(solution)/shard_map/ppermute | solution.py:55
  10.8 11.9 %collective-permute-start.5 = (bf16[1,8,128,128]{3,2,1,0:T(8,128)(2,1)S(1)}, bf16[1,8,128,128]{3,2,1,0:T(8,128)(2,1)S(1)}, u32[]{:S(2)}, u32[]{:S(2)}) collective-permute-start(bf16[1,8,128,128]{3,2,1,0:T(8,128)(2,1)S(1)} %get-tuple-element.20.refs_0_), channel_id=1, source_target_pairs={{0,24},{4,28},{1,25},{5,29},{2,26},{6,30},{3,27},{7,31}} | collective-permute-start | bytes 786440 | tf_op jit(solution)/shard_map/ppermute | solution.py:55
  12.8 11.2 %copy-start.12 = (s32[1,16,6]{1,0,2:T(1,128)S(1)}, s32[1,16,6]{1,0,2:T(1,128)}, u32[]{:S(2)}) copy-start(s32[1,16,6]{1,0,2:T(1,128)} %param.12) | copy-start | bytes 1156
  15.0 7.7 %copy-start.5 = (bf16[1,8,128,128]{3,2,1,0:T(8,128)(2,1)}, bf16[1,8,128,128]{3,2,1,0:T(8,128)(2,1)S(1)}, u32[]{:S(2)}) copy-start(bf16[1,8,128,128]{3,2,1,0:T(8,128)(2,1)S(1)} %collective-permute-done.refs_4_) | copy-start | bytes 786436
  15.0 7.7 %copy-start.6 = (bf16[1,8,128,128]{3,2,1,0:T(8,128)(2,1)}, bf16[1,8,128,128]{3,2,1,0:T(8,128)(2,1)S(1)}, u32[]{:S(2)}) copy-start(bf16[1,8,128,128]{3,2,1,0:T(8,128)(2,1)S(1)} %collective-permute-done.1.refs_5_) | copy-start | bytes 786436
  15.1 18.7 %collective-permute-start.2 = (bf16[1,2,8,128,128]{4,3,2,1,0:T(8,128)(2,1)S(1)}, bf16[1,2,8,128,128]{4,3,2,1,0:T(8,128)(2,1)S(1)}, u32[]{:S(2)}, u32[]{:S(2)}) collective-permute-start(bf16[1,2,8,128,128]{4,3,2,1,0:T(8,128)(2,1)S(1)} %get-tuple-element.24), channel_id=1, source_target_pairs={{0,8},{4,12},{16,24},{20,28},{8,0},{12,4},{24,16},{28,20},{1,9},{5... | collective-permute-start | bytes 1572872 | tf_op jit(solution)/shard_map/ppermute | solution.py:55
  16.5 17.4 %collective-permute-start.3 = (bf16[1,2,8,128,128]{4,3,2,1,0:T(8,128)(2,1)S(1)}, bf16[1,2,8,128,128]{4,3,2,1,0:T(8,128)(2,1)}, u32[]{:S(2)}, u32[]{:S(2)}) collective-permute-start(bf16[1,2,8,128,128]{4,3,2,1,0:T(8,128)(2,1)S(1)} %get-tuple-element.25), channel_id=1, source_target_pairs={{8,16},{12,20},{16,8},{20,12},{9,17},{13,21},{17,9},{21,13},{10,18... | collective-permute-start | bytes 1572872 | tf_op jit(solution)/shard_map/ppermute | solution.py:55
  18.0 15.9 %copy-start.3 = (bf16[1,8,128,128]{3,2,1,0:T(8,128)(2,1)}, bf16[1,8,128,128]{3,2,1,0:T(8,128)(2,1)S(1)}, u32[]{:S(2)}) copy-start(bf16[1,8,128,128]{3,2,1,0:T(8,128)(2,1)S(1)} %collective-permute-done.4.refs_6_) | copy-start | bytes 786436
  22.6 11.2 %copy-start.4 = (bf16[1,8,128,128]{3,2,1,0:T(8,128)(2,1)}, bf16[1,8,128,128]{3,2,1,0:T(8,128)(2,1)S(1)}, u32[]{:S(2)}) copy-start(bf16[1,8,128,128]{3,2,1,0:T(8,128)(2,1)S(1)} %collective-permute-done.5.refs_7_) | copy-start | bytes 786436
  22.7 4.6 %collective-permute-start.6 = (bf16[1,8,128,128]{3,2,1,0:T(8,128)(2,1)S(1)}, bf16[1,8,128,128]{3,2,1,0:T(8,128)(2,1)S(1)}, u32[]{:S(2)}, u32[]{:S(2)}) collective-permute-start(bf16[1,8,128,128]{3,2,1,0:T(8,128)(2,1)S(1)} %select_select_fusion), channel_id=1, source_target_pairs={{4,0},{16,20},{20,16},{24,28},{28,24},{5,1},{17,21},{21,17},{25,29... | collective-permute-start | bytes 786440 | tf_op jit(solution)/shard_map/ppermute | solution.py:55
  27.3 6.6 %copy-start.11 = (bf16[1,8,128,128]{3,2,1,0:T(8,128)(2,1)}, bf16[1,8,128,128]{3,2,1,0:T(8,128)(2,1)S(1)}, u32[]{:S(2)}) copy-start(bf16[1,8,128,128]{3,2,1,0:T(8,128)(2,1)S(1)} %collective-permute-done.6.refs_8_) | copy-start | bytes 786436
  33.9 0.8 copy-start.8
  64.5 23.7 %collective-permute-start.7 = (bf16[1,2,2,4,128,128]{5,4,3,2,1,0:T(8,128)(2,1)}, bf16[1,2,2,4,128,128]{5,4,3,2,1,0:T(8,128)(2,1)S(1)}, u32[]{:S(2)}, u32[]{:S(2)}) collective-permute-start(bf16[1,2,2,4,128,128]{5,4,3,2,1,0:T(8,128)(2,1)} %get-tuple-element.28), channel_id=1, source_target_pairs={{16,8},{20,12},{8,16},{12,20},{17,9},{21,13},{9,17},{13,21},{18,10... | collective-permute-start | bytes 1572872 | tf_op jit(solution)/shard_map/ppermute | solution.py:59
  65.2 23.8 %collective-permute-start.8 = (bf16[1,2,2,4,128,128]{5,4,3,2,1,0:T(8,128)(2,1)}, bf16[1,2,2,4,128,128]{5,4,3,2,1,0:T(8,128)(2,1)}, u32[]{:S(2)}, u32[]{:S(2)}) collective-permute-start(bf16[1,2,2,4,128,128]{5,4,3,2,1,0:T(8,128)(2,1)} %get-tuple-element.29), channel_id=1, source_target_pairs={{8,0},{12,4},{24,16},{28,20},{0,8},{4,12},{16,24},{20,28},{9,1},{1... | collective-permute-start | bytes 1572872 | tf_op jit(solution)/shard_map/ppermute | solution.py:59
  70.6 12.8 %collective-permute-start.9 = (bf16[1,2,4,128,128]{4,3,2,1,0:T(8,128)(2,1)}, bf16[1,2,4,128,128]{4,3,2,1,0:T(8,128)(2,1)S(1)}, u32[]{:S(2)}, u32[]{:S(2)}) collective-permute-start(bf16[1,2,4,128,128]{4,3,2,1,0:T(8,128)(2,1)} %get-tuple-element.30), channel_id=1, source_target_pairs={{0,4},{20,16},{16,20},{28,24},{24,28},{1,5},{21,17},{17,21},{29,25... | collective-permute-start | bytes 786440 | tf_op jit(solution)/shard_map/ppermute | solution.py:59
  71.9 8.1 %collective-permute-start.14 = (f32[4096]{0:T(1024)}, f32[4096]{0:T(1024)S(1)}, u32[]{:S(2)}, u32[]{:S(2)}) collective-permute-start(f32[4096]{0:T(1024)} %bitcast.66), channel_id=1, source_target_pairs={{0,4},{4,0},{8,12},{12,8},{16,20},{20,16},{24,28},{28,24},{1,5},{5... | collective-permute-start | bytes 49160 | tf_op jit(solution)/shard_map/ppermute | solution.py:303
  80.7 2.7 %collective-permute-start.15 = (f32[4096]{0:T(1024)S(1)}, f32[4096]{0:T(1024)S(1)}, u32[]{:S(2)}, u32[]{:S(2)}) collective-permute-start(f32[4096]{0:T(1024)S(1)} %add.101), channel_id=1, source_target_pairs={{0,8},{4,12},{8,0},{12,4},{16,24},{20,28},{24,16},{28,20},{1,9},{5... | collective-permute-start | bytes 49160 | tf_op jit(solution)/shard_map/ppermute | solution.py:303
  83.4 11.9 %collective-permute-start.16 = (f32[4096]{0:T(1024)S(1)}, f32[4096]{0:T(1024)S(1)}, u32[]{:S(2)}, u32[]{:S(2)}) collective-permute-start(f32[4096]{0:T(1024)S(1)} %add.102), channel_id=1, source_target_pairs={{0,16},{4,20},{8,24},{12,28},{16,0},{20,4},{24,8},{28,12},{1,17},{... | collective-permute-start | bytes 49160 | tf_op jit(solution)/shard_map/ppermute | solution.py:303
  83.4 7.0 %copy-start.9 = (bf16[1,2,4,128,128]{4,3,2,1,0:T(8,128)(2,1)S(1)}, bf16[1,2,4,128,128]{4,3,2,1,0:T(8,128)(2,1)}, u32[]{:S(2)}) copy-start(bf16[1,2,4,128,128]{4,3,2,1,0:T(8,128)(2,1)} %get-tuple-element.31) | copy-start | bytes 786436
  83.4 7.0 %copy-start.10 = (bf16[1,2,4,128,128]{4,3,2,1,0:T(8,128)(2,1)S(1)}, bf16[1,2,4,128,128]{4,3,2,1,0:T(8,128)(2,1)}, u32[]{:S(2)}) copy-start(bf16[1,2,4,128,128]{4,3,2,1,0:T(8,128)(2,1)} %get-tuple-element.32) | copy-start | bytes 786436
  85.5 18.4 %collective-permute-start.12 = (bf16[1,2,4,128,128]{4,3,2,1,0:T(8,128)(2,1)}, bf16[1,2,4,128,128]{4,3,2,1,0:T(8,128)(2,1)}, u32[]{:S(2)}, u32[]{:S(2)}) collective-permute-start(bf16[1,2,4,128,128]{4,3,2,1,0:T(8,128)(2,1)} %get-tuple-element.52), channel_id=1, source_target_pairs={{16,0},{20,4},{24,28},{17,1},{21,5},{25,29},{18,2},{22,6},{26,30},... | collective-permute-start | bytes 786440 | tf_op jit(solution)/shard_map/ppermute | solution.py:59
  86.8 21.5 %copy-start.2 = (f32[1,2,2,4,128,128]{5,4,3,2,1,0:T(8,128)S(1)}, f32[1,2,2,4,128,128]{5,4,3,2,1,0:T(8,128)}, u32[]{:S(2)}) copy-start(f32[1,2,2,4,128,128]{5,4,3,2,1,0:T(8,128)} %get-tuple-element.27) | copy-start | bytes 3145732
  86.8 17.1 %collective-permute-start.13 = (bf16[1,2,4,128,128]{4,3,2,1,0:T(8,128)(2,1)}, bf16[1,2,4,128,128]{4,3,2,1,0:T(8,128)(2,1)}, u32[]{:S(2)}, u32[]{:S(2)}) collective-permute-start(bf16[1,2,4,128,128]{4,3,2,1,0:T(8,128)(2,1)} %get-tuple-element.53), channel_id=1, source_target_pairs={{24,0},{28,4},{25,1},{29,5},{26,2},{30,6},{27,3},{31,7}} | collective-permute-start | bytes 786440 | tf_op jit(solution)/shard_map/ppermute | solution.py:59
  88.2 0.8 copy-start.7
  91.4 12.6 %collective-permute-start.10 = (bf16[1,2,4,128,128]{4,3,2,1,0:T(8,128)(2,1)}, bf16[1,2,4,128,128]{4,3,2,1,0:T(8,128)(2,1)}, u32[]{:S(2)}, u32[]{:S(2)}) collective-permute-start(bf16[1,2,4,128,128]{4,3,2,1,0:T(8,128)(2,1)} %get-tuple-element.38), channel_id=1, source_target_pairs={{4,0},{12,8},{20,16},{28,24},{0,4},{8,12},{16,20},{24,28},{5,1},{1... | collective-permute-start | bytes 786440 | tf_op jit(solution)/shard_map/ppermute | solution.py:59
  91.4 16.9 %collective-permute-start.11 = (bf16[1,2,4,128,128]{4,3,2,1,0:T(8,128)(2,1)}, bf16[1,2,4,128,128]{4,3,2,1,0:T(8,128)(2,1)}, u32[]{:S(2)}, u32[]{:S(2)}) collective-permute-start(bf16[1,2,4,128,128]{4,3,2,1,0:T(8,128)(2,1)} %get-tuple-element.39), channel_id=1, source_target_pairs={{8,4},{16,12},{24,20},{4,8},{12,16},{20,24},{9,5},{17,13},{25,21},... | collective-permute-start | bytes 786440 | tf_op jit(solution)/shard_map/ppermute | solution.py:59
  95.3 5.0 %collective-permute-start.17 = (f32[4096]{0:T(1024)S(1)}, f32[4096]{0:T(1024)S(1)}, u32[]{:S(2)}, u32[]{:S(2)}) collective-permute-start(f32[4096]{0:T(1024)S(1)} %add.103), channel_id=1, source_target_pairs={{0,1},{1,0},{2,3},{3,2},{4,5},{5,4},{6,7},{7,6},{8,9},{9,8},{10,11... | collective-permute-start | bytes 49160 | tf_op jit(solution)/shard_map/ppermute | solution.py:303
  100.3 3.0 %collective-permute-start.18 = (f32[4096]{0:T(1024)S(1)}, f32[4096]{0:T(1024)S(1)}, u32[]{:S(2)}, u32[]{:S(2)}) collective-permute-start(f32[4096]{0:T(1024)S(1)} %add.104), channel_id=1, source_target_pairs={{0,2},{1,3},{2,0},{3,1},{4,6},{5,7},{6,4},{7,5},{8,10},{9,11},{10,... | collective-permute-start | bytes 49160 | tf_op jit(solution)/shard_map/ppermute | solution.py:303

commit v4 on v3

--- a/solution.py
+++ b/solution.py
@@ -212,18 +212,20 @@
             else:
                 dbias_ref[:, cols] += row
 
-    def key_grad(task, count):
+    def key_grad(task, count, which=(0, 1)):
         half, pair = divmod(task, pairs)
         span = slice((pair - count + 1) * width, (pair + 1) * width)
-        dk = scale * jnp.dot(
-            ds_buf[half, :, span], q_buf[half, span], preferred_element_type=jnp.float32
-        )
-        dv = jnp.dot(
-            probs_buf[half, :, span], g_buf[half, span], preferred_element_type=jnp.float32
-        )
-        for c in range(CAND):
-            acc[places[half][c], 0] += dk[part[c]]
-            acc[places[half][c], 1] += dv[part[c]]
+        for value in which:
+            if value:
+                grad = jnp.dot(
+                    probs_buf[half, :, span], g_buf[half, span], preferred_element_type=jnp.float32
+                )
+            else:
+                grad = scale * jnp.dot(
+                    ds_buf[half, :, span], q_buf[half, span], preferred_element_type=jnp.float32
+                )
+            for c in range(CAND):
+                acc[places[half][c], value] += grad[part[c]]
 
     tasks = 2 * pairs
     load(0)
@@ -232,10 +234,15 @@
         if task + 1 < tasks:
             load(task + 1)
             products(task + 1)
+        if task > 0:
+            query_grad(task - 1)
+            if task % 2 == 0:
+                key_grad(task - 1, 2, (0,))
+            elif task > 1:
+                key_grad(task - 2, 2, (1,))
         softmax(task)
-        query_grad(task)
-        if task % pairs == pairs - 1:
-            key_grad(task, pairs)
+    query_grad(tasks - 1)
+    key_grad(tasks - 1, 2)
 
     for i in range(2):
         own_ref[0, i, :, 0] = acc[i]
@@ -296,14 +303,22 @@
     )(rank, blocks, lens, query_in, grad_out, bias, *bufs)
 
 
-def butterfly(value, axis):
-    count = lax.axis_size(axis)
-    stride = 1
-    while stride < count:
-        got = lax.ppermute(value, axis, [(s, s ^ stride) for s in range(count)])
-        value = value + got
+def swapped(value, axis, stride):
+    pairs = [(s, s ^ stride) for s in range(lax.axis_size(axis))]
+    return lax.ppermute(value, axis, pairs)
+
+
+def butterfly(value, axis, stride=1, stop=None):
+    stop = lax.axis_size(axis) if stop is None else stop
+    while stride < stop:
+        value = value + swapped(value, axis, stride)
         stride *= 2
     return value
+
+
+def quad(value, axis, stride):
+    first, second, third = (swapped(value, axis, i * stride) for i in (1, 2, 3))
+    return (value + first) + (second + third)
 
 
 def body(query_in, key_in, value_rows_input, grad_out, query_bias, key_blocks, trace_len):
@@ -398,10 +413,13 @@
     low_grad = low_grad + back_near.astype(f32) + back_far.astype(f32)
     high_grad = own[:, 1] + from_down[:, 0] + jnp.where(even, back_d, back_c).astype(f32)
     both = jnp.stack([low_grad, high_grad], axis=1).astype(bf16)
-    both = both.transpose(0, 1, 2, 4, 3, 5)
-    grad_key = both[:, :, 0].reshape(traces, 2 * BLOCK, width_kv)
-    grad_value = both[:, :, 1].reshape(traces, 2 * BLOCK, width_kv)
-    bias_total = butterfly(butterfly(dbias.reshape(-1), "ctx"), "dp")
+    grad_key, grad_value = (
+        jnp.concatenate([both[:, :, i, h] for h in range(heads)], axis=-1).reshape(
+            traces, 2 * BLOCK, width_kv
+        )
+        for i in range(2)
+    )
+    bias_total = butterfly(butterfly(quad(butterfly(dbias.reshape(-1), "ctx", 1, 2), "ctx", 2), "ctx", 8), "dp")
     rows = traces * lax.axis_size("dp") * 2 * BLOCK * n
     return dq, grad_key, grad_value, bias_total / math.sqrt(rows)
 

time: 112 us -> 109 us (0.973)
  the two profiles are of different devices: /device:TPU:7 before, /device:TPU:3 now
where the time goes in v4:
time: 109 us
  starting transfers between devices  37.2 us (34%)
  waiting for transfers between devices  29.8 us (27%)
  Pallas kernels  27.5 us (25%)
  other arithmetic  10.1 us (9%)
  local copies, waits for them, and re-layouts  2.63 us (2%)
  between operations  1.61 us (1%)
    pallas_call x1, Pallas kernels, attend(): pl.pallas_call(functools.partial(attend_kernel, n, nbuf, heads, group), o...  27.5 us
    ppermute x7, waiting for transfers between devices, send(): return lax.ppermute(value, 'ctx', pairs)  15.2 us
    ppermute x7, starting transfers between devices, send(): return lax.ppermute(value, 'ctx', pairs)  14.9 us
    ppermute x7, starting transfers between devices, send_back(): return lax.ppermute(value, 'ctx', [(b, a) for a, b in pairs])  12.3 us
    ppermute x6, starting transfers between devices, swapped(): return lax.ppermute(value, axis, pairs)  9.97 us
    ppermute x6, waiting for transfers between devices, swapped(): return lax.ppermute(value, axis, pairs)  8.48 us
    ppermute x7, waiting for transfers between devices, send_back(): return lax.ppermute(value, 'ctx', [(b, a) for a, b in pairs])  6.12 us
  transfers between devices with their start and end apart: 20, of which 8 were waited for; matrix products, arithmetic and copies ran while one was open for 6% of the time, Pallas kernels for 0%

profile of v4, /device:TPU:3, one launch (start us, length us, event | category | flops | bytes accessed | tf_op | source)
XLA Modules:
  0.0 108.8 jit_solution(17079988654627896735)
XLA Ops:
  0.6 1.1 maximum_bitcast_fusion
  1.7 0.1 copy.17
  1.9 0.1 copy_bitcast_fusion
  2.0 0.0 copy-start.1
  2.0 0.0 copy-start
  2.0 0.1 broadcast_select_fusion.2
  2.1 0.1 collective-permute-start
  2.2 4.4 %collective-permute-start.1 = (bf16[1,8,128,128]{3,2,1,0:T(8,128)(2,1)S(1)}, bf16[1,8,128,128]{3,2,1,0:T(8,128)(2,1)S(1)}, u32[]{:S(2)}, u32[]{:S(2)}) collective-permute-start(bf16[1,8,128,128]{3,2,1,0:T(8,128)(2,1)S(1)} %get-tuple-element.23), channel_id=1, source_target_pairs={{4,8},{12,16},{20,24},{8,4},{16,12},{24,20},{5,9},{13,17},{21,25},... | collective-permute-start | bytes 786440 | tf_op jit(solution)/shard_map/ppermute | solution.py:55
  6.5 4.2 %collective-permute-start.4 = (bf16[1,8,128,128]{3,2,1,0:T(8,128)(2,1)S(1)}, bf16[1,8,128,128]{3,2,1,0:T(8,128)(2,1)S(1)}, u32[]{:S(2)}, u32[]{:S(2)}) collective-permute-start(bf16[1,8,128,128]{3,2,1,0:T(8,128)(2,1)S(1)} %get-tuple-element.20.refs_0_), channel_id=1, source_target_pairs={{0,16},{4,20},{28,24},{1,17},{5,21},{29,25},{2,18},{6,22},{30,26},... | collective-permute-start | bytes 786440 | tf_op jit(solution)/shard_map/ppermute | solution.py:55
  10.8 2.1 %collective-permute-start.5 = (bf16[1,8,128,128]{3,2,1,0:T(8,128)(2,1)S(1)}, bf16[1,8,128,128]{3,2,1,0:T(8,128)(2,1)S(1)}, u32[]{:S(2)}, u32[]{:S(2)}) collective-permute-start(bf16[1,8,128,128]{3,2,1,0:T(8,128)(2,1)S(1)} %get-tuple-element.20.refs_0_), channel_id=1, source_target_pairs={{0,24},{4,28},{1,25},{5,29},{2,26},{6,30},{3,27},{7,31}} | collective-permute-start | bytes 786440 | tf_op jit(solution)/shard_map/ppermute | solution.py:55
  12.8 0.0 copy-start.13
  12.9 2.1 %collective-permute-done.refs_4_ = bf16[1,8,128,128]{3,2,1,0:T(8,128)(2,1)S(1)} collective-permute-done((bf16[1,8,128,128]{3,2,1,0:T(8,128)(2,1)S(1)}, bf16[1,8,128,128]{3,2,1,0:T(8,128)(2,1)S(1)}, u32[]{:S(2)}, u32[]{:S(2)}) %collective-permute-start) | collective-permute-done | bytes 262176 | tf_op jit(solution)/shard_map/ppermute | solution.py:55
  15.0 0.0 collective-permute-done.1.refs_5_
  15.0 0.1 broadcast_select_fusion
  15.1 1.4 %collective-permute-start.2 = (bf16[1,2,8,128,128]{4,3,2,1,0:T(8,128)(2,1)S(1)}, bf16[1,2,8,128,128]{4,3,2,1,0:T(8,128)(2,1)S(1)}, u32[]{:S(2)}, u32[]{:S(2)}) collective-permute-start(bf16[1,2,8,128,128]{4,3,2,1,0:T(8,128)(2,1)S(1)} %get-tuple-element.24), channel_id=1, source_target_pairs={{0,8},{4,12},{16,24},{20,28},{8,0},{12,4},{24,16},{28,20},{1,9},{5... | collective-permute-start | bytes 1572872 | tf_op jit(solution)/shard_map/ppermute | solution.py:55
  16.5 1.5 %collective-permute-start.3 = (bf16[1,2,8,128,128]{4,3,2,1,0:T(8,128)(2,1)S(1)}, bf16[1,2,8,128,128]{4,3,2,1,0:T(8,128)(2,1)}, u32[]{:S(2)}, u32[]{:S(2)}) collective-permute-start(bf16[1,2,8,128,128]{4,3,2,1,0:T(8,128)(2,1)S(1)} %get-tuple-element.25), channel_id=1, source_target_pairs={{8,16},{12,20},{16,8},{20,12},{9,17},{13,21},{17,9},{21,13},{10,18... | collective-permute-start | bytes 1572872 | tf_op jit(solution)/shard_map/ppermute | solution.py:55
  18.0 4.7 %collective-permute-done.5.refs_7_ = bf16[1,8,128,128]{3,2,1,0:T(8,128)(2,1)S(1)} collective-permute-done((bf16[1,8,128,128]{3,2,1,0:T(8,128)(2,1)S(1)}, bf16[1,8,128,128]{3,2,1,0:T(8,128)(2,1)S(1)}, u32[]{:S(2)}, u32[]{:S(2)}) %collective-permute-start.5) | collective-permute-done | bytes 262176 | tf_op jit(solution)/shard_map/ppermute | solution.py:55
  22.7 1.3 %collective-permute-start.6 = (bf16[1,8,128,128]{3,2,1,0:T(8,128)(2,1)S(1)}, bf16[1,8,128,128]{3,2,1,0:T(8,128)(2,1)S(1)}, u32[]{:S(2)}, u32[]{:S(2)}) collective-permute-start(bf16[1,8,128,128]{3,2,1,0:T(8,128)(2,1)S(1)} %select_select_fusion), channel_id=1, source_target_pairs={{4,0},{16,20},{20,16},{24,28},{28,24},{5,1},{17,21},{21,17},{25,29... | collective-permute-start | bytes 786440 | tf_op jit(solution)/shard_map/ppermute | solution.py:55
  24.0 0.1 copy.12
  24.1 0.7 reshape.322.blocks_ref
  25.4 1.9 %collective-permute-done.6.refs_8_ = bf16[1,8,128,128]{3,2,1,0:T(8,128)(2,1)S(1)} collective-permute-done((bf16[1,8,128,128]{3,2,1,0:T(8,128)(2,1)S(1)}, bf16[1,8,128,128]{3,2,1,0:T(8,128)(2,1)S(1)}, u32[]{:S(2)}, u32[]{:S(2)}) %collective-permute-start.6) | collective-permute-done | bytes 262176 | tf_op jit(solution)/shard_map/ppermute | solution.py:55
  27.3 6.6 %collective-permute-done.2.refs_2_ = bf16[1,2,8,128,128]{4,3,2,1,0:T(8,128)(2,1)S(1)} collective-permute-done((bf16[1,2,8,128,128]{4,3,2,1,0:T(8,128)(2,1)S(1)}, bf16[1,2,8,128,128]{4,3,2,1,0:T(8,128)(2,1)S(1)}, u32[]{:S(2)}, u32[]{:S(2)}) %collective-permute-start.2) | collective-permute-done | bytes 524320 | tf_op jit(solution)/shard_map/ppermute | solution.py:55
  33.9 0.8 copy-done.9
  34.7 27.5 %attend.1 = (bf16[1,256,4096]{2,1,0:T(8,128)(2,1)}, f32[1,4096]{1,0:T(1,128)}, f32[1,2,2,4,128,128]{5,4,3,2,1,0:T(8,128)}, bf16[1,2,2,4,128,128]{5,4,3,2,1,0:T(8...) custom-call(s32[1]{0:T(128)} %bitcast.rank_ref, ...), custom_call_target="tpu_custom_call" | custom-call | tf_op jit(solution)/shard_map/attend/pallas_call | solution.py:274
  62.2 0.7 collective-permute-start.7
  62.9 5.4 %collective-permute-start.8 = (bf16[1,2,2,4,128,128]{5,4,3,2,1,0:T(8,128)(2,1)}, bf16[1,2,2,4,128,128]{5,4,3,2,1,0:T(8,128)(2,1)S(1)}, u32[]{:S(2)}, u32[]{:S(2)}) collective-permute-start(bf16[1,2,2,4,128,128]{5,4,3,2,1,0:T(8,128)(2,1)} %get-tuple-element.29), channel_id=1, source_target_pairs={{8,0},{12,4},{24,16},{28,20},{0,8},{4,12},{16,24},{20,28},{9,1},{1... | collective-permute-start | bytes 1572872 | tf_op jit(solution)/shard_map/ppermute | solution.py:59
  68.2 1.3 %collective-permute-start.9 = (bf16[1,2,4,128,128]{4,3,2,1,0:T(8,128)(2,1)}, bf16[1,2,4,128,128]{4,3,2,1,0:T(8,128)(2,1)S(1)}, u32[]{:S(2)}, u32[]{:S(2)}) collective-permute-start(bf16[1,2,4,128,128]{4,3,2,1,0:T(8,128)(2,1)} %get-tuple-element.30), channel_id=1, source_target_pairs={{0,4},{20,16},{16,20},{28,24},{24,28},{1,5},{21,17},{17,21},{29,25... | collective-permute-start | bytes 786440 | tf_op jit(solution)/shard_map/ppermute | solution.py:59
  69.5 2.2 %collective-permute-start.14 = (f32[4096]{0:T(1024)}, f32[4096]{0:T(1024)S(1)}, u32[]{:S(2)}, u32[]{:S(2)}) collective-permute-start(f32[4096]{0:T(1024)} %bitcast.76), channel_id=1, source_target_pairs={{0,4},{4,0},{8,12},{12,8},{16,20},{20,16},{24,28},{28,24},{1,5},{5... | collective-permute-start | bytes 49160 | tf_op jit(solution)/shard_map/ppermute | solution.py:308
  71.7 5.9 %collective-permute-done.14 = f32[4096]{0:T(1024)S(1)} collective-permute-done((f32[4096]{0:T(1024)}, f32[4096]{0:T(1024)S(1)}, u32[]{:S(2)}, u32[]{:S(2)}) %collective-permute-start.14) | collective-permute-done | bytes 16416 | tf_op jit(solution)/shard_map/ppermute | solution.py:308
  77.6 0.7 add.104
  78.3 0.3 collective-permute-start.16
  78.6 3.3 %collective-permute-start.17 = (f32[4096]{0:T(1024)S(1)}, f32[4096]{0:T(1024)S(1)}, u32[]{:S(2)}, u32[]{:S(2)}) collective-permute-start(f32[4096]{0:T(1024)S(1)} %add.104), channel_id=1, source_target_pairs={{0,24},{4,28},{8,16},{12,20},{16,8},{20,12},{24,0},{28,4},{1,25},{... | collective-permute-start | bytes 49160 | tf_op jit(solution)/shard_map/ppermute | solution.py:308
  81.9 2.1 %fusion.6 = (bf16[1,2,4,128,128]{4,3,2,1,0:T(8,128)(2,1)}, bf16[1,2,4,128,128]{4,3,2,1,0:T(8,128)(2,1)}) fusion(bf16[1,2,4,128,128]{4,3,2,1,0:T(8,128)(2,1)S(1)} %collective-permute-done.9, bf16[1,2,4,128,128]{4,3,2,1,0:T(8,128)(2,1)} %get-tuple-element.33, pred[]{:T(512)S(6)} %and.14, pred[]{:T(512)S(6)} %ge.7, ...), kind=kLoop, calls=%fused_computation.23 | loop fusion | flops 1179648 | bytes 1310722 | tf_op jit(solution)/shard_map/convert_element_type | solution.py:407
  83.9 1.3 %collective-permute-start.12 = (bf16[1,2,4,128,128]{4,3,2,1,0:T(8,128)(2,1)}, bf16[1,2,4,128,128]{4,3,2,1,0:T(8,128)(2,1)}, u32[]{:S(2)}, u32[]{:S(2)}) collective-permute-start(bf16[1,2,4,128,128]{4,3,2,1,0:T(8,128)(2,1)} %get-tuple-element.58), channel_id=1, source_target_pairs={{16,0},{20,4},{24,28},{17,1},{21,5},{25,29},{18,2},{22,6},{26,30},... | collective-permute-start | bytes 786440 | tf_op jit(solution)/shard_map/ppermute | solution.py:59
  85.2 0.8 copy-done.8
  86.0 1.4 %collective-permute-start.13 = (bf16[1,2,4,128,128]{4,3,2,1,0:T(8,128)(2,1)}, bf16[1,2,4,128,128]{4,3,2,1,0:T(8,128)(2,1)}, u32[]{:S(2)}, u32[]{:S(2)}) collective-permute-start(bf16[1,2,4,128,128]{4,3,2,1,0:T(8,128)(2,1)} %get-tuple-element.59), channel_id=1, source_target_pairs={{24,0},{28,4},{25,1},{29,5},{26,2},{30,6},{27,3},{31,7}} | collective-permute-start | bytes 786440 | tf_op jit(solution)/shard_map/ppermute | solution.py:59
  87.5 1.3 %select_convert_fusion = (f32[1,2,2,4,128,128]{5,4,3,2,1,0:T(8,128)S(1)}, f32[1,2,2,4,128,128]{5,4,3,2,1,0:T(8,128)S(1)}) fusion(bf16[1,2,2,4,128,128]{5,4,3,2,1,0:T(8,128)(2,1)} %copy-done.8, bf16[1,2,2,4,128,128]{5,4,3,2,1,0:T(8,128)(2,1)} %copy-done.7, pred[]{:T(512)S(6)} %ne.10), kind=kLoop, calls=%fused_computation.40 | loop fusion | flops 1048576 | bytes 3145729 | tf_op jit(solution)/shard_map/convert_element_type | solution.py:390
  88.8 0.9 fusion.14
  89.8 2.3 %collective-permute-start.11 = (bf16[1,2,4,128,128]{4,3,2,1,0:T(8,128)(2,1)}, bf16[1,2,4,128,128]{4,3,2,1,0:T(8,128)(2,1)}, u32[]{:S(2)}, u32[]{:S(2)}) collective-permute-start(bf16[1,2,4,128,128]{4,3,2,1,0:T(8,128)(2,1)} %get-tuple-element.38), channel_id=1, source_target_pairs={{8,4},{16,12},{24,20},{4,8},{12,16},{20,24},{9,5},{17,13},{25,21},... | collective-permute-start | bytes 786440 | tf_op jit(solution)/shard_map/ppermute | solution.py:59
  92.1 3.0 %collective-permute-start.18 = (f32[4096]{0:T(1024)S(1)}, f32[4096]{0:T(1024)S(1)}, u32[]{:S(2)}, u32[]{:S(2)}) collective-permute-start(f32[4096]{0:T(1024)S(1)} %add_add_fusion), channel_id=1, source_target_pairs={{0,1},{1,0},{2,3},{3,2},{4,5},{5,4},{6,7},{7,6},{8,9},{9,8},{10,11... | collective-permute-start | bytes 49160 | tf_op jit(solution)/shard_map/ppermute | solution.py:308
  95.2 0.8 collective-permute-done.18
  96.0 1.2 %collective-permute-start.19 = (f32[4096]{0:T(1024)S(1)}, f32[4096]{0:T(1024)S(1)}, u32[]{:S(2)}, u32[]{:S(2)}) collective-permute-start(f32[4096]{0:T(1024)S(1)} %add.108), channel_id=1, source_target_pairs={{0,2},{1,3},{2,0},{3,1},{4,6},{5,7},{6,4},{7,5},{8,10},{9,11},{10,... | collective-permute-start | bytes 49160 | tf_op jit(solution)/shard_map/ppermute | solution.py:308
  97.2 1.8 %collective-permute-done.19 = f32[4096]{0:T(1024)S(1)} collective-permute-done((f32[4096]{0:T(1024)S(1)}, f32[4096]{0:T(1024)S(1)}, u32[]{:S(2)}, u32[]{:S(2)}) %collective-permute-start.19) | collective-permute-done | bytes 16416 | tf_op jit(solution)/shard_map/ppermute | solution.py:308
  99.0 0.6 add_multiply_fusion
  99.6 6.1 %collective-permute-done.11 = bf16[1,2,4,128,128]{4,3,2,1,0:T(8,128)(2,1)} collective-permute-done((bf16[1,2,4,128,128]{4,3,2,1,0:T(8,128)(2,1)}, bf16[1,2,4,128,128]{4,3,2,1,0:T(8,128)(2,1)}, u32[]{:S(2)}, u32[]{:S(2)}) %collective-permute-start.11) | collective-permute-done | bytes 262176 | tf_op jit(solution)/shard_map/ppermute | solution.py:59
  105.7 1.5 %fusion.16 = (bf16[1,1,2,4,128,128]{5,4,3,2,1,0:T(8,128)(2,1)S(1)}, bf16[1,1,2,4,128,128]{5,4,3,2,1,0:T(8,128)(2,1)S(1)}) fusion(f32[1,2,2,4,128,128]{5,4,3,2,1,0:T(8,128)S(1)} %get-tuple-element.40, f32[1,2,2,4,128,128]{5,4,3,2,1,0:T(8,128)S(1)} %copy-done.2, bf16[1,2,4,128,128]{4,3,2,1,0:T(8,128)(2,1)} %collective-permute-done.11, ...), kind=kLoop, calls=%fused_computation.44 | loop fusion | flops 2490368 | bytes 4456451 | tf_op jit(solution)/shard_map/stack | solution.py:415
  107.3 0.7 pad_maximum_fusion.3
  108.1 0.7 pad_maximum_fusion.2
  (42 shorter events, 0.3 us)
Async XLA Ops:
  2.0 13.1 %copy-start.1 = (bf16[1,8,128,128]{3,2,1,0:T(8,128)(2,1)}, bf16[1,8,128,128]{3,2,1,0:T(8,128)(2,1)S(1)}, u32[]{:S(2)}) copy-start(bf16[1,8,128,128]{3,2,1,0:T(8,128)(2,1)S(1)} %get-tuple-element.21.refs_1_) | copy-start | bytes 786436
  2.0 20.7 %copy-start = (bf16[1,8,128,128]{3,2,1,0:T(8,128)(2,1)}, bf16[1,8,128,128]{3,2,1,0:T(8,128)(2,1)S(1)}, u32[]{:S(2)}) copy-start(bf16[1,8,128,128]{3,2,1,0:T(8,128)(2,1)S(1)} %get-tuple-element.20.refs_0_) | copy-start | bytes 786436
  2.1 12.9 %collective-permute-start = (bf16[1,8,128,128]{3,2,1,0:T(8,128)(2,1)S(1)}, bf16[1,8,128,128]{3,2,1,0:T(8,128)(2,1)S(1)}, u32[]{:S(2)}, u32[]{:S(2)}) collective-permute-start(bf16[1,8,128,128]{3,2,1,0:T(8,128)(2,1)S(1)} %get-tuple-element.22), channel_id=1, source_target_pairs={{0,4},{8,12},{16,20},{24,28},{4,0},{12,8},{20,16},{28,24},{1,5},{9... | collective-permute-start | bytes 786440 | tf_op jit(solution)/shard_map/ppermute | solution.py:55
  2.2 12.8 %collective-permute-start.1 = (bf16[1,8,128,128]{3,2,1,0:T(8,128)(2,1)S(1)}, bf16[1,8,128,128]{3,2,1,0:T(8,128)(2,1)S(1)}, u32[]{:S(2)}, u32[]{:S(2)}) collective-permute-start(bf16[1,8,128,128]{3,2,1,0:T(8,128)(2,1)S(1)} %get-tuple-element.23), channel_id=1, source_target_pairs={{4,8},{12,16},{20,24},{8,4},{16,12},{24,20},{5,9},{13,17},{21,25},... | collective-permute-start | bytes 786440 | tf_op jit(solution)/shard_map/ppermute | solution.py:55
  6.5 11.4 %collective-permute-start.4 = (bf16[1,8,128,128]{3,2,1,0:T(8,128)(2,1)S(1)}, bf16[1,8,128,128]{3,2,1,0:T(8,128)(2,1)S(1)}, u32[]{:S(2)}, u32[]{:S(2)}) collective-permute-start(bf16[1,8,128,128]{3,2,1,0:T(8,128)(2,1)S(1)} %get-tuple-element.20.refs_0_), channel_id=1, source_target_pairs={{0,16},{4,20},{28,24},{1,17},{5,21},{29,25},{2,18},{6,22},{30,26},... | collective-permute-start | bytes 786440 | tf_op jit(solution)/shard_map/ppermute | solution.py:55
  10.8 11.9 %collective-permute-start.5 = (bf16[1,8,128,128]{3,2,1,0:T(8,128)(2,1)S(1)}, bf16[1,8,128,128]{3,2,1,0:T(8,128)(2,1)S(1)}, u32[]{:S(2)}, u32[]{:S(2)}) collective-permute-start(bf16[1,8,128,128]{3,2,1,0:T(8,128)(2,1)S(1)} %get-tuple-element.20.refs_0_), channel_id=1, source_target_pairs={{0,24},{4,28},{1,25},{5,29},{2,26},{6,30},{3,27},{7,31}} | collective-permute-start | bytes 786440 | tf_op jit(solution)/shard_map/ppermute | solution.py:55
  12.8 11.2 %copy-start.13 = (s32[1,16,6]{1,0,2:T(1,128)S(1)}, s32[1,16,6]{1,0,2:T(1,128)}, u32[]{:S(2)}) copy-start(s32[1,16,6]{1,0,2:T(1,128)} %param.12) | copy-start | bytes 1156
  15.0 7.7 %copy-start.5 = (bf16[1,8,128,128]{3,2,1,0:T(8,128)(2,1)}, bf16[1,8,128,128]{3,2,1,0:T(8,128)(2,1)S(1)}, u32[]{:S(2)}) copy-start(bf16[1,8,128,128]{3,2,1,0:T(8,128)(2,1)S(1)} %collective-permute-done.refs_4_) | copy-start | bytes 786436
  15.0 7.7 %copy-start.6 = (bf16[1,8,128,128]{3,2,1,0:T(8,128)(2,1)}, bf16[1,8,128,128]{3,2,1,0:T(8,128)(2,1)S(1)}, u32[]{:S(2)}) copy-start(bf16[1,8,128,128]{3,2,1,0:T(8,128)(2,1)S(1)} %collective-permute-done.1.refs_5_) | copy-start | bytes 786436
  15.1 18.7 %collective-permute-start.2 = (bf16[1,2,8,128,128]{4,3,2,1,0:T(8,128)(2,1)S(1)}, bf16[1,2,8,128,128]{4,3,2,1,0:T(8,128)(2,1)S(1)}, u32[]{:S(2)}, u32[]{:S(2)}) collective-permute-start(bf16[1,2,8,128,128]{4,3,2,1,0:T(8,128)(2,1)S(1)} %get-tuple-element.24), channel_id=1, source_target_pairs={{0,8},{4,12},{16,24},{20,28},{8,0},{12,4},{24,16},{28,20},{1,9},{5... | collective-permute-start | bytes 1572872 | tf_op jit(solution)/shard_map/ppermute | solution.py:55
  16.5 17.4 %collective-permute-start.3 = (bf16[1,2,8,128,128]{4,3,2,1,0:T(8,128)(2,1)S(1)}, bf16[1,2,8,128,128]{4,3,2,1,0:T(8,128)(2,1)}, u32[]{:S(2)}, u32[]{:S(2)}) collective-permute-start(bf16[1,2,8,128,128]{4,3,2,1,0:T(8,128)(2,1)S(1)} %get-tuple-element.25), channel_id=1, source_target_pairs={{8,16},{12,20},{16,8},{20,12},{9,17},{13,21},{17,9},{21,13},{10,18... | collective-permute-start | bytes 1572872 | tf_op jit(solution)/shard_map/ppermute | solution.py:55
  18.0 15.9 %copy-start.3 = (bf16[1,8,128,128]{3,2,1,0:T(8,128)(2,1)}, bf16[1,8,128,128]{3,2,1,0:T(8,128)(2,1)S(1)}, u32[]{:S(2)}) copy-start(bf16[1,8,128,128]{3,2,1,0:T(8,128)(2,1)S(1)} %collective-permute-done.4.refs_6_) | copy-start | bytes 786436
  22.6 11.2 %copy-start.4 = (bf16[1,8,128,128]{3,2,1,0:T(8,128)(2,1)}, bf16[1,8,128,128]{3,2,1,0:T(8,128)(2,1)S(1)}, u32[]{:S(2)}) copy-start(bf16[1,8,128,128]{3,2,1,0:T(8,128)(2,1)S(1)} %collective-permute-done.5.refs_7_) | copy-start | bytes 786436
  22.7 4.6 %collective-permute-start.6 = (bf16[1,8,128,128]{3,2,1,0:T(8,128)(2,1)S(1)}, bf16[1,8,128,128]{3,2,1,0:T(8,128)(2,1)S(1)}, u32[]{:S(2)}, u32[]{:S(2)}) collective-permute-start(bf16[1,8,128,128]{3,2,1,0:T(8,128)(2,1)S(1)} %select_select_fusion), channel_id=1, source_target_pairs={{4,0},{16,20},{20,16},{24,28},{28,24},{5,1},{17,21},{21,17},{25,29... | collective-permute-start | bytes 786440 | tf_op jit(solution)/shard_map/ppermute | solution.py:55
  27.3 6.6 %copy-start.12 = (bf16[1,8,128,128]{3,2,1,0:T(8,128)(2,1)}, bf16[1,8,128,128]{3,2,1,0:T(8,128)(2,1)S(1)}, u32[]{:S(2)}) copy-start(bf16[1,8,128,128]{3,2,1,0:T(8,128)(2,1)S(1)} %collective-permute-done.6.refs_8_) | copy-start | bytes 786436
  33.9 0.8 copy-start.9
  62.2 21.7 %collective-permute-start.7 = (bf16[1,2,2,4,128,128]{5,4,3,2,1,0:T(8,128)(2,1)}, bf16[1,2,2,4,128,128]{5,4,3,2,1,0:T(8,128)(2,1)S(1)}, u32[]{:S(2)}, u32[]{:S(2)}) collective-permute-start(bf16[1,2,2,4,128,128]{5,4,3,2,1,0:T(8,128)(2,1)} %get-tuple-element.28), channel_id=1, source_target_pairs={{16,8},{20,12},{8,16},{12,20},{17,9},{21,13},{9,17},{13,21},{18,10... | collective-permute-start | bytes 1572872 | tf_op jit(solution)/shard_map/ppermute | solution.py:59
  62.9 22.3 %collective-permute-start.8 = (bf16[1,2,2,4,128,128]{5,4,3,2,1,0:T(8,128)(2,1)}, bf16[1,2,2,4,128,128]{5,4,3,2,1,0:T(8,128)(2,1)S(1)}, u32[]{:S(2)}, u32[]{:S(2)}) collective-permute-start(bf16[1,2,2,4,128,128]{5,4,3,2,1,0:T(8,128)(2,1)} %get-tuple-element.29), channel_id=1, source_target_pairs={{8,0},{12,4},{24,16},{28,20},{0,8},{4,12},{16,24},{20,28},{9,1},{1... | collective-permute-start | bytes 1572872 | tf_op jit(solution)/shard_map/ppermute | solution.py:59
  68.2 10.3 %collective-permute-start.9 = (bf16[1,2,4,128,128]{4,3,2,1,0:T(8,128)(2,1)}, bf16[1,2,4,128,128]{4,3,2,1,0:T(8,128)(2,1)S(1)}, u32[]{:S(2)}, u32[]{:S(2)}) collective-permute-start(bf16[1,2,4,128,128]{4,3,2,1,0:T(8,128)(2,1)} %get-tuple-element.30), channel_id=1, source_target_pairs={{0,4},{20,16},{16,20},{28,24},{24,28},{1,5},{21,17},{17,21},{29,25... | collective-permute-start | bytes 786440 | tf_op jit(solution)/shard_map/ppermute | solution.py:59
  69.5 8.0 %collective-permute-start.14 = (f32[4096]{0:T(1024)}, f32[4096]{0:T(1024)S(1)}, u32[]{:S(2)}, u32[]{:S(2)}) collective-permute-start(f32[4096]{0:T(1024)} %bitcast.76), channel_id=1, source_target_pairs={{0,4},{4,0},{8,12},{12,8},{16,20},{20,16},{24,28},{28,24},{1,5},{5... | collective-permute-start | bytes 49160 | tf_op jit(solution)/shard_map/ppermute | solution.py:308
  78.3 11.5 %collective-permute-start.15 = (f32[4096]{0:T(1024)S(1)}, f32[4096]{0:T(1024)S(1)}, u32[]{:S(2)}, u32[]{:S(2)}) collective-permute-start(f32[4096]{0:T(1024)S(1)} %add.104), channel_id=1, source_target_pairs={{0,8},{4,12},{8,0},{12,4},{16,24},{20,28},{24,16},{28,20},{1,9},{5... | collective-permute-start | bytes 49160 | tf_op jit(solution)/shard_map/ppermute | solution.py:308
  78.3 11.5 %collective-permute-start.16 = (f32[4096]{0:T(1024)S(1)}, f32[4096]{0:T(1024)S(1)}, u32[]{:S(2)}, u32[]{:S(2)}) collective-permute-start(f32[4096]{0:T(1024)S(1)} %add.104), channel_id=1, source_target_pairs={{0,16},{4,20},{8,24},{12,28},{16,0},{20,4},{24,8},{28,12},{1,17},{... | collective-permute-start | bytes 49160 | tf_op jit(solution)/shard_map/ppermute | solution.py:308
  78.6 13.5 %collective-permute-start.17 = (f32[4096]{0:T(1024)S(1)}, f32[4096]{0:T(1024)S(1)}, u32[]{:S(2)}, u32[]{:S(2)}) collective-permute-start(f32[4096]{0:T(1024)S(1)} %add.104), channel_id=1, source_target_pairs={{0,24},{4,28},{8,16},{12,20},{16,8},{20,12},{24,0},{28,4},{1,25},{... | collective-permute-start | bytes 49160 | tf_op jit(solution)/shard_map/ppermute | solution.py:308
  81.8 7.0 %copy-start.10 = (bf16[1,2,4,128,128]{4,3,2,1,0:T(8,128)(2,1)S(1)}, bf16[1,2,4,128,128]{4,3,2,1,0:T(8,128)(2,1)}, u32[]{:S(2)}) copy-start(bf16[1,2,4,128,128]{4,3,2,1,0:T(8,128)(2,1)} %get-tuple-element.31) | copy-start | bytes 786436
  81.8 7.0 %copy-start.11 = (bf16[1,2,4,128,128]{4,3,2,1,0:T(8,128)(2,1)S(1)}, bf16[1,2,4,128,128]{4,3,2,1,0:T(8,128)(2,1)}, u32[]{:S(2)}) copy-start(bf16[1,2,4,128,128]{4,3,2,1,0:T(8,128)(2,1)} %get-tuple-element.32) | copy-start | bytes 786436
  83.9 1.3 %copy-start.7 = (bf16[1,2,2,4,128,128]{5,4,3,2,1,0:T(8,128)(2,1)}, bf16[1,2,2,4,128,128]{5,4,3,2,1,0:T(8,128)(2,1)S(1)}, u32[]{:S(2)}) copy-start(bf16[1,2,2,4,128,128]{5,4,3,2,1,0:T(8,128)(2,1)S(1)} %collective-permute-done.7) | copy-start | bytes 1572868
  83.9 15.7 %collective-permute-start.12 = (bf16[1,2,4,128,128]{4,3,2,1,0:T(8,128)(2,1)}, bf16[1,2,4,128,128]{4,3,2,1,0:T(8,128)(2,1)}, u32[]{:S(2)}, u32[]{:S(2)}) collective-permute-start(bf16[1,2,4,128,128]{4,3,2,1,0:T(8,128)(2,1)} %get-tuple-element.58), channel_id=1, source_target_pairs={{16,0},{20,4},{24,28},{17,1},{21,5},{25,29},{18,2},{22,6},{26,30},... | collective-permute-start | bytes 786440 | tf_op jit(solution)/shard_map/ppermute | solution.py:59
  85.2 0.8 copy-start.8
  86.0 19.7 %copy-start.2 = (f32[1,2,2,4,128,128]{5,4,3,2,1,0:T(8,128)S(1)}, f32[1,2,2,4,128,128]{5,4,3,2,1,0:T(8,128)}, u32[]{:S(2)}) copy-start(f32[1,2,2,4,128,128]{5,4,3,2,1,0:T(8,128)} %get-tuple-element.27) | copy-start | bytes 3145732
  86.0 13.6 %collective-permute-start.13 = (bf16[1,2,4,128,128]{4,3,2,1,0:T(8,128)(2,1)}, bf16[1,2,4,128,128]{4,3,2,1,0:T(8,128)(2,1)}, u32[]{:S(2)}, u32[]{:S(2)}) collective-permute-start(bf16[1,2,4,128,128]{4,3,2,1,0:T(8,128)(2,1)} %get-tuple-element.59), channel_id=1, source_target_pairs={{24,0},{28,4},{25,1},{29,5},{26,2},{30,6},{27,3},{31,7}} | collective-permute-start | bytes 786440 | tf_op jit(solution)/shard_map/ppermute | solution.py:59
  89.8 9.8 %collective-permute-start.10 = (bf16[1,2,4,128,128]{4,3,2,1,0:T(8,128)(2,1)}, bf16[1,2,4,128,128]{4,3,2,1,0:T(8,128)(2,1)}, u32[]{:S(2)}, u32[]{:S(2)}) collective-permute-start(bf16[1,2,4,128,128]{4,3,2,1,0:T(8,128)(2,1)} %get-tuple-element.39), channel_id=1, source_target_pairs={{4,0},{12,8},{20,16},{28,24},{0,4},{8,12},{16,20},{24,28},{5,1},{1... | collective-permute-start | bytes 786440 | tf_op jit(solution)/shard_map/ppermute | solution.py:59
  89.8 15.9 %collective-permute-start.11 = (bf16[1,2,4,128,128]{4,3,2,1,0:T(8,128)(2,1)}, bf16[1,2,4,128,128]{4,3,2,1,0:T(8,128)(2,1)}, u32[]{:S(2)}, u32[]{:S(2)}) collective-permute-start(bf16[1,2,4,128,128]{4,3,2,1,0:T(8,128)(2,1)} %get-tuple-element.38), channel_id=1, source_target_pairs={{8,4},{16,12},{24,20},{4,8},{12,16},{20,24},{9,5},{17,13},{25,21},... | collective-permute-start | bytes 786440 | tf_op jit(solution)/shard_map/ppermute | solution.py:59
  92.1 3.9 %collective-permute-start.18 = (f32[4096]{0:T(1024)S(1)}, f32[4096]{0:T(1024)S(1)}, u32[]{:S(2)}, u32[]{:S(2)}) collective-permute-start(f32[4096]{0:T(1024)S(1)} %add_add_fusion), channel_id=1, source_target_pairs={{0,1},{1,0},{2,3},{3,2},{4,5},{5,4},{6,7},{7,6},{8,9},{9,8},{10,11... | collective-permute-start | bytes 49160 | tf_op jit(solution)/shard_map/ppermute | solution.py:308
  96.0 3.0 %collective-permute-start.19 = (f32[4096]{0:T(1024)S(1)}, f32[4096]{0:T(1024)S(1)}, u32[]{:S(2)}, u32[]{:S(2)}) collective-permute-start(f32[4096]{0:T(1024)S(1)} %add.108), channel_id=1, source_target_pairs={{0,2},{1,3},{2,0},{3,1},{4,6},{5,7},{6,4},{7,5},{8,10},{9,11},{10,... | collective-permute-start | bytes 49160 | tf_op jit(solution)/shard_map/ppermute | solution.py:308

commit v5 on v4

--- a/solution.py
+++ b/solution.py
@@ -237,9 +237,9 @@
         if task > 0:
             query_grad(task - 1)
             if task % 2 == 0:
-                key_grad(task - 1, 2, (0,))
+                key_grad(task - 1, 2, (1,))
             elif task > 1:
-                key_grad(task - 2, 2, (1,))
+                key_grad(task - 2, 2, (0,))
         softmax(task)
     query_grad(tasks - 1)
     key_grad(tasks - 1, 2)
@@ -419,7 +419,11 @@
         )
         for i in range(2)
     )
-    bias_total = butterfly(butterfly(quad(butterfly(dbias.reshape(-1), "ctx", 1, 2), "ctx", 2), "ctx", 8), "dp")
+    bias_sum = butterfly(quad(butterfly(dbias.reshape(-1), "ctx", 1, 2), "ctx", 2), "ctx", 8)
+    if lax.axis_size("dp") == 4:
+        bias_total = quad(bias_sum, "dp", 1)
+    else:
+        bias_total = butterfly(bias_sum, "dp")
     rows = traces * lax.axis_size("dp") * 2 * BLOCK * n
     return dq, grad_key, grad_value, bias_total / math.sqrt(rows)
 

time: 109 us -> 116 us (1.064)
  waiting for transfers between devices: 29.8 us -> 37.1 us
    ppermute x6 -> x7, waiting for transfers between devices: 8.48 us -> 15.2 us  [swapped(): return lax.ppermute(value, axis, pairs)]
    ppermute x6 -> x7, starting transfers between devices: 9.97 us -> 9.39 us  [swapped(): return lax.ppermute(value, axis, pairs)]
  transfers between devices with their start and end apart: 20 -> 21, of which waited for: 8 -> 9; matrix products, arithmetic and copies ran while one was open for 6% -> 6% of each run, Pallas kernels for 0% -> 0%
where the time goes in v5:
time: 116 us
  starting transfers between devices  37.6 us (32%)
  waiting for transfers between devices  37.1 us (32%)
  Pallas kernels  26.8 us (23%)
  other arithmetic  10.1 us (9%)
  local copies, waits for them, and re-layouts  2.63 us (2%)
  between operations  1.61 us (1%)
    pallas_call x1, Pallas kernels, attend(): pl.pallas_call(functools.partial(attend_kernel, n, nbuf, heads, group), o...  26.8 us
    ppermute x7, waiting for transfers between devices, swapped(): return lax.ppermute(value, axis, pairs)  15.2 us
    ppermute x7, waiting for transfers between devices, send(): return lax.ppermute(value, 'ctx', pairs)  15.2 us
    ppermute x7, starting transfers between devices, send(): return lax.ppermute(value, 'ctx', pairs)  14.9 us
    ppermute x7, starting transfers between devices, send_back(): return lax.ppermute(value, 'ctx', [(b, a) for a, b in pairs])  13.4 us
    ppermute x7, starting transfers between devices, swapped(): return lax.ppermute(value, axis, pairs)  9.39 us
    ppermute x7, waiting for transfers between devices, send_back(): return lax.ppermute(value, 'ctx', [(b, a) for a, b in pairs])  6.72 us
  transfers between devices with their start and end apart: 21, of which 9 were waited for; matrix products, arithmetic and copies ran while one was open for 6% of the time, Pallas kernels for 0%

profile of v5, /device:TPU:3, one launch (start us, length us, event | category | flops | bytes accessed | tf_op | source)
XLA Modules:
  0.0 116.0 jit_solution(12465749190296295652)
XLA Ops:
  0.6 1.1 maximum_bitcast_fusion
  1.7 0.1 copy.17
  1.9 0.1 copy_bitcast_fusion
  2.0 0.0 copy-start.1
  2.0 0.0 copy-start
  2.0 0.1 broadcast_select_fusion.2
  2.1 0.1 collective-permute-start
  2.2 4.4 %collective-permute-start.1 = (bf16[1,8,128,128]{3,2,1,0:T(8,128)(2,1)S(1)}, bf16[1,8,128,128]{3,2,1,0:T(8,128)(2,1)S(1)}, u32[]{:S(2)}, u32[]{:S(2)}) collective-permute-start(bf16[1,8,128,128]{3,2,1,0:T(8,128)(2,1)S(1)} %get-tuple-element.23), channel_id=1, source_target_pairs={{4,8},{12,16},{20,24},{8,4},{16,12},{24,20},{5,9},{13,17},{21,25},... | collective-permute-start | bytes 786440 | tf_op jit(solution)/shard_map/ppermute | solution.py:55
  6.5 4.2 %collective-permute-start.4 = (bf16[1,8,128,128]{3,2,1,0:T(8,128)(2,1)S(1)}, bf16[1,8,128,128]{3,2,1,0:T(8,128)(2,1)S(1)}, u32[]{:S(2)}, u32[]{:S(2)}) collective-permute-start(bf16[1,8,128,128]{3,2,1,0:T(8,128)(2,1)S(1)} %get-tuple-element.20.refs_0_), channel_id=1, source_target_pairs={{0,16},{4,20},{28,24},{1,17},{5,21},{29,25},{2,18},{6,22},{30,26},... | collective-permute-start | bytes 786440 | tf_op jit(solution)/shard_map/ppermute | solution.py:55
  10.8 2.1 %collective-permute-start.5 = (bf16[1,8,128,128]{3,2,1,0:T(8,128)(2,1)S(1)}, bf16[1,8,128,128]{3,2,1,0:T(8,128)(2,1)S(1)}, u32[]{:S(2)}, u32[]{:S(2)}) collective-permute-start(bf16[1,8,128,128]{3,2,1,0:T(8,128)(2,1)S(1)} %get-tuple-element.20.refs_0_), channel_id=1, source_target_pairs={{0,24},{4,28},{1,25},{5,29},{2,26},{6,30},{3,27},{7,31}} | collective-permute-start | bytes 786440 | tf_op jit(solution)/shard_map/ppermute | solution.py:55
  12.9 2.1 %collective-permute-done.refs_4_ = bf16[1,8,128,128]{3,2,1,0:T(8,128)(2,1)S(1)} collective-permute-done((bf16[1,8,128,128]{3,2,1,0:T(8,128)(2,1)S(1)}, bf16[1,8,128,128]{3,2,1,0:T(8,128)(2,1)S(1)}, u32[]{:S(2)}, u32[]{:S(2)}) %collective-permute-start) | collective-permute-done | bytes 262176 | tf_op jit(solution)/shard_map/ppermute | solution.py:55
  15.0 0.1 broadcast_select_fusion
  15.1 1.4 %collective-permute-start.2 = (bf16[1,2,8,128,128]{4,3,2,1,0:T(8,128)(2,1)S(1)}, bf16[1,2,8,128,128]{4,3,2,1,0:T(8,128)(2,1)S(1)}, u32[]{:S(2)}, u32[]{:S(2)}) collective-permute-start(bf16[1,2,8,128,128]{4,3,2,1,0:T(8,128)(2,1)S(1)} %get-tuple-element.24), channel_id=1, source_target_pairs={{0,8},{4,12},{16,24},{20,28},{8,0},{12,4},{24,16},{28,20},{1,9},{5... | collective-permute-start | bytes 1572872 | tf_op jit(solution)/shard_map/ppermute | solution.py:55
  16.5 1.5 %collective-permute-start.3 = (bf16[1,2,8,128,128]{4,3,2,1,0:T(8,128)(2,1)S(1)}, bf16[1,2,8,128,128]{4,3,2,1,0:T(8,128)(2,1)}, u32[]{:S(2)}, u32[]{:S(2)}) collective-permute-start(bf16[1,2,8,128,128]{4,3,2,1,0:T(8,128)(2,1)S(1)} %get-tuple-element.25), channel_id=1, source_target_pairs={{8,16},{12,20},{16,8},{20,12},{9,17},{13,21},{17,9},{21,13},{10,18... | collective-permute-start | bytes 1572872 | tf_op jit(solution)/shard_map/ppermute | solution.py:55
  18.0 4.7 %collective-permute-done.5.refs_7_ = bf16[1,8,128,128]{3,2,1,0:T(8,128)(2,1)S(1)} collective-permute-done((bf16[1,8,128,128]{3,2,1,0:T(8,128)(2,1)S(1)}, bf16[1,8,128,128]{3,2,1,0:T(8,128)(2,1)S(1)}, u32[]{:S(2)}, u32[]{:S(2)}) %collective-permute-start.5) | collective-permute-done | bytes 262176 | tf_op jit(solution)/shard_map/ppermute | solution.py:55
  22.7 1.3 %collective-permute-start.6 = (bf16[1,8,128,128]{3,2,1,0:T(8,128)(2,1)S(1)}, bf16[1,8,128,128]{3,2,1,0:T(8,128)(2,1)S(1)}, u32[]{:S(2)}, u32[]{:S(2)}) collective-permute-start(bf16[1,8,128,128]{3,2,1,0:T(8,128)(2,1)S(1)} %select_select_fusion), channel_id=1, source_target_pairs={{4,0},{16,20},{20,16},{24,28},{28,24},{5,1},{17,21},{21,17},{25,29... | collective-permute-start | bytes 786440 | tf_op jit(solution)/shard_map/ppermute | solution.py:55
  24.0 0.1 copy.12
  24.1 0.7 reshape.322.blocks_ref
  25.4 1.9 %collective-permute-done.6.refs_8_ = bf16[1,8,128,128]{3,2,1,0:T(8,128)(2,1)S(1)} collective-permute-done((bf16[1,8,128,128]{3,2,1,0:T(8,128)(2,1)S(1)}, bf16[1,8,128,128]{3,2,1,0:T(8,128)(2,1)S(1)}, u32[]{:S(2)}, u32[]{:S(2)}) %collective-permute-start.6) | collective-permute-done | bytes 262176 | tf_op jit(solution)/shard_map/ppermute | solution.py:55
  27.3 6.6 %collective-permute-done.2.refs_2_ = bf16[1,2,8,128,128]{4,3,2,1,0:T(8,128)(2,1)S(1)} collective-permute-done((bf16[1,2,8,128,128]{4,3,2,1,0:T(8,128)(2,1)S(1)}, bf16[1,2,8,128,128]{4,3,2,1,0:T(8,128)(2,1)S(1)}, u32[]{:S(2)}, u32[]{:S(2)}) %collective-permute-start.2) | collective-permute-done | bytes 524320 | tf_op jit(solution)/shard_map/ppermute | solution.py:55
  33.9 0.8 copy-done.8
  34.7 26.8 %attend.1 = (bf16[1,256,4096]{2,1,0:T(8,128)(2,1)}, f32[1,4096]{1,0:T(1,128)}, f32[1,2,2,4,128,128]{5,4,3,2,1,0:T(8,128)}, bf16[1,2,2,4,128,128]{5,4,3,2,1,0:T(8...) custom-call(s32[1]{0:T(128)} %bitcast.rank_ref, ...), custom_call_target="tpu_custom_call" | custom-call | tf_op jit(solution)/shard_map/attend/pallas_call | solution.py:274
  61.5 0.1 collective-permute-start.14
  61.6 0.7 collective-permute-start.7
  62.3 5.3 %collective-permute-start.8 = (bf16[1,2,2,4,128,128]{5,4,3,2,1,0:T(8,128)(2,1)}, bf16[1,2,2,4,128,128]{5,4,3,2,1,0:T(8,128)(2,1)}, u32[]{:S(2)}, u32[]{:S(2)}) collective-permute-start(bf16[1,2,2,4,128,128]{5,4,3,2,1,0:T(8,128)(2,1)} %get-tuple-element.29), channel_id=1, source_target_pairs={{8,0},{12,4},{24,16},{28,20},{0,8},{4,12},{16,24},{20,28},{9,1},{1... | collective-permute-start | bytes 1572872 | tf_op jit(solution)/shard_map/ppermute | solution.py:59
  67.7 1.3 %collective-permute-start.9 = (bf16[1,2,4,128,128]{4,3,2,1,0:T(8,128)(2,1)}, bf16[1,2,4,128,128]{4,3,2,1,0:T(8,128)(2,1)S(1)}, u32[]{:S(2)}, u32[]{:S(2)}) collective-permute-start(bf16[1,2,4,128,128]{4,3,2,1,0:T(8,128)(2,1)} %get-tuple-element.30), channel_id=1, source_target_pairs={{0,4},{20,16},{16,20},{28,24},{24,28},{1,5},{21,17},{17,21},{29,25... | collective-permute-start | bytes 786440 | tf_op jit(solution)/shard_map/ppermute | solution.py:59
  69.0 0.7 add.107
  69.7 3.2 %collective-permute-start.16 = (f32[4096]{0:T(1024)S(1)}, f32[4096]{0:T(1024)S(1)}, u32[]{:S(2)}, u32[]{:S(2)}) collective-permute-start(f32[4096]{0:T(1024)S(1)} %add.107), channel_id=1, source_target_pairs={{0,16},{4,20},{8,24},{12,28},{16,0},{20,4},{24,8},{28,12},{1,17},{... | collective-permute-start | bytes 49160 | tf_op jit(solution)/shard_map/ppermute | solution.py:308
  72.9 7.2 %collective-permute-done.15 = f32[4096]{0:T(1024)S(1)} collective-permute-done((f32[4096]{0:T(1024)S(1)}, f32[4096]{0:T(1024)S(1)}, u32[]{:S(2)}, u32[]{:S(2)}) %collective-permute-start.15) | collective-permute-done | bytes 16416 | tf_op jit(solution)/shard_map/ppermute | solution.py:308
  80.1 4.4 %collective-permute-done.17 = f32[4096]{0:T(1024)S(1)} collective-permute-done((f32[4096]{0:T(1024)S(1)}, f32[4096]{0:T(1024)S(1)}, u32[]{:S(2)}, u32[]{:S(2)}) %collective-permute-start.17) | collective-permute-done | bytes 16416 | tf_op jit(solution)/shard_map/ppermute | solution.py:308
  84.5 2.6 %collective-permute-start.18 = (f32[4096]{0:T(1024)S(1)}, f32[4096]{0:T(1024)S(1)}, u32[]{:S(2)}, u32[]{:S(2)}) collective-permute-start(f32[4096]{0:T(1024)S(1)} %add_add_fusion), channel_id=1, source_target_pairs={{0,1},{1,0},{2,3},{3,2},{4,5},{5,4},{6,7},{7,6},{8,9},{9,8},{10,11... | collective-permute-start | bytes 49160 | tf_op jit(solution)/shard_map/ppermute | solution.py:308
  87.1 2.1 %fusion.6 = (bf16[1,2,4,128,128]{4,3,2,1,0:T(8,128)(2,1)}, bf16[1,2,4,128,128]{4,3,2,1,0:T(8,128)(2,1)}) fusion(bf16[1,2,4,128,128]{4,3,2,1,0:T(8,128)(2,1)S(1)} %collective-permute-done.9, bf16[1,2,4,128,128]{4,3,2,1,0:T(8,128)(2,1)} %get-tuple-element.33, pred[]{:T(512)S(6)} %and.14, pred[]{:T(512)S(6)} %ge.7, ...), kind=kLoop, calls=%fused_computation.23 | loop fusion | flops 1179648 | bytes 1310722 | tf_op jit(solution)/shard_map/convert_element_type | solution.py:407
  89.1 1.3 %collective-permute-start.12 = (bf16[1,2,4,128,128]{4,3,2,1,0:T(8,128)(2,1)}, bf16[1,2,4,128,128]{4,3,2,1,0:T(8,128)(2,1)}, u32[]{:S(2)}, u32[]{:S(2)}) collective-permute-start(bf16[1,2,4,128,128]{4,3,2,1,0:T(8,128)(2,1)} %get-tuple-element.58), channel_id=1, source_target_pairs={{16,0},{20,4},{24,28},{17,1},{21,5},{25,29},{18,2},{22,6},{26,30},... | collective-permute-start | bytes 786440 | tf_op jit(solution)/shard_map/ppermute | solution.py:59
  90.4 1.4 %collective-permute-start.13 = (bf16[1,2,4,128,128]{4,3,2,1,0:T(8,128)(2,1)}, bf16[1,2,4,128,128]{4,3,2,1,0:T(8,128)(2,1)}, u32[]{:S(2)}, u32[]{:S(2)}) collective-permute-start(bf16[1,2,4,128,128]{4,3,2,1,0:T(8,128)(2,1)} %get-tuple-element.59), channel_id=1, source_target_pairs={{24,0},{28,4},{25,1},{29,5},{26,2},{30,6},{27,3},{31,7}} | collective-permute-start | bytes 786440 | tf_op jit(solution)/shard_map/ppermute | solution.py:59
  91.9 0.8 copy-done.7
  92.7 1.3 %select_convert_fusion = (f32[1,2,2,4,128,128]{5,4,3,2,1,0:T(8,128)S(1)}, f32[1,2,2,4,128,128]{5,4,3,2,1,0:T(8,128)S(1)}) fusion(bf16[1,2,2,4,128,128]{5,4,3,2,1,0:T(8,128)(2,1)} %collective-permute-done.8, bf16[1,2,2,4,128,128]{5,4,3,2,1,0:T(8,128)(2,1)} %copy-done.7, pred[]{:T(512)S(6)} %ne.10), kind=kLoop, calls=%fused_computation.40 | loop fusion | flops 1048576 | bytes 3145729 | tf_op jit(solution)/shard_map/convert_element_type | solution.py:390
  94.1 0.9 fusion.14
  95.0 1.4 %collective-permute-start.10 = (bf16[1,2,4,128,128]{4,3,2,1,0:T(8,128)(2,1)}, bf16[1,2,4,128,128]{4,3,2,1,0:T(8,128)(2,1)}, u32[]{:S(2)}, u32[]{:S(2)}) collective-permute-start(bf16[1,2,4,128,128]{4,3,2,1,0:T(8,128)(2,1)} %get-tuple-element.39), channel_id=1, source_target_pairs={{4,0},{12,8},{20,16},{28,24},{0,4},{8,12},{16,20},{24,28},{5,1},{1... | collective-permute-start | bytes 786440 | tf_op jit(solution)/shard_map/ppermute | solution.py:59
  96.4 1.9 %collective-permute-start.11 = (bf16[1,2,4,128,128]{4,3,2,1,0:T(8,128)(2,1)}, bf16[1,2,4,128,128]{4,3,2,1,0:T(8,128)(2,1)}, u32[]{:S(2)}, u32[]{:S(2)}) collective-permute-start(bf16[1,2,4,128,128]{4,3,2,1,0:T(8,128)(2,1)} %get-tuple-element.38), channel_id=1, source_target_pairs={{8,4},{16,12},{24,20},{4,8},{12,16},{20,24},{9,5},{17,13},{25,21},... | collective-permute-start | bytes 786440 | tf_op jit(solution)/shard_map/ppermute | solution.py:59
  98.4 1.3 %collective-permute-start.19 = (f32[4096]{0:T(1024)S(1)}, f32[4096]{0:T(1024)S(1)}, u32[]{:S(2)}, u32[]{:S(2)}) collective-permute-start(f32[4096]{0:T(1024)S(1)} %add_add_fusion), channel_id=1, source_target_pairs={{0,2},{1,3},{2,0},{3,1},{4,6},{5,7},{6,4},{7,5},{8,10},{9,11},{10,... | collective-permute-start | bytes 49160 | tf_op jit(solution)/shard_map/ppermute | solution.py:308
  99.7 1.8 %collective-permute-done.19 = f32[4096]{0:T(1024)S(1)} collective-permute-done((f32[4096]{0:T(1024)S(1)}, f32[4096]{0:T(1024)S(1)}, u32[]{:S(2)}, u32[]{:S(2)}) %collective-permute-start.19) | collective-permute-done | bytes 16416 | tf_op jit(solution)/shard_map/ppermute | solution.py:308
  101.4 2.2 %collective-permute-start.20 = (f32[4096]{0:T(1024)S(1)}, f32[4096]{0:T(1024)S(1)}, u32[]{:S(2)}, u32[]{:S(2)}) collective-permute-start(f32[4096]{0:T(1024)S(1)} %add_add_fusion), channel_id=1, source_target_pairs={{0,3},{1,2},{2,1},{3,0},{4,7},{5,6},{6,5},{7,4},{8,11},{9,10},{10,... | collective-permute-start | bytes 49160 | tf_op jit(solution)/shard_map/ppermute | solution.py:308
  103.6 1.9 %collective-permute-done.20 = f32[4096]{0:T(1024)S(1)} collective-permute-done((f32[4096]{0:T(1024)S(1)}, f32[4096]{0:T(1024)S(1)}, u32[]{:S(2)}, u32[]{:S(2)}) %collective-permute-start.20) | collective-permute-done | bytes 16416 | tf_op jit(solution)/shard_map/ppermute | solution.py:308
  105.5 0.6 add_multiply_fusion
  106.2 6.7 %collective-permute-done.11 = bf16[1,2,4,128,128]{4,3,2,1,0:T(8,128)(2,1)} collective-permute-done((bf16[1,2,4,128,128]{4,3,2,1,0:T(8,128)(2,1)}, bf16[1,2,4,128,128]{4,3,2,1,0:T(8,128)(2,1)}, u32[]{:S(2)}, u32[]{:S(2)}) %collective-permute-start.11) | collective-permute-done | bytes 262176 | tf_op jit(solution)/shard_map/ppermute | solution.py:59
  112.9 1.5 %fusion.16 = (bf16[1,1,2,4,128,128]{5,4,3,2,1,0:T(8,128)(2,1)S(1)}, bf16[1,1,2,4,128,128]{5,4,3,2,1,0:T(8,128)(2,1)S(1)}) fusion(f32[1,2,2,4,128,128]{5,4,3,2,1,0:T(8,128)S(1)} %get-tuple-element.40, f32[1,2,2,4,128,128]{5,4,3,2,1,0:T(8,128)S(1)} %copy-done.2, bf16[1,2,4,128,128]{4,3,2,1,0:T(8,128)(2,1)} %collective-permute-done.11, ...), kind=kLoop, calls=%fused_computation.44 | loop fusion | flops 2490368 | bytes 4456451 | tf_op jit(solution)/shard_map/stack | solution.py:415
  114.5 0.7 pad_maximum_fusion.3
  115.2 0.7 pad_maximum_fusion.2
  (41 shorter events, 0.3 us)
Async XLA Ops:
  2.0 13.1 %copy-start.1 = (bf16[1,8,128,128]{3,2,1,0:T(8,128)(2,1)}, bf16[1,8,128,128]{3,2,1,0:T(8,128)(2,1)S(1)}, u32[]{:S(2)}) copy-start(bf16[1,8,128,128]{3,2,1,0:T(8,128)(2,1)S(1)} %get-tuple-element.21.refs_1_) | copy-start | bytes 786436
  2.0 20.7 %copy-start = (bf16[1,8,128,128]{3,2,1,0:T(8,128)(2,1)}, bf16[1,8,128,128]{3,2,1,0:T(8,128)(2,1)S(1)}, u32[]{:S(2)}) copy-start(bf16[1,8,128,128]{3,2,1,0:T(8,128)(2,1)S(1)} %get-tuple-element.20.refs_0_) | copy-start | bytes 786436
  2.1 12.9 %collective-permute-start = (bf16[1,8,128,128]{3,2,1,0:T(8,128)(2,1)S(1)}, bf16[1,8,128,128]{3,2,1,0:T(8,128)(2,1)S(1)}, u32[]{:S(2)}, u32[]{:S(2)}) collective-permute-start(bf16[1,8,128,128]{3,2,1,0:T(8,128)(2,1)S(1)} %get-tuple-element.22), channel_id=1, source_target_pairs={{0,4},{8,12},{16,20},{24,28},{4,0},{12,8},{20,16},{28,24},{1,5},{9... | collective-permute-start | bytes 786440 | tf_op jit(solution)/shard_map/ppermute | solution.py:55
  2.2 12.8 %collective-permute-start.1 = (bf16[1,8,128,128]{3,2,1,0:T(8,128)(2,1)S(1)}, bf16[1,8,128,128]{3,2,1,0:T(8,128)(2,1)S(1)}, u32[]{:S(2)}, u32[]{:S(2)}) collective-permute-start(bf16[1,8,128,128]{3,2,1,0:T(8,128)(2,1)S(1)} %get-tuple-element.23), channel_id=1, source_target_pairs={{4,8},{12,16},{20,24},{8,4},{16,12},{24,20},{5,9},{13,17},{21,25},... | collective-permute-start | bytes 786440 | tf_op jit(solution)/shard_map/ppermute | solution.py:55
  6.5 11.4 %collective-permute-start.4 = (bf16[1,8,128,128]{3,2,1,0:T(8,128)(2,1)S(1)}, bf16[1,8,128,128]{3,2,1,0:T(8,128)(2,1)S(1)}, u32[]{:S(2)}, u32[]{:S(2)}) collective-permute-start(bf16[1,8,128,128]{3,2,1,0:T(8,128)(2,1)S(1)} %get-tuple-element.20.refs_0_), channel_id=1, source_target_pairs={{0,16},{4,20},{28,24},{1,17},{5,21},{29,25},{2,18},{6,22},{30,26},... | collective-permute-start | bytes 786440 | tf_op jit(solution)/shard_map/ppermute | solution.py:55
  10.8 11.9 %collective-permute-start.5 = (bf16[1,8,128,128]{3,2,1,0:T(8,128)(2,1)S(1)}, bf16[1,8,128,128]{3,2,1,0:T(8,128)(2,1)S(1)}, u32[]{:S(2)}, u32[]{:S(2)}) collective-permute-start(bf16[1,8,128,128]{3,2,1,0:T(8,128)(2,1)S(1)} %get-tuple-element.20.refs_0_), channel_id=1, source_target_pairs={{0,24},{4,28},{1,25},{5,29},{2,26},{6,30},{3,27},{7,31}} | collective-permute-start | bytes 786440 | tf_op jit(solution)/shard_map/ppermute | solution.py:55
  12.8 11.2 %copy-start.12 = (s32[1,16,6]{1,0,2:T(1,128)S(1)}, s32[1,16,6]{1,0,2:T(1,128)}, u32[]{:S(2)}) copy-start(s32[1,16,6]{1,0,2:T(1,128)} %param.12) | copy-start | bytes 1156
  15.0 7.7 %copy-start.5 = (bf16[1,8,128,128]{3,2,1,0:T(8,128)(2,1)}, bf16[1,8,128,128]{3,2,1,0:T(8,128)(2,1)S(1)}, u32[]{:S(2)}) copy-start(bf16[1,8,128,128]{3,2,1,0:T(8,128)(2,1)S(1)} %collective-permute-done.refs_4_) | copy-start | bytes 786436
  15.0 7.7 %copy-start.6 = (bf16[1,8,128,128]{3,2,1,0:T(8,128)(2,1)}, bf16[1,8,128,128]{3,2,1,0:T(8,128)(2,1)S(1)}, u32[]{:S(2)}) copy-start(bf16[1,8,128,128]{3,2,1,0:T(8,128)(2,1)S(1)} %collective-permute-done.1.refs_5_) | copy-start | bytes 786436
  15.1 18.7 %collective-permute-start.2 = (bf16[1,2,8,128,128]{4,3,2,1,0:T(8,128)(2,1)S(1)}, bf16[1,2,8,128,128]{4,3,2,1,0:T(8,128)(2,1)S(1)}, u32[]{:S(2)}, u32[]{:S(2)}) collective-permute-start(bf16[1,2,8,128,128]{4,3,2,1,0:T(8,128)(2,1)S(1)} %get-tuple-element.24), channel_id=1, source_target_pairs={{0,8},{4,12},{16,24},{20,28},{8,0},{12,4},{24,16},{28,20},{1,9},{5... | collective-permute-start | bytes 1572872 | tf_op jit(solution)/shard_map/ppermute | solution.py:55
  16.5 17.4 %collective-permute-start.3 = (bf16[1,2,8,128,128]{4,3,2,1,0:T(8,128)(2,1)S(1)}, bf16[1,2,8,128,128]{4,3,2,1,0:T(8,128)(2,1)}, u32[]{:S(2)}, u32[]{:S(2)}) collective-permute-start(bf16[1,2,8,128,128]{4,3,2,1,0:T(8,128)(2,1)S(1)} %get-tuple-element.25), channel_id=1, source_target_pairs={{8,16},{12,20},{16,8},{20,12},{9,17},{13,21},{17,9},{21,13},{10,18... | collective-permute-start | bytes 1572872 | tf_op jit(solution)/shard_map/ppermute | solution.py:55
  18.0 15.9 %copy-start.3 = (bf16[1,8,128,128]{3,2,1,0:T(8,128)(2,1)}, bf16[1,8,128,128]{3,2,1,0:T(8,128)(2,1)S(1)}, u32[]{:S(2)}) copy-start(bf16[1,8,128,128]{3,2,1,0:T(8,128)(2,1)S(1)} %collective-permute-done.4.refs_6_) | copy-start | bytes 786436
  22.6 11.2 %copy-start.4 = (bf16[1,8,128,128]{3,2,1,0:T(8,128)(2,1)}, bf16[1,8,128,128]{3,2,1,0:T(8,128)(2,1)S(1)}, u32[]{:S(2)}) copy-start(bf16[1,8,128,128]{3,2,1,0:T(8,128)(2,1)S(1)} %collective-permute-done.5.refs_7_) | copy-start | bytes 786436
  22.7 4.6 %collective-permute-start.6 = (bf16[1,8,128,128]{3,2,1,0:T(8,128)(2,1)S(1)}, bf16[1,8,128,128]{3,2,1,0:T(8,128)(2,1)S(1)}, u32[]{:S(2)}, u32[]{:S(2)}) collective-permute-start(bf16[1,8,128,128]{3,2,1,0:T(8,128)(2,1)S(1)} %select_select_fusion), channel_id=1, source_target_pairs={{4,0},{16,20},{20,16},{24,28},{28,24},{5,1},{17,21},{21,17},{25,29... | collective-permute-start | bytes 786440 | tf_op jit(solution)/shard_map/ppermute | solution.py:55
  27.3 6.6 %copy-start.11 = (bf16[1,8,128,128]{3,2,1,0:T(8,128)(2,1)}, bf16[1,8,128,128]{3,2,1,0:T(8,128)(2,1)S(1)}, u32[]{:S(2)}) copy-start(bf16[1,8,128,128]{3,2,1,0:T(8,128)(2,1)S(1)} %collective-permute-done.6.refs_8_) | copy-start | bytes 786436
  33.9 0.8 copy-start.8
  61.5 7.4 %collective-permute-start.14 = (f32[4096]{0:T(1024)}, f32[4096]{0:T(1024)S(1)}, u32[]{:S(2)}, u32[]{:S(2)}) collective-permute-start(f32[4096]{0:T(1024)} %bitcast.76), channel_id=1, source_target_pairs={{0,4},{4,0},{8,12},{12,8},{16,20},{20,16},{24,28},{28,24},{1,5},{5... | collective-permute-start | bytes 49160 | tf_op jit(solution)/shard_map/ppermute | solution.py:308
  61.6 30.2 %collective-permute-start.7 = (bf16[1,2,2,4,128,128]{5,4,3,2,1,0:T(8,128)(2,1)}, bf16[1,2,2,4,128,128]{5,4,3,2,1,0:T(8,128)(2,1)S(1)}, u32[]{:S(2)}, u32[]{:S(2)}) collective-permute-start(bf16[1,2,2,4,128,128]{5,4,3,2,1,0:T(8,128)(2,1)} %get-tuple-element.28), channel_id=1, source_target_pairs={{16,8},{20,12},{8,16},{12,20},{17,9},{21,13},{9,17},{13,21},{18,10... | collective-permute-start | bytes 1572872 | tf_op jit(solution)/shard_map/ppermute | solution.py:59
  62.3 30.4 %collective-permute-start.8 = (bf16[1,2,2,4,128,128]{5,4,3,2,1,0:T(8,128)(2,1)}, bf16[1,2,2,4,128,128]{5,4,3,2,1,0:T(8,128)(2,1)}, u32[]{:S(2)}, u32[]{:S(2)}) collective-permute-start(bf16[1,2,2,4,128,128]{5,4,3,2,1,0:T(8,128)(2,1)} %get-tuple-element.29), channel_id=1, source_target_pairs={{8,0},{12,4},{24,16},{28,20},{0,8},{4,12},{16,24},{20,28},{9,1},{1... | collective-permute-start | bytes 1572872 | tf_op jit(solution)/shard_map/ppermute | solution.py:59
  67.7 19.4 %collective-permute-start.9 = (bf16[1,2,4,128,128]{4,3,2,1,0:T(8,128)(2,1)}, bf16[1,2,4,128,128]{4,3,2,1,0:T(8,128)(2,1)S(1)}, u32[]{:S(2)}, u32[]{:S(2)}) collective-permute-start(bf16[1,2,4,128,128]{4,3,2,1,0:T(8,128)(2,1)} %get-tuple-element.30), channel_id=1, source_target_pairs={{0,4},{20,16},{16,20},{28,24},{24,28},{1,5},{21,17},{17,21},{29,25... | collective-permute-start | bytes 786440 | tf_op jit(solution)/shard_map/ppermute | solution.py:59
  69.7 10.4 %collective-permute-start.15 = (f32[4096]{0:T(1024)S(1)}, f32[4096]{0:T(1024)S(1)}, u32[]{:S(2)}, u32[]{:S(2)}) collective-permute-start(f32[4096]{0:T(1024)S(1)} %add.107), channel_id=1, source_target_pairs={{0,8},{4,12},{8,0},{12,4},{16,24},{20,28},{24,16},{28,20},{1,9},{5... | collective-permute-start | bytes 49160 | tf_op jit(solution)/shard_map/ppermute | solution.py:308
  69.7 10.4 %collective-permute-start.16 = (f32[4096]{0:T(1024)S(1)}, f32[4096]{0:T(1024)S(1)}, u32[]{:S(2)}, u32[]{:S(2)}) collective-permute-start(f32[4096]{0:T(1024)S(1)} %add.107), channel_id=1, source_target_pairs={{0,16},{4,20},{8,24},{12,28},{16,0},{20,4},{24,8},{28,12},{1,17},{... | collective-permute-start | bytes 49160 | tf_op jit(solution)/shard_map/ppermute | solution.py:308
  80.1 4.4 %collective-permute-start.17 = (f32[4096]{0:T(1024)S(1)}, f32[4096]{0:T(1024)S(1)}, u32[]{:S(2)}, u32[]{:S(2)}) collective-permute-start(f32[4096]{0:T(1024)S(1)} %add.107), channel_id=1, source_target_pairs={{0,24},{4,28},{8,16},{12,20},{16,8},{20,12},{24,0},{28,4},{1,25},{... | collective-permute-start | bytes 49160 | tf_op jit(solution)/shard_map/ppermute | solution.py:308
  84.5 13.9 %collective-permute-start.18 = (f32[4096]{0:T(1024)S(1)}, f32[4096]{0:T(1024)S(1)}, u32[]{:S(2)}, u32[]{:S(2)}) collective-permute-start(f32[4096]{0:T(1024)S(1)} %add_add_fusion), channel_id=1, source_target_pairs={{0,1},{1,0},{2,3},{3,2},{4,5},{5,4},{6,7},{7,6},{8,9},{9,8},{10,11... | collective-permute-start | bytes 49160 | tf_op jit(solution)/shard_map/ppermute | solution.py:308
  87.1 7.0 %copy-start.9 = (bf16[1,2,4,128,128]{4,3,2,1,0:T(8,128)(2,1)S(1)}, bf16[1,2,4,128,128]{4,3,2,1,0:T(8,128)(2,1)}, u32[]{:S(2)}) copy-start(bf16[1,2,4,128,128]{4,3,2,1,0:T(8,128)(2,1)} %get-tuple-element.31) | copy-start | bytes 786436
  87.1 7.0 %copy-start.10 = (bf16[1,2,4,128,128]{4,3,2,1,0:T(8,128)(2,1)S(1)}, bf16[1,2,4,128,128]{4,3,2,1,0:T(8,128)(2,1)}, u32[]{:S(2)}) copy-start(bf16[1,2,4,128,128]{4,3,2,1,0:T(8,128)(2,1)} %get-tuple-element.32) | copy-start | bytes 786436
  89.1 17.0 %collective-permute-start.12 = (bf16[1,2,4,128,128]{4,3,2,1,0:T(8,128)(2,1)}, bf16[1,2,4,128,128]{4,3,2,1,0:T(8,128)(2,1)}, u32[]{:S(2)}, u32[]{:S(2)}) collective-permute-start(bf16[1,2,4,128,128]{4,3,2,1,0:T(8,128)(2,1)} %get-tuple-element.58), channel_id=1, source_target_pairs={{16,0},{20,4},{24,28},{17,1},{21,5},{25,29},{18,2},{22,6},{26,30},... | collective-permute-start | bytes 786440 | tf_op jit(solution)/shard_map/ppermute | solution.py:59
  90.4 22.5 %copy-start.2 = (f32[1,2,2,4,128,128]{5,4,3,2,1,0:T(8,128)S(1)}, f32[1,2,2,4,128,128]{5,4,3,2,1,0:T(8,128)}, u32[]{:S(2)}) copy-start(f32[1,2,2,4,128,128]{5,4,3,2,1,0:T(8,128)} %get-tuple-element.27) | copy-start | bytes 3145732
  90.4 15.7 %collective-permute-start.13 = (bf16[1,2,4,128,128]{4,3,2,1,0:T(8,128)(2,1)}, bf16[1,2,4,128,128]{4,3,2,1,0:T(8,128)(2,1)}, u32[]{:S(2)}, u32[]{:S(2)}) collective-permute-start(bf16[1,2,4,128,128]{4,3,2,1,0:T(8,128)(2,1)} %get-tuple-element.59), channel_id=1, source_target_pairs={{24,0},{28,4},{25,1},{29,5},{26,2},{30,6},{27,3},{31,7}} | collective-permute-start | bytes 786440 | tf_op jit(solution)/shard_map/ppermute | solution.py:59
  91.9 0.8 copy-start.7
  95.0 11.2 %collective-permute-start.10 = (bf16[1,2,4,128,128]{4,3,2,1,0:T(8,128)(2,1)}, bf16[1,2,4,128,128]{4,3,2,1,0:T(8,128)(2,1)}, u32[]{:S(2)}, u32[]{:S(2)}) collective-permute-start(bf16[1,2,4,128,128]{4,3,2,1,0:T(8,128)(2,1)} %get-tuple-element.39), channel_id=1, source_target_pairs={{4,0},{12,8},{20,16},{28,24},{0,4},{8,12},{16,20},{24,28},{5,1},{1... | collective-permute-start | bytes 786440 | tf_op jit(solution)/shard_map/ppermute | solution.py:59
  96.4 16.4 %collective-permute-start.11 = (bf16[1,2,4,128,128]{4,3,2,1,0:T(8,128)(2,1)}, bf16[1,2,4,128,128]{4,3,2,1,0:T(8,128)(2,1)}, u32[]{:S(2)}, u32[]{:S(2)}) collective-permute-start(bf16[1,2,4,128,128]{4,3,2,1,0:T(8,128)(2,1)} %get-tuple-element.38), channel_id=1, source_target_pairs={{8,4},{16,12},{24,20},{4,8},{12,16},{20,24},{9,5},{17,13},{25,21},... | collective-permute-start | bytes 786440 | tf_op jit(solution)/shard_map/ppermute | solution.py:59
  98.4 3.1 %collective-permute-start.19 = (f32[4096]{0:T(1024)S(1)}, f32[4096]{0:T(1024)S(1)}, u32[]{:S(2)}, u32[]{:S(2)}) collective-permute-start(f32[4096]{0:T(1024)S(1)} %add_add_fusion), channel_id=1, source_target_pairs={{0,2},{1,3},{2,0},{3,1},{4,6},{5,7},{6,4},{7,5},{8,10},{9,11},{10,... | collective-permute-start | bytes 49160 | tf_op jit(solution)/shard_map/ppermute | solution.py:308
  101.4 4.1 %collective-permute-start.20 = (f32[4096]{0:T(1024)S(1)}, f32[4096]{0:T(1024)S(1)}, u32[]{:S(2)}, u32[]{:S(2)}) collective-permute-start(f32[4096]{0:T(1024)S(1)} %add_add_fusion), channel_id=1, source_target_pairs={{0,3},{1,2},{2,1},{3,0},{4,7},{5,6},{6,5},{7,4},{8,11},{9,10},{10,... | collective-permute-start | bytes 49160 | tf_op jit(solution)/shard_map/ppermute | solution.py:308

commit v6 on v5

--- a/solution.py
+++ b/solution.py
@@ -388,8 +388,10 @@
     back_sw = send_back(d_sw, exchange["swap"])
     from_up = jnp.where(upper, back_b, back_a).astype(f32)
     from_down = jnp.where(upper, back_a, back_b).astype(f32)
-    d_c = (d_c.astype(f32) + jnp.where(even, from_down[:, 1], from_up[:, 1])).astype(bf16)
-    d_d = (d_d.astype(f32) + jnp.where(even, from_up[:, 1], from_down[:, 1])).astype(bf16)
+    same = even == upper
+    further_a, further_b = back_a[:, 1], back_b[:, 1]
+    d_c = (d_c.astype(f32) + jnp.where(same, further_a, further_b).astype(f32)).astype(bf16)
+    d_d = (d_d.astype(f32) + jnp.where(same, further_b, further_a).astype(f32)).astype(bf16)
     d_near = d_near.astype(f32) + gate((r >= 4) & (r < 6), back_sw)
     d_far = d_far.astype(f32) + gate(r >= n - 2, back_sw)
     low_extra = 0.0

time: 116 us -> 112 us (0.966)
  other arithmetic: 10.1 us -> 7.09 us
    ppermute x7, waiting for transfers between devices: 15.2 us -> 5.19 us  [swapped(): return lax.ppermute(value, axis, pairs)]
    ppermute x7, waiting for transfers between devices: 6.72 us -> 16.1 us  [send_back(): return lax.ppermute(value, 'ctx', [(b, a) for a, b in pairs])]
    ppermute x7, starting transfers between devices: 13.4 us -> 12.1 us  [send_back(): return lax.ppermute(value, 'ctx', [(b, a) for a, b in pairs])]
    convert_element_type x1, other arithmetic: 1.34 us -> 0.08 us  [body(): from_down = jnp.where(upper, back_a, back_b).astype(f32)]
  transfers between devices with their start and end apart: 21 -> 21, of which waited for: 9 -> 9; matrix products, arithmetic and copies ran while one was open for 6% -> 4% of each run, Pallas kernels for 0% -> 0%
where the time goes in v6:
time: 112 us; the launch traced here: 111 us
  starting transfers between devices  37.3 us (33%)
  waiting for transfers between devices  36.5 us (33%)
  Pallas kernels  26.8 us (24%)
  other arithmetic  7.09 us (6%)
  local copies, waits for them, and re-layouts  1.75 us (2%)
  between operations  1.61 us (1%)
    pallas_call x1, Pallas kernels, attend(): pl.pallas_call(functools.partial(attend_kernel, n, nbuf, heads, group), o...  26.8 us
    ppermute x7, waiting for transfers between devices, send_back(): return lax.ppermute(value, 'ctx', [(b, a) for a, b in pairs])  16.1 us
    ppermute x7, waiting for transfers between devices, send(): return lax.ppermute(value, 'ctx', pairs)  15.3 us
    ppermute x7, starting transfers between devices, send(): return lax.ppermute(value, 'ctx', pairs)  14.8 us
    ppermute x7, starting transfers between devices, send_back(): return lax.ppermute(value, 'ctx', [(b, a) for a, b in pairs])  12.1 us
    ppermute x7, starting transfers between devices, swapped(): return lax.ppermute(value, axis, pairs)  10.4 us
    ppermute x7, waiting for transfers between devices, swapped(): return lax.ppermute(value, axis, pairs)  5.19 us
  transfers between devices with their start and end apart: 21, of which 9 were waited for; matrix products, arithmetic and copies ran while one was open for 4% of the time, Pallas kernels for 0%

profile of v6, /device:TPU:3, one launch (start us, length us, event | category | flops | bytes accessed | tf_op | source)
XLA Modules:
  0.0 111.1 jit_solution(1530710013443897605)
XLA Ops:
  0.6 1.1 maximum_bitcast_fusion
  1.7 0.1 copy.17
  1.9 0.1 copy_bitcast_fusion
  2.0 0.0 copy-start.1
  2.0 0.1 broadcast_select_fusion.2
  2.1 0.1 collective-permute-start
  2.2 4.4 %collective-permute-start.1 = (bf16[1,8,128,128]{3,2,1,0:T(8,128)(2,1)S(1)}, bf16[1,8,128,128]{3,2,1,0:T(8,128)(2,1)S(1)}, u32[]{:S(2)}, u32[]{:S(2)}) collective-permute-start(bf16[1,8,128,128]{3,2,1,0:T(8,128)(2,1)S(1)} %get-tuple-element.23), channel_id=1, source_target_pairs={{4,8},{12,16},{20,24},{8,4},{16,12},{24,20},{5,9},{13,17},{21,25},... | collective-permute-start | bytes 786440 | tf_op jit(solution)/shard_map/ppermute | solution.py:55
  6.5 4.2 %collective-permute-start.4 = (bf16[1,8,128,128]{3,2,1,0:T(8,128)(2,1)S(1)}, bf16[1,8,128,128]{3,2,1,0:T(8,128)(2,1)S(1)}, u32[]{:S(2)}, u32[]{:S(2)}) collective-permute-start(bf16[1,8,128,128]{3,2,1,0:T(8,128)(2,1)S(1)} %get-tuple-element.20.refs_0_), channel_id=1, source_target_pairs={{0,16},{4,20},{28,24},{1,17},{5,21},{29,25},{2,18},{6,22},{30,26},... | collective-permute-start | bytes 786440 | tf_op jit(solution)/shard_map/ppermute | solution.py:55
  10.8 2.1 %collective-permute-start.5 = (bf16[1,8,128,128]{3,2,1,0:T(8,128)(2,1)S(1)}, bf16[1,8,128,128]{3,2,1,0:T(8,128)(2,1)S(1)}, u32[]{:S(2)}, u32[]{:S(2)}) collective-permute-start(bf16[1,8,128,128]{3,2,1,0:T(8,128)(2,1)S(1)} %get-tuple-element.20.refs_0_), channel_id=1, source_target_pairs={{0,24},{4,28},{1,25},{5,29},{2,26},{6,30},{3,27},{7,31}} | collective-permute-start | bytes 786440 | tf_op jit(solution)/shard_map/ppermute | solution.py:55
  12.9 2.1 %collective-permute-done.refs_4_ = bf16[1,8,128,128]{3,2,1,0:T(8,128)(2,1)S(1)} collective-permute-done((bf16[1,8,128,128]{3,2,1,0:T(8,128)(2,1)S(1)}, bf16[1,8,128,128]{3,2,1,0:T(8,128)(2,1)S(1)}, u32[]{:S(2)}, u32[]{:S(2)}) %collective-permute-start) | collective-permute-done | bytes 262176 | tf_op jit(solution)/shard_map/ppermute | solution.py:55
  15.0 0.1 broadcast_select_fusion
  15.1 1.4 %collective-permute-start.2 = (bf16[1,2,8,128,128]{4,3,2,1,0:T(8,128)(2,1)S(1)}, bf16[1,2,8,128,128]{4,3,2,1,0:T(8,128)(2,1)S(1)}, u32[]{:S(2)}, u32[]{:S(2)}) collective-permute-start(bf16[1,2,8,128,128]{4,3,2,1,0:T(8,128)(2,1)S(1)} %get-tuple-element.24), channel_id=1, source_target_pairs={{0,8},{4,12},{16,24},{20,28},{8,0},{12,4},{24,16},{28,20},{1,9},{5... | collective-permute-start | bytes 1572872 | tf_op jit(solution)/shard_map/ppermute | solution.py:55
  16.5 1.5 %collective-permute-start.3 = (bf16[1,2,8,128,128]{4,3,2,1,0:T(8,128)(2,1)S(1)}, bf16[1,2,8,128,128]{4,3,2,1,0:T(8,128)(2,1)}, u32[]{:S(2)}, u32[]{:S(2)}) collective-permute-start(bf16[1,2,8,128,128]{4,3,2,1,0:T(8,128)(2,1)S(1)} %get-tuple-element.25), channel_id=1, source_target_pairs={{8,16},{12,20},{16,8},{20,12},{9,17},{13,21},{17,9},{21,13},{10,18... | collective-permute-start | bytes 1572872 | tf_op jit(solution)/shard_map/ppermute | solution.py:55
  18.0 4.7 %collective-permute-done.5.refs_7_ = bf16[1,8,128,128]{3,2,1,0:T(8,128)(2,1)S(1)} collective-permute-done((bf16[1,8,128,128]{3,2,1,0:T(8,128)(2,1)S(1)}, bf16[1,8,128,128]{3,2,1,0:T(8,128)(2,1)S(1)}, u32[]{:S(2)}, u32[]{:S(2)}) %collective-permute-start.5) | collective-permute-done | bytes 262176 | tf_op jit(solution)/shard_map/ppermute | solution.py:55
  22.7 1.3 %collective-permute-start.6 = (bf16[1,8,128,128]{3,2,1,0:T(8,128)(2,1)S(1)}, bf16[1,8,128,128]{3,2,1,0:T(8,128)(2,1)S(1)}, u32[]{:S(2)}, u32[]{:S(2)}) collective-permute-start(bf16[1,8,128,128]{3,2,1,0:T(8,128)(2,1)S(1)} %select_select_fusion), channel_id=1, source_target_pairs={{4,0},{16,20},{20,16},{24,28},{28,24},{5,1},{17,21},{21,17},{25,29... | collective-permute-start | bytes 786440 | tf_op jit(solution)/shard_map/ppermute | solution.py:55
  24.0 0.1 copy.12
  24.1 0.6 reshape.334.blocks_ref
  25.4 1.9 %collective-permute-done.6.refs_8_ = bf16[1,8,128,128]{3,2,1,0:T(8,128)(2,1)S(1)} collective-permute-done((bf16[1,8,128,128]{3,2,1,0:T(8,128)(2,1)S(1)}, bf16[1,8,128,128]{3,2,1,0:T(8,128)(2,1)S(1)}, u32[]{:S(2)}, u32[]{:S(2)}) %collective-permute-start.6) | collective-permute-done | bytes 262176 | tf_op jit(solution)/shard_map/ppermute | solution.py:55
  27.3 6.6 %collective-permute-done.2.refs_2_ = bf16[1,2,8,128,128]{4,3,2,1,0:T(8,128)(2,1)S(1)} collective-permute-done((bf16[1,2,8,128,128]{4,3,2,1,0:T(8,128)(2,1)S(1)}, bf16[1,2,8,128,128]{4,3,2,1,0:T(8,128)(2,1)S(1)}, u32[]{:S(2)}, u32[]{:S(2)}) %collective-permute-start.2) | collective-permute-done | bytes 524320 | tf_op jit(solution)/shard_map/ppermute | solution.py:55
  33.9 0.8 copy-done.7
  34.7 26.8 %attend.1 = (bf16[1,256,4096]{2,1,0:T(8,128)(2,1)}, f32[1,4096]{1,0:T(1,128)}, f32[1,2,2,4,128,128]{5,4,3,2,1,0:T(8,128)}, bf16[1,2,2,4,128,128]{5,4,3,2,1,0:T(8...) custom-call(s32[1]{0:T(128)} %bitcast.rank_ref, ...), custom_call_target="tpu_custom_call" | custom-call | tf_op jit(solution)/shard_map/attend/pallas_call | solution.py:274
  61.5 0.1 collective-permute-start.14
  61.6 2.8 %collective-permute-done.14 = f32[4096]{0:T(1024)S(1)} collective-permute-done((f32[4096]{0:T(1024)}, f32[4096]{0:T(1024)S(1)}, u32[]{:S(2)}, u32[]{:S(2)}) %collective-permute-start.14) | collective-permute-done | bytes 16416 | tf_op jit(solution)/shard_map/ppermute | solution.py:308
  64.4 0.7 add.107
  65.1 2.2 %collective-permute-start.15 = (f32[4096]{0:T(1024)S(1)}, f32[4096]{0:T(1024)S(1)}, u32[]{:S(2)}, u32[]{:S(2)}) collective-permute-start(f32[4096]{0:T(1024)S(1)} %add.107), channel_id=1, source_target_pairs={{0,8},{4,12},{8,0},{12,4},{16,24},{20,28},{24,16},{28,20},{1,9},{5... | collective-permute-start | bytes 49160 | tf_op jit(solution)/shard_map/ppermute | solution.py:308
  67.3 1.6 %collective-permute-start.16 = (f32[4096]{0:T(1024)S(1)}, f32[4096]{0:T(1024)S(1)}, u32[]{:S(2)}, u32[]{:S(2)}) collective-permute-start(f32[4096]{0:T(1024)S(1)} %add.107), channel_id=1, source_target_pairs={{0,16},{4,20},{8,24},{12,28},{16,0},{20,4},{24,8},{28,12},{1,17},{... | collective-permute-start | bytes 49160 | tf_op jit(solution)/shard_map/ppermute | solution.py:308
  68.9 1.2 %collective-permute-start.17 = (f32[4096]{0:T(1024)S(1)}, f32[4096]{0:T(1024)S(1)}, u32[]{:S(2)}, u32[]{:S(2)}) collective-permute-start(f32[4096]{0:T(1024)S(1)} %add.107), channel_id=1, source_target_pairs={{0,24},{4,28},{8,16},{12,20},{16,8},{20,12},{24,0},{28,4},{1,25},{... | collective-permute-start | bytes 49160 | tf_op jit(solution)/shard_map/ppermute | solution.py:308
  70.1 1.3 %collective-permute-start.9 = (bf16[1,2,4,128,128]{4,3,2,1,0:T(8,128)(2,1)}, bf16[1,2,4,128,128]{4,3,2,1,0:T(8,128)(2,1)S(1)}, u32[]{:S(2)}, u32[]{:S(2)}) collective-permute-start(bf16[1,2,4,128,128]{4,3,2,1,0:T(8,128)(2,1)} %get-tuple-element.30), channel_id=1, source_target_pairs={{0,4},{20,16},{16,20},{28,24},{24,28},{1,5},{21,17},{17,21},{29,25... | collective-permute-start | bytes 786440 | tf_op jit(solution)/shard_map/ppermute | solution.py:59
  71.4 0.7 collective-permute-start.7
  72.1 3.7 %collective-permute-start.8 = (bf16[1,2,2,4,128,128]{5,4,3,2,1,0:T(8,128)(2,1)}, bf16[1,2,2,4,128,128]{5,4,3,2,1,0:T(8,128)(2,1)S(1)}, u32[]{:S(2)}, u32[]{:S(2)}) collective-permute-start(bf16[1,2,2,4,128,128]{5,4,3,2,1,0:T(8,128)(2,1)} %get-tuple-element.29), channel_id=1, source_target_pairs={{8,0},{12,4},{24,16},{28,20},{0,8},{4,12},{16,24},{20,28},{9,1},{1... | collective-permute-start | bytes 1572872 | tf_op jit(solution)/shard_map/ppermute | solution.py:59
  75.7 3.1 %collective-permute-start.18 = (f32[4096]{0:T(1024)S(1)}, f32[4096]{0:T(1024)S(1)}, u32[]{:S(2)}, u32[]{:S(2)}) collective-permute-start(f32[4096]{0:T(1024)S(1)} %add_add_fusion), channel_id=1, source_target_pairs={{0,1},{1,0},{2,3},{3,2},{4,5},{5,4},{6,7},{7,6},{8,9},{9,8},{10,11... | collective-permute-start | bytes 49160 | tf_op jit(solution)/shard_map/ppermute | solution.py:308
  78.8 1.2 %collective-permute-start.19 = (f32[4096]{0:T(1024)S(1)}, f32[4096]{0:T(1024)S(1)}, u32[]{:S(2)}, u32[]{:S(2)}) collective-permute-start(f32[4096]{0:T(1024)S(1)} %add_add_fusion), channel_id=1, source_target_pairs={{0,2},{1,3},{2,0},{3,1},{4,6},{5,7},{6,4},{7,5},{8,10},{9,11},{10,... | collective-permute-start | bytes 49160 | tf_op jit(solution)/shard_map/ppermute | solution.py:308
  80.0 1.1 collective-permute-start.20
  81.1 0.6 collective-permute-done.19
  81.7 1.8 %collective-permute-done.20 = f32[4096]{0:T(1024)S(1)} collective-permute-done((f32[4096]{0:T(1024)S(1)}, f32[4096]{0:T(1024)S(1)}, u32[]{:S(2)}, u32[]{:S(2)}) %collective-permute-start.20) | collective-permute-done | bytes 16416 | tf_op jit(solution)/shard_map/ppermute | solution.py:308
  83.5 0.6 add_multiply_fusion
  84.1 1.2 %fusion.6 = (bf16[1,2,4,128,128]{4,3,2,1,0:T(8,128)(2,1)S(1)}, bf16[1,2,4,128,128]{4,3,2,1,0:T(8,128)(2,1)S(1)}) fusion(bf16[1,2,4,128,128]{4,3,2,1,0:T(8,128)(2,1)S(1)} %collective-permute-done.9, bf16[1,2,4,128,128]{4,3,2,1,0:T(8,128)(2,1)} %get-tuple-element.33, pred[]{:T(512)S(6)} %and.14, pred[]{:T(512)S(6)} %ge.7, ...), kind=kLoop, calls=%fused_computation.23 | loop fusion | flops 1179648 | bytes 1310722 | tf_op jit(solution)/shard_map/convert_element_type | solution.py:409
  85.3 1.4 %collective-permute-start.12 = (bf16[1,2,4,128,128]{4,3,2,1,0:T(8,128)(2,1)S(1)}, bf16[1,2,4,128,128]{4,3,2,1,0:T(8,128)(2,1)S(1)}, u32[]{:S(2)}, u32[]{:S(2)}) collective-permute-start(bf16[1,2,4,128,128]{4,3,2,1,0:T(8,128)(2,1)S(1)} %get-tuple-element.56), channel_id=1, source_target_pairs={{16,0},{20,4},{24,28},{17,1},{21,5},{25,29},{18,2},{22,6},{26,30},... | collective-permute-start | bytes 786440 | tf_op jit(solution)/shard_map/ppermute | solution.py:59
  86.7 1.3 %collective-permute-start.13 = (bf16[1,2,4,128,128]{4,3,2,1,0:T(8,128)(2,1)S(1)}, bf16[1,2,4,128,128]{4,3,2,1,0:T(8,128)(2,1)S(1)}, u32[]{:S(2)}, u32[]{:S(2)}) collective-permute-start(bf16[1,2,4,128,128]{4,3,2,1,0:T(8,128)(2,1)S(1)} %get-tuple-element.57), channel_id=1, source_target_pairs={{24,0},{28,4},{25,1},{29,5},{26,2},{30,6},{27,3},{31,7}} | collective-permute-start | bytes 786440 | tf_op jit(solution)/shard_map/ppermute | solution.py:59
  88.1 1.2 %fusion.14 = (bf16[1,2,4,128,128]{4,3,2,1,0:T(8,128)(2,1)S(1)}, bf16[1,2,4,128,128]{4,3,2,1,0:T(8,128)(2,1)S(1)}) fusion(bf16[1,2,4,128,128]{4,3,2,1,0:T(8,128)(2,1)} %get-tuple-element.32, pred[]{:T(512)S(6)} %eq.18, bf16[1,2,2,4,128,128]{5,4,3,2,1,0:T(8,128)(2,1)S(1)} %collective-permute-done.7, ...), kind=kLoop, calls=%fused_computation.37 | loop fusion | flops 1310720 | bytes 1572865 | tf_op jit(solution)/shard_map/convert_element_type | solution.py:394
  89.3 1.8 %collective-permute-start.10 = (bf16[1,2,4,128,128]{4,3,2,1,0:T(8,128)(2,1)S(1)}, bf16[1,2,4,128,128]{4,3,2,1,0:T(8,128)(2,1)S(1)}, u32[]{:S(2)}, u32[]{:S(2)}) collective-permute-start(bf16[1,2,4,128,128]{4,3,2,1,0:T(8,128)(2,1)S(1)} %get-tuple-element.39), channel_id=1, source_target_pairs={{4,0},{12,8},{20,16},{28,24},{0,4},{8,12},{16,20},{24,28},{5,1},{1... | collective-permute-start | bytes 786440 | tf_op jit(solution)/shard_map/ppermute | solution.py:59
  91.1 1.9 %collective-permute-start.11 = (bf16[1,2,4,128,128]{4,3,2,1,0:T(8,128)(2,1)S(1)}, bf16[1,2,4,128,128]{4,3,2,1,0:T(8,128)(2,1)S(1)}, u32[]{:S(2)}, u32[]{:S(2)}) collective-permute-start(bf16[1,2,4,128,128]{4,3,2,1,0:T(8,128)(2,1)S(1)} %get-tuple-element.38), channel_id=1, source_target_pairs={{8,4},{16,12},{24,20},{4,8},{12,16},{20,24},{9,5},{17,13},{25,21},... | collective-permute-start | bytes 786440 | tf_op jit(solution)/shard_map/ppermute | solution.py:59
  93.0 0.1 select_convert_fusion
  93.1 8.6 %collective-permute-done.12 = bf16[1,2,4,128,128]{4,3,2,1,0:T(8,128)(2,1)S(1)} collective-permute-done((bf16[1,2,4,128,128]{4,3,2,1,0:T(8,128)(2,1)S(1)}, bf16[1,2,4,128,128]{4,3,2,1,0:T(8,128)(2,1)S(1)}, u32[]{:S(2)}, u32[]{:S(2)}) %collective-permute-start.12) | collective-permute-done | bytes 262176 | tf_op jit(solution)/shard_map/ppermute | solution.py:59
  101.7 7.5 %collective-permute-done.11 = bf16[1,2,4,128,128]{4,3,2,1,0:T(8,128)(2,1)S(1)} collective-permute-done((bf16[1,2,4,128,128]{4,3,2,1,0:T(8,128)(2,1)S(1)}, bf16[1,2,4,128,128]{4,3,2,1,0:T(8,128)(2,1)S(1)}, u32[]{:S(2)}, u32[]{:S(2)}) %collective-permute-start.11) | collective-permute-done | bytes 262176 | tf_op jit(solution)/shard_map/ppermute | solution.py:59
  109.2 0.4 fusion.16
  109.6 0.7 pad_maximum_fusion.3
  110.4 0.7 pad_maximum_fusion.2
  (35 shorter events, 0.2 us)
Async XLA Ops:
  2.0 13.1 %copy-start.1 = (bf16[1,8,128,128]{3,2,1,0:T(8,128)(2,1)}, bf16[1,8,128,128]{3,2,1,0:T(8,128)(2,1)S(1)}, u32[]{:S(2)}) copy-start(bf16[1,8,128,128]{3,2,1,0:T(8,128)(2,1)S(1)} %get-tuple-element.21.refs_1_) | copy-start | bytes 786436
  2.0 20.7 %copy-start = (bf16[1,8,128,128]{3,2,1,0:T(8,128)(2,1)}, bf16[1,8,128,128]{3,2,1,0:T(8,128)(2,1)S(1)}, u32[]{:S(2)}) copy-start(bf16[1,8,128,128]{3,2,1,0:T(8,128)(2,1)S(1)} %get-tuple-element.20.refs_0_) | copy-start | bytes 786436
  2.1 12.9 %collective-permute-start = (bf16[1,8,128,128]{3,2,1,0:T(8,128)(2,1)S(1)}, bf16[1,8,128,128]{3,2,1,0:T(8,128)(2,1)S(1)}, u32[]{:S(2)}, u32[]{:S(2)}) collective-permute-start(bf16[1,8,128,128]{3,2,1,0:T(8,128)(2,1)S(1)} %get-tuple-element.22), channel_id=1, source_target_pairs={{0,4},{8,12},{16,20},{24,28},{4,0},{12,8},{20,16},{28,24},{1,5},{9... | collective-permute-start | bytes 786440 | tf_op jit(solution)/shard_map/ppermute | solution.py:55
  2.2 12.8 %collective-permute-start.1 = (bf16[1,8,128,128]{3,2,1,0:T(8,128)(2,1)S(1)}, bf16[1,8,128,128]{3,2,1,0:T(8,128)(2,1)S(1)}, u32[]{:S(2)}, u32[]{:S(2)}) collective-permute-start(bf16[1,8,128,128]{3,2,1,0:T(8,128)(2,1)S(1)} %get-tuple-element.23), channel_id=1, source_target_pairs={{4,8},{12,16},{20,24},{8,4},{16,12},{24,20},{5,9},{13,17},{21,25},... | collective-permute-start | bytes 786440 | tf_op jit(solution)/shard_map/ppermute | solution.py:55
  6.5 11.4 %collective-permute-start.4 = (bf16[1,8,128,128]{3,2,1,0:T(8,128)(2,1)S(1)}, bf16[1,8,128,128]{3,2,1,0:T(8,128)(2,1)S(1)}, u32[]{:S(2)}, u32[]{:S(2)}) collective-permute-start(bf16[1,8,128,128]{3,2,1,0:T(8,128)(2,1)S(1)} %get-tuple-element.20.refs_0_), channel_id=1, source_target_pairs={{0,16},{4,20},{28,24},{1,17},{5,21},{29,25},{2,18},{6,22},{30,26},... | collective-permute-start | bytes 786440 | tf_op jit(solution)/shard_map/ppermute | solution.py:55
  10.8 11.9 %collective-permute-start.5 = (bf16[1,8,128,128]{3,2,1,0:T(8,128)(2,1)S(1)}, bf16[1,8,128,128]{3,2,1,0:T(8,128)(2,1)S(1)}, u32[]{:S(2)}, u32[]{:S(2)}) collective-permute-start(bf16[1,8,128,128]{3,2,1,0:T(8,128)(2,1)S(1)} %get-tuple-element.20.refs_0_), channel_id=1, source_target_pairs={{0,24},{4,28},{1,25},{5,29},{2,26},{6,30},{3,27},{7,31}} | collective-permute-start | bytes 786440 | tf_op jit(solution)/shard_map/ppermute | solution.py:55
  12.8 11.2 %copy-start.9 = (s32[1,16,6]{1,0,2:T(1,128)S(1)}, s32[1,16,6]{1,0,2:T(1,128)}, u32[]{:S(2)}) copy-start(s32[1,16,6]{1,0,2:T(1,128)} %param.12) | copy-start | bytes 1156
  15.0 7.7 %copy-start.5 = (bf16[1,8,128,128]{3,2,1,0:T(8,128)(2,1)}, bf16[1,8,128,128]{3,2,1,0:T(8,128)(2,1)S(1)}, u32[]{:S(2)}) copy-start(bf16[1,8,128,128]{3,2,1,0:T(8,128)(2,1)S(1)} %collective-permute-done.refs_4_) | copy-start | bytes 786436
  15.0 7.7 %copy-start.6 = (bf16[1,8,128,128]{3,2,1,0:T(8,128)(2,1)}, bf16[1,8,128,128]{3,2,1,0:T(8,128)(2,1)S(1)}, u32[]{:S(2)}) copy-start(bf16[1,8,128,128]{3,2,1,0:T(8,128)(2,1)S(1)} %collective-permute-done.1.refs_5_) | copy-start | bytes 786436
  15.1 18.7 %collective-permute-start.2 = (bf16[1,2,8,128,128]{4,3,2,1,0:T(8,128)(2,1)S(1)}, bf16[1,2,8,128,128]{4,3,2,1,0:T(8,128)(2,1)S(1)}, u32[]{:S(2)}, u32[]{:S(2)}) collective-permute-start(bf16[1,2,8,128,128]{4,3,2,1,0:T(8,128)(2,1)S(1)} %get-tuple-element.24), channel_id=1, source_target_pairs={{0,8},{4,12},{16,24},{20,28},{8,0},{12,4},{24,16},{28,20},{1,9},{5... | collective-permute-start | bytes 1572872 | tf_op jit(solution)/shard_map/ppermute | solution.py:55
  16.5 17.4 %collective-permute-start.3 = (bf16[1,2,8,128,128]{4,3,2,1,0:T(8,128)(2,1)S(1)}, bf16[1,2,8,128,128]{4,3,2,1,0:T(8,128)(2,1)}, u32[]{:S(2)}, u32[]{:S(2)}) collective-permute-start(bf16[1,2,8,128,128]{4,3,2,1,0:T(8,128)(2,1)S(1)} %get-tuple-element.25), channel_id=1, source_target_pairs={{8,16},{12,20},{16,8},{20,12},{9,17},{13,21},{17,9},{21,13},{10,18... | collective-permute-start | bytes 1572872 | tf_op jit(solution)/shard_map/ppermute | solution.py:55
  18.0 15.9 %copy-start.3 = (bf16[1,8,128,128]{3,2,1,0:T(8,128)(2,1)}, bf16[1,8,128,128]{3,2,1,0:T(8,128)(2,1)S(1)}, u32[]{:S(2)}) copy-start(bf16[1,8,128,128]{3,2,1,0:T(8,128)(2,1)S(1)} %collective-permute-done.4.refs_6_) | copy-start | bytes 786436
  22.6 11.2 %copy-start.4 = (bf16[1,8,128,128]{3,2,1,0:T(8,128)(2,1)}, bf16[1,8,128,128]{3,2,1,0:T(8,128)(2,1)S(1)}, u32[]{:S(2)}) copy-start(bf16[1,8,128,128]{3,2,1,0:T(8,128)(2,1)S(1)} %collective-permute-done.5.refs_7_) | copy-start | bytes 786436
  22.7 4.6 %collective-permute-start.6 = (bf16[1,8,128,128]{3,2,1,0:T(8,128)(2,1)S(1)}, bf16[1,8,128,128]{3,2,1,0:T(8,128)(2,1)S(1)}, u32[]{:S(2)}, u32[]{:S(2)}) collective-permute-start(bf16[1,8,128,128]{3,2,1,0:T(8,128)(2,1)S(1)} %select_select_fusion), channel_id=1, source_target_pairs={{4,0},{16,20},{20,16},{24,28},{28,24},{5,1},{17,21},{21,17},{25,29... | collective-permute-start | bytes 786440 | tf_op jit(solution)/shard_map/ppermute | solution.py:55
  27.3 6.6 %copy-start.8 = (bf16[1,8,128,128]{3,2,1,0:T(8,128)(2,1)}, bf16[1,8,128,128]{3,2,1,0:T(8,128)(2,1)S(1)}, u32[]{:S(2)}) copy-start(bf16[1,8,128,128]{3,2,1,0:T(8,128)(2,1)S(1)} %collective-permute-done.6.refs_8_) | copy-start | bytes 786436
  33.9 0.8 copy-start.7
  61.5 2.9 %collective-permute-start.14 = (f32[4096]{0:T(1024)}, f32[4096]{0:T(1024)S(1)}, u32[]{:S(2)}, u32[]{:S(2)}) collective-permute-start(f32[4096]{0:T(1024)} %bitcast.74), channel_id=1, source_target_pairs={{0,4},{4,0},{8,12},{12,8},{16,20},{20,16},{24,28},{28,24},{1,5},{5... | collective-permute-start | bytes 49160 | tf_op jit(solution)/shard_map/ppermute | solution.py:308
  65.1 7.0 %collective-permute-start.15 = (f32[4096]{0:T(1024)S(1)}, f32[4096]{0:T(1024)S(1)}, u32[]{:S(2)}, u32[]{:S(2)}) collective-permute-start(f32[4096]{0:T(1024)S(1)} %add.107), channel_id=1, source_target_pairs={{0,8},{4,12},{8,0},{12,4},{16,24},{20,28},{24,16},{28,20},{1,9},{5... | collective-permute-start | bytes 49160 | tf_op jit(solution)/shard_map/ppermute | solution.py:308
  67.3 8.4 %collective-permute-start.16 = (f32[4096]{0:T(1024)S(1)}, f32[4096]{0:T(1024)S(1)}, u32[]{:S(2)}, u32[]{:S(2)}) collective-permute-start(f32[4096]{0:T(1024)S(1)} %add.107), channel_id=1, source_target_pairs={{0,16},{4,20},{8,24},{12,28},{16,0},{20,4},{24,8},{28,12},{1,17},{... | collective-permute-start | bytes 49160 | tf_op jit(solution)/shard_map/ppermute | solution.py:308
  68.9 6.8 %collective-permute-start.17 = (f32[4096]{0:T(1024)S(1)}, f32[4096]{0:T(1024)S(1)}, u32[]{:S(2)}, u32[]{:S(2)}) collective-permute-start(f32[4096]{0:T(1024)S(1)} %add.107), channel_id=1, source_target_pairs={{0,24},{4,28},{8,16},{12,20},{16,8},{20,12},{24,0},{28,4},{1,25},{... | collective-permute-start | bytes 49160 | tf_op jit(solution)/shard_map/ppermute | solution.py:308
  70.1 14.0 %collective-permute-start.9 = (bf16[1,2,4,128,128]{4,3,2,1,0:T(8,128)(2,1)}, bf16[1,2,4,128,128]{4,3,2,1,0:T(8,128)(2,1)S(1)}, u32[]{:S(2)}, u32[]{:S(2)}) collective-permute-start(bf16[1,2,4,128,128]{4,3,2,1,0:T(8,128)(2,1)} %get-tuple-element.30), channel_id=1, source_target_pairs={{0,4},{20,16},{16,20},{28,24},{24,28},{1,5},{21,17},{17,21},{29,25... | collective-permute-start | bytes 786440 | tf_op jit(solution)/shard_map/ppermute | solution.py:59
  71.4 16.7 %collective-permute-start.7 = (bf16[1,2,2,4,128,128]{5,4,3,2,1,0:T(8,128)(2,1)}, bf16[1,2,2,4,128,128]{5,4,3,2,1,0:T(8,128)(2,1)S(1)}, u32[]{:S(2)}, u32[]{:S(2)}) collective-permute-start(bf16[1,2,2,4,128,128]{5,4,3,2,1,0:T(8,128)(2,1)} %get-tuple-element.28), channel_id=1, source_target_pairs={{16,8},{20,12},{8,16},{12,20},{17,9},{21,13},{9,17},{13,21},{18,10... | collective-permute-start | bytes 1572872 | tf_op jit(solution)/shard_map/ppermute | solution.py:59
  72.1 16.0 %collective-permute-start.8 = (bf16[1,2,2,4,128,128]{5,4,3,2,1,0:T(8,128)(2,1)}, bf16[1,2,2,4,128,128]{5,4,3,2,1,0:T(8,128)(2,1)S(1)}, u32[]{:S(2)}, u32[]{:S(2)}) collective-permute-start(bf16[1,2,2,4,128,128]{5,4,3,2,1,0:T(8,128)(2,1)} %get-tuple-element.29), channel_id=1, source_target_pairs={{8,0},{12,4},{24,16},{28,20},{0,8},{4,12},{16,24},{20,28},{9,1},{1... | collective-permute-start | bytes 1572872 | tf_op jit(solution)/shard_map/ppermute | solution.py:59
  75.7 4.3 %collective-permute-start.18 = (f32[4096]{0:T(1024)S(1)}, f32[4096]{0:T(1024)S(1)}, u32[]{:S(2)}, u32[]{:S(2)}) collective-permute-start(f32[4096]{0:T(1024)S(1)} %add_add_fusion), channel_id=1, source_target_pairs={{0,1},{1,0},{2,3},{3,2},{4,5},{5,4},{6,7},{7,6},{8,9},{9,8},{10,11... | collective-permute-start | bytes 49160 | tf_op jit(solution)/shard_map/ppermute | solution.py:308
  78.8 2.9 %collective-permute-start.19 = (f32[4096]{0:T(1024)S(1)}, f32[4096]{0:T(1024)S(1)}, u32[]{:S(2)}, u32[]{:S(2)}) collective-permute-start(f32[4096]{0:T(1024)S(1)} %add_add_fusion), channel_id=1, source_target_pairs={{0,2},{1,3},{2,0},{3,1},{4,6},{5,7},{6,4},{7,5},{8,10},{9,11},{10,... | collective-permute-start | bytes 49160 | tf_op jit(solution)/shard_map/ppermute | solution.py:308
  80.0 3.5 %collective-permute-start.20 = (f32[4096]{0:T(1024)S(1)}, f32[4096]{0:T(1024)S(1)}, u32[]{:S(2)}, u32[]{:S(2)}) collective-permute-start(f32[4096]{0:T(1024)S(1)} %add_add_fusion), channel_id=1, source_target_pairs={{0,3},{1,2},{2,1},{3,0},{4,7},{5,6},{6,5},{7,4},{8,11},{9,10},{10,... | collective-permute-start | bytes 49160 | tf_op jit(solution)/shard_map/ppermute | solution.py:308
  85.3 23.9 %copy-start.2 = (f32[1,2,2,4,128,128]{5,4,3,2,1,0:T(8,128)S(1)}, f32[1,2,2,4,128,128]{5,4,3,2,1,0:T(8,128)}, u32[]{:S(2)}) copy-start(f32[1,2,2,4,128,128]{5,4,3,2,1,0:T(8,128)} %get-tuple-element.27) | copy-start | bytes 3145732
  85.3 16.3 %collective-permute-start.12 = (bf16[1,2,4,128,128]{4,3,2,1,0:T(8,128)(2,1)S(1)}, bf16[1,2,4,128,128]{4,3,2,1,0:T(8,128)(2,1)S(1)}, u32[]{:S(2)}, u32[]{:S(2)}) collective-permute-start(bf16[1,2,4,128,128]{4,3,2,1,0:T(8,128)(2,1)S(1)} %get-tuple-element.56), channel_id=1, source_target_pairs={{16,0},{20,4},{24,28},{17,1},{21,5},{25,29},{18,2},{22,6},{26,30},... | collective-permute-start | bytes 786440 | tf_op jit(solution)/shard_map/ppermute | solution.py:59
  86.7 14.9 %collective-permute-start.13 = (bf16[1,2,4,128,128]{4,3,2,1,0:T(8,128)(2,1)S(1)}, bf16[1,2,4,128,128]{4,3,2,1,0:T(8,128)(2,1)S(1)}, u32[]{:S(2)}, u32[]{:S(2)}) collective-permute-start(bf16[1,2,4,128,128]{4,3,2,1,0:T(8,128)(2,1)S(1)} %get-tuple-element.57), channel_id=1, source_target_pairs={{24,0},{28,4},{25,1},{29,5},{26,2},{30,6},{27,3},{31,7}} | collective-permute-start | bytes 786440 | tf_op jit(solution)/shard_map/ppermute | solution.py:59
  89.3 12.4 %collective-permute-start.10 = (bf16[1,2,4,128,128]{4,3,2,1,0:T(8,128)(2,1)S(1)}, bf16[1,2,4,128,128]{4,3,2,1,0:T(8,128)(2,1)S(1)}, u32[]{:S(2)}, u32[]{:S(2)}) collective-permute-start(bf16[1,2,4,128,128]{4,3,2,1,0:T(8,128)(2,1)S(1)} %get-tuple-element.39), channel_id=1, source_target_pairs={{4,0},{12,8},{20,16},{28,24},{0,4},{8,12},{16,20},{24,28},{5,1},{1... | collective-permute-start | bytes 786440 | tf_op jit(solution)/shard_map/ppermute | solution.py:59
  91.1 18.1 %collective-permute-start.11 = (bf16[1,2,4,128,128]{4,3,2,1,0:T(8,128)(2,1)S(1)}, bf16[1,2,4,128,128]{4,3,2,1,0:T(8,128)(2,1)S(1)}, u32[]{:S(2)}, u32[]{:S(2)}) collective-permute-start(bf16[1,2,4,128,128]{4,3,2,1,0:T(8,128)(2,1)S(1)} %get-tuple-element.38), channel_id=1, source_target_pairs={{8,4},{16,12},{24,20},{4,8},{12,16},{20,24},{9,5},{17,13},{25,21},... | collective-permute-start | bytes 786440 | tf_op jit(solution)/shard_map/ppermute | solution.py:59
